TPU v7x, 32 devices: a whole 2x2x4 slice. The times are simulated.
32 devices in a mesh: clip: 2 (over x), seq: 16 (over z, y, core).
Axes of the slice: x: 2, y: 2, z: 4, core: 2. Of those that a mesh axis runs over, the one named last changes fastest.
Arguments:
- hidden: bfloat16 [2, 1792, 1536], P(None, ('clip', 'seq')), parts along dimension 1, may hold values from -6 to 6
- latent: float32 [1792, 100], P(('clip', 'seq')), parts along dimension 0, may hold values from -6 to 6
- lengths: int32 [2], P('clip'), parts along dimension 0, may hold values from 448 to 896
- step_index: int32 [1], replicated, may hold values from 0 to 31
- guidance: float32 [1], replicated, may hold values from 1.5 to 2.5
- modulation: float32 [5, 1536], replicated, may hold values from -2.5 to 2.5
- conv_kernel: float32 [31, 1536], replicated, may hold values from -1 to 1
- w_qkv: bfloat16 [1536, 3072], replicated, may hold values from -1 to 1
- w_out: bfloat16 [1024, 1536], replicated, may hold values from -0.1875 to 0.1875
- w_mel: bfloat16 [1536, 100], replicated, may hold values from -0.15625 to 0.15625
Outputs:
- velocity: float32 [1792, 100], P(('clip', 'seq')), parts along dimension 0
- estimate: float32 [1792, 100], P(('clip', 'seq')), parts along dimension 0
There are 2 independent parts, one for each index of `clip`. A program takes and returns all parts, laid end to end along the dimension named above; an argument that names none is the same for every part. Nothing has to cross between parts.
All inputs are finite; a program needn't handle non-finite values.
Results may differ from a plain program's by a relative error of at most 0.0061.
Values may be sent and summed in bfloat16 or wider, within the bound.
No kernel may reach another device: no remote copies, remote signals or barrier semaphores. Data moves between devices by JAX's collectives and lax.ppermute only.
A program may use at most 192 MiB of HBM per device.

v0:
```python
import functools

import jax
import jax.numpy as jnp
from jax import lax
from jax.experimental import pallas as pl
from jax.experimental.pallas import tpu as pltpu
from jax.sharding import PartitionSpec as P


HEADS = 16
HEAD_DIM = 64
KERNEL = 31
STEPS = 32
LANES = 128
HALO = 16


EPSILON = 1e-06
NEGATIVE = -1e30
CORE, CHIP, LENGTH = 0, 1, 2
VMEM = pltpu.VMEM
SMEM = pltpu.SMEM
GRANT = 12 << 20


def vmem_spec():
    return pl.BlockSpec(memory_space=VMEM)


def smem_spec():
    return pl.BlockSpec(memory_space=SMEM)


def rotary_tables(positions):
    half_dim = HEAD_DIM // 2
    lane = jnp.arange(LANES, dtype=jnp.int32)
    inverse = 10000.0 ** (-(lane % half_dim).astype(jnp.float32) / half_dim)
    angles = positions.astype(jnp.float32)[:, None] * inverse[None, :]
    sign = jnp.where(lane % HEAD_DIM < half_dim, -1.0, 1.0)
    return jnp.cos(angles), jnp.sin(angles) * sign[None, :]


def hbm_spec():
    return pl.BlockSpec(memory_space=pltpu.HBM)


def tile_lanes(tile):
    return pl.ds(pl.multiple_of(tile * LANES, LANES), LANES)


def row_norm(load, store, tiles, mod_ref, row, total):
    width = tiles * LANES
    mean = jnp.sum(total, axis=-1, keepdims=True) * (1.0 / width)

    def square(tile, acc):
        centered = load(tile) - mean
        return acc + centered * centered

    squares = lax.fori_loop(0, tiles, square, jnp.zeros(total.shape, jnp.float32), unroll=6)
    variance = jnp.sum(squares, axis=-1, keepdims=True) * (1.0 / width)
    factor = lax.rsqrt(variance + EPSILON)

    def write(tile, carry):
        lanes = tile_lanes(tile)
        scale = 1.0 + mod_ref[row + 1 : row + 2, lanes]
        shift = mod_ref[row : row + 1, lanes]
        store(lanes, (load(tile) - mean) * factor * scale + shift)
        return carry

    lax.fori_loop(0, tiles, write, 0, unroll=6)


def run_copies(pairs, sems):
    copies = [
        pltpu.make_async_copy(source, target, sems.at[at])
        for at, (source, target) in enumerate(pairs)
    ]
    for copy in copies:
        copy.start()
    for copy in copies:
        copy.wait()


def stage_kernel(
    info_ref, hidden_hbm, taps_hbm, mod_hbm, own_ref, taps_ref, mod_ref, first_ref, live_ref, sems
):
    rows = own_ref.shape[0]
    core = info_ref[CORE]
    first_ref[...] = jnp.zeros(first_ref.shape, jnp.float32) + (1 - core).astype(jnp.float32)
    row = lax.broadcasted_iota(jnp.int32, live_ref.shape, 0)
    frame = row + (2 * info_ref[CHIP] + core) * rows
    live_ref[...] = (frame < info_ref[LENGTH]).astype(jnp.float32)
    run_copies(
        [(hidden_hbm.at[core], own_ref), (taps_hbm, taps_ref), (mod_hbm, mod_ref)], sems
    )


def front_kernel(
    info_ref, own_ref, partner_ref, near_ref, far_ref, taps_ref, mod_ref, weight_hbm,
    residual_ref, normed_ref, weight_ref, padded, sems,
):
    rows, width = own_ref.shape
    halo = near_ref.shape[1]
    total_rows = 2 * rows
    tiles = width // LANES
    parts = 8
    depth = width // parts
    loads = []
    for part in range(parts):
        here = pl.ds(part * depth, depth)
        loads.append(
            pltpu.make_async_copy(weight_hbm.at[here], weight_ref.at[here], sems.at[part])
        )
    for load in loads:
        load.start()
    length, core = info_ref[LENGTH], info_ref[CORE]
    offset = info_ref[CHIP] * total_rows
    span = total_rows + 2 * halo
    frame = offset - halo + lax.broadcasted_iota(jnp.int32, (span, LANES), 0)
    live = ((frame >= 0) & (frame < length)).astype(jnp.float32)
    first = halo - KERNEL // 2
    own_at = pl.ds(pl.multiple_of(halo + core * rows, 8), rows)
    partner_at = pl.ds(pl.multiple_of(halo + (1 - core) * rows, 8), rows)
    near_at = pl.ds(pl.multiple_of(core * (halo + total_rows), 8), halo)
    far_at = pl.ds(pl.multiple_of((1 - core) * (halo + total_rows), 8), halo)

    def convolve(tile, total):
        lanes = tile_lanes(tile)
        padded[near_at] = near_ref[core, :, lanes].astype(jnp.float32)
        padded[far_at] = far_ref[core, :, lanes].astype(jnp.float32)
        padded[own_at] = own_ref[:, lanes].astype(jnp.float32)
        padded[partner_at] = partner_ref[:, lanes].astype(jnp.float32)
        own = padded[halo : halo + total_rows]
        padded[...] = padded[...] * live
        acc = jnp.zeros((total_rows, LANES), jnp.float32)
        for tap in range(KERNEL):
            acc = acc + taps_ref[tap : tap + 1, lanes] * padded[
                first + tap : first + tap + total_rows
            ]
        grown = jnp.exp(jnp.minimum(acc, 20.0))
        product = grown * (grown + 2.0)
        value = own + acc * (product / (product + 2.0))
        residual_ref[:, lanes] = value
        return total + value

    total = lax.fori_loop(
        0, tiles, convolve, jnp.zeros((total_rows, LANES), jnp.float32), unroll=3
    )

    def store(lanes, value):
        normed_ref[:, lanes] = value.astype(jnp.bfloat16)

    row_norm(lambda tile: residual_ref[:, tile_lanes(tile)], store, tiles, mod_ref, 0, total)
    for load in loads:
        load.wait()


def project_kernel(firsts, origin, info_ref, normed_ref, weight_ref, cos_ref, sin_ref, *out_refs):
    rows = normed_ref.shape[0]
    attn = weight_ref.shape[1] // 3
    wide = 2 * LANES
    half = HEAD_DIM // 2
    cosine, sine = cos_ref[...], sin_ref[...]
    lower = lax.broadcasted_iota(jnp.int32, (rows, LANES), 1) % HEAD_DIM < half
    chip = info_ref[CHIP] if origin is None else origin
    swap = jnp.full((rows, LANES), chip & 1, jnp.int32) > 0
    for at, apart in enumerate(firsts):
        pair = (chip ^ apart) >> 1
        for part in range(3):
            start = part * attn + pair * wide
            both = jnp.dot(
                normed_ref[...],
                weight_ref[:, pl.ds(pl.multiple_of(start, wide), wide)],
                preferred_element_type=jnp.float32,
            )
            sides = []
            for side in range(2):
                value = both[:, side * LANES : (side + 1) * LANES]
                if part < 2:
                    swapped = jnp.where(
                        lower, pltpu.roll(value, LANES - half, 1), pltpu.roll(value, half, 1)
                    )
                    value = value * cosine + swapped * sine
                if part == 0:
                    value = value * HEAD_DIM**-0.5
                sides.append(value)
            out_refs[2 * at][part] = jnp.where(swap, sides[1], sides[0]).astype(jnp.bfloat16)
            out_refs[2 * at + 1][part] = jnp.where(swap, sides[0], sides[1]).astype(jnp.bfloat16)


def gather_keys(info_ref, got_refs, keys, values):
    _, rows, _ = got_refs[0].shape
    length, chip = info_ref[LENGTH], info_ref[CHIP]
    lane = lax.broadcasted_iota(jnp.int32, (rows, LANES), 1)
    row = lax.broadcasted_iota(jnp.int32, (rows, LANES), 0)
    for apart, got_ref in enumerate(got_refs):
        here = slice(apart * rows, (apart + 1) * rows)
        keys[here, :LANES] = got_ref[1]
        dead = (lane == 0) & (row + (chip ^ apart) * rows >= length)
        keys[here, LANES:] = jnp.where(dead, NEGATIVE, 0.0).astype(jnp.bfloat16)
        values[here, :] = got_ref[2]


def attend_rows(query_refs, keys, values, out_ref, queries):
    _, rows, _ = query_refs[0].shape
    low = lax.broadcasted_iota(jnp.int32, (rows, LANES), 1) < HEAD_DIM
    zero = jnp.zeros((rows, LANES), jnp.bfloat16)
    queries[:, LANES:] = jnp.where(
        lax.broadcasted_iota(jnp.int32, (queries.shape[0], LANES), 1) == 0, 1.0, 0.0
    ).astype(jnp.bfloat16)
    for at, query_ref in enumerate(query_refs):
        query = query_ref[0]
        base = 2 * at * rows
        queries[base : base + rows, :LANES] = jnp.where(low, query, zero)
        queries[base + rows : base + 2 * rows, :LANES] = jnp.where(low, zero, query)
    for first in range(0, len(query_refs), 2):
        base = 2 * first * rows
        scores = lax.dot_general(
            queries[base : base + 4 * rows, :], keys[...], (((1,), (1,)), ((), ())),
            preferred_element_type=jnp.float32,
        )
        weights = jnp.exp(scores - jnp.max(scores, axis=1, keepdims=True))
        weight_sum = jnp.sum(weights, axis=1, keepdims=True)
        mixed = jnp.dot(
            weights.astype(jnp.bfloat16), values[...], preferred_element_type=jnp.float32
        )
        mixed = mixed / weight_sum
        for side in range(2):
            base = 2 * side * rows
            out_ref[first + side] = jnp.where(
                low, mixed[base : base + rows], mixed[base + rows : base + 2 * rows]
            ).astype(jnp.bfloat16)


def attend_first_kernel(info_ref, *refs):
    chips = len(refs) - 4
    got_refs = refs[:chips]
    out_ref, keys, values, queries = refs[chips:]
    gather_keys(info_ref, got_refs, keys, values)
    attend_rows(got_refs[1::2], keys, values, out_ref, queries)


def attend_second_kernel(info_ref, keys, values, *refs):
    del info_ref
    attend_rows(refs[:-2], keys, values, refs[-2], refs[-1])


def merge_kernel(info_ref, own_ref, got_ref, *out_refs):
    del info_ref
    for at, out_ref in enumerate(out_refs):
        out_ref[0] = own_ref[at + 1]
        out_ref[1] = got_ref[at + 1]


def back_kernel(blocks, info_ref, residual, w_mel, mod_ref, w_out_ref, *refs):
    count = 1 + max(at for at, _, _ in blocks)
    got_refs = refs[:count]
    keep_ref, send_ref, attended, after, speed = refs[count:]
    rows, width = residual.shape
    tiles = width // LANES
    core, chip = info_ref[CORE], info_ref[CHIP]
    for at, place, apart in blocks:
        group = place if apart is None else chip ^ apart
        attended[:, tile_lanes(group)] = got_refs[at][place]
    wide = 2 * LANES
    total = jnp.zeros((rows, LANES), jnp.float32)
    for block in range(width // wide):
        lanes = slice(block * wide, (block + 1) * wide)
        branch = jnp.dot(attended[...], w_out_ref[:, lanes], preferred_element_type=jnp.float32)
        value = residual[:, lanes] + mod_ref[2:3, lanes] * branch
        after[:, lanes] = value
        total = total + value[:, :LANES] + value[:, LANES:]

    def store(lanes, value):
        after[:, lanes] = value

    row_norm(lambda tile: after[:, tile_lanes(tile)], store, tiles, mod_ref, 3, total)
    speed[...] = lax.dot_general(
        after[...].astype(jnp.bfloat16), w_mel[...], (((1,), (1,)), ((), ())),
        preferred_element_type=jnp.float32,
    )
    half = rows // 2
    keep_ref[...] = speed[pl.ds(pl.multiple_of(core * half, 8), half), :]
    send_ref[...] = speed[pl.ds(pl.multiple_of((1 - core) * half, 8), half), :]


def call(kernel, out_shape, inputs, scratch, hbm=()):
    single = not isinstance(out_shape, tuple)
    specs = [hbm_spec() if at in hbm else vmem_spec() for at in range(1, len(inputs))]
    inputs = list(inputs)
    for at in hbm:
        inputs[at] = pltpu.with_memory_space_constraint(inputs[at], pltpu.HBM)
    return pl.pallas_call(
        kernel,
        out_shape=out_shape,
        in_specs=[smem_spec()] + specs,
        out_specs=vmem_spec() if single else tuple(vmem_spec() for _ in out_shape),
        scratch_shapes=scratch,
        compiler_params=pltpu.CompilerParams(vmem_limit_bytes=GRANT),
    )(*inputs)


def array(shape, dtype=jnp.float32):
    return jax.ShapeDtypeStruct(shape, dtype)


def project(normed, w_qkv, tables, info, firsts, origin=None):
    shape = array((3, normed.shape[0], LANES), jnp.bfloat16)
    return call(
        functools.partial(project_kernel, tuple(firsts), origin),
        (shape,) * (2 * len(firsts)),
        (info, normed, w_qkv) + tables,
        [],
    )


def same_core(count):
    return [list(range(core, count, 2)) for core in range(2)]


def facing_pairs(clips, count):
    pairs = []
    for clip in range(clips):
        base = clip * count
        for at in range(1, count - 1, 2):
            pairs += [(base + at, base + at + 1), (base + at + 1, base + at)]
        if clip ^ 1 < clips:
            pairs += [(base + end, (clip ^ 1) * count + end) for end in (0, count - 1)]
    return pairs


def across(value, apart, count):
    return lax.ppermute(value, "seq", [(i, i ^ apart) for i in range(count)])


def to_groups(values, subs):
    rows, _ = values.shape
    grouped = values.reshape(subs, rows // subs, HEADS, HEAD_DIM).transpose(2, 0, 1, 3)
    return grouped.reshape(HEADS * subs, rows // subs, HEAD_DIM)


def from_groups(grouped, rows, subs):
    split = grouped.reshape(HEADS, subs, rows // subs, HEAD_DIM).transpose(1, 2, 0, 3)
    return split.reshape(rows, HEADS * HEAD_DIM)


def attend_blocks(queries, keys, values, live):
    groups, total, _ = queries.shape
    block = max(size for size in range(1, min(total, 1024) + 1) if total % size == 0)
    blocks = queries.reshape(groups, total // block, block, HEAD_DIM).transpose(1, 0, 2, 3)
    live = live[None, None, :]

    def one_block(query):
        scores = jnp.einsum("gqd,gkd->gqk", query, keys, preferred_element_type=jnp.float32)
        scores = jnp.where(live, scores, NEGATIVE)
        weights = jnp.exp(scores - jnp.max(scores, axis=-1, keepdims=True))
        weights = jnp.where(live, weights, 0.0)
        mixed = jnp.einsum(
            "gqk,gkd->gqd",
            weights.astype(jnp.bfloat16),
            values,
            preferred_element_type=jnp.float32,
        )
        return (mixed / jnp.sum(weights, axis=-1)[..., None]).astype(jnp.bfloat16)

    return lax.map(one_block, blocks).transpose(1, 0, 2, 3).reshape(groups, total, HEAD_DIM)


def attend_any(normed, w_qkv, tables, info, length, count):
    rows = normed.shape[0]
    chips = count // 2
    groups = HEADS * HEAD_DIM // LANES
    sent = project(normed, w_qkv, tables, info, range(0, groups, 2), 0)
    subs = max(1, chips // HEADS)
    chip = lax.axis_index("seq") >> 1
    part_rows = rows // subs

    def exchange(part):
        whole = jnp.concatenate([group[part] for group in sent], axis=1)
        return lax.all_to_all(
            to_groups(whole, subs), "seq", split_axis=0, concat_axis=1, tiled=True,
            axis_index_groups=same_core(count),
        )

    queries, keys, values = (exchange(part) for part in range(3))

    def frames_of(sub):
        start = jnp.arange(chips, dtype=jnp.int32)[:, None] * rows + sub * part_rows
        return (start + jnp.arange(part_rows, dtype=jnp.int32)[None, :]).reshape(-1)

    frames = [frames_of(chip % subs)]
    parts = [(keys, values)]
    for apart in range(1, subs):
        perm = []
        for i in range(count):
            at = i // 2
            target = at - at % subs + (at + apart) % subs
            perm.append((i, 2 * target + i % 2))
        parts.append(tuple(lax.ppermute(part, "seq", perm) for part in (keys, values)))
        frames.append(frames_of((chip - apart) % subs))
    keys = jnp.concatenate([part[0] for part in parts], axis=1)
    values = jnp.concatenate([part[1] for part in parts], axis=1)
    attended = attend_blocks(queries, keys, values, jnp.concatenate(frames) < length)
    back = lax.all_to_all(
        attended, "seq", split_axis=1, concat_axis=0, tiled=True,
        axis_index_groups=same_core(count),
    )
    return from_groups(back, rows, subs).reshape(rows, groups, LANES).transpose(1, 0, 2)


def chips_hold_groups(count):
    chips = count // 2
    return chips == HEADS * HEAD_DIM // LANES and chips >= 4 and chips & (chips - 1) == 0


def send_order(chips):
    far = list(range(chips // 2, chips, 2))
    return far[:1] + list(range(2, chips // 2, 2)) + far[1:] + [0]


def attend_chips(normed, w_qkv, tables, info, count):
    rows = normed.shape[0]
    chips = count // 2
    held = {}
    for first in send_order(chips):
        made = project(normed, w_qkv, tables, info, [first])
        for side in range(2):
            apart = first + side
            held[apart] = across(made[side], 2 * apart, count) if apart else made[side]
    total, half = chips * rows, chips // 2
    queries = VMEM((total, 2 * LANES), jnp.bfloat16)
    crossing, keys, values = call(
        attend_first_kernel,
        (
            array((half, rows, LANES), jnp.bfloat16),
            array((total, 2 * LANES), jnp.bfloat16),
            array((total, LANES), jnp.bfloat16),
        ),
        (info,) + tuple(held[apart] for apart in range(chips)),
        [queries],
    )
    crossed = across(crossing, 2, count)
    staying = call(
        attend_second_kernel,
        array((half, rows, LANES), jnp.bfloat16),
        (info, keys, values) + tuple(held[apart] for apart in range(0, chips, 2)),
        [queries],
    )
    joined = call(
        merge_kernel,
        (array((2, rows, LANES), jnp.bfloat16),) * (half - 1),
        (info, staying, crossed),
        [],
    )
    back, blocks = [staying, crossed], [(0, 0, 0), (1, 0, 1)]
    apart_first = sorted(range(1, half), reverse=True)
    got = {apart: across(joined[apart - 1], 4 * apart, count) for apart in apart_first}
    for apart in range(1, half):
        blocks += [(len(back), side, 2 * apart + side) for side in range(2)]
        back.append(got[apart])
    return back, blocks


def per_device(
    hidden, latent, lengths, step_index, guidance, modulation, conv_kernel, w_qkv, w_out, w_mel
):
    copies, rows, width = hidden.shape
    count = lax.axis_size("seq")
    index = lax.axis_index("seq").astype(jnp.int32)
    chip, core = index >> 1, index & 1
    chip_rows = 2 * rows
    info = jnp.stack([core, chip, lengths[0]])

    edges = lax.dynamic_slice(hidden, (0, core * (rows - HALO), 0), (copies, HALO, width))
    partner = lax.dynamic_slice(hidden, (1 - core, 0, 0), (1, rows, width))[0]
    near = lax.ppermute(edges, ("clip", "seq"), facing_pairs(lax.axis_size("clip"), count))
    far = across(near, 1, count)
    partner = across(partner, 1, count)
    own, taps, mods, is_first, live = call(
        stage_kernel,
        (
            array((rows, width), jnp.bfloat16),
            array(conv_kernel.shape),
            array(modulation.shape),
            array(latent.shape),
            array(latent.shape),
        ),
        (info, hidden, conv_kernel, modulation),
        [pltpu.SemaphoreType.DMA((3,))],
        hbm=(1, 2, 3),
    )
    tables = rotary_tables(chip * chip_rows + jnp.arange(chip_rows, dtype=jnp.int32))
    residual, normed, weight = call(
        front_kernel,
        (
            array((chip_rows, width)),
            array((chip_rows, width), jnp.bfloat16),
            array(w_qkv.shape, jnp.bfloat16),
        ),
        (info, own, partner, near, far, taps, mods, w_qkv),
        [VMEM((chip_rows + 2 * HALO, LANES), jnp.float32), pltpu.SemaphoreType.DMA((8,))],
        hbm=(7,),
    )
    if chips_hold_groups(count):
        back, blocks = attend_chips(normed, weight, tables, info, count)
    else:
        back = [attend_any(normed, weight, tables, info, lengths[0], count)]
        blocks = [(0, group, None) for group in range(back[0].shape[0])]
    mels = w_mel.shape[1]
    keep, send = call(
        functools.partial(back_kernel, tuple(blocks)),
        (array((rows, mels)),) * 2,
        (info, residual, w_mel.T, mods, w_out) + tuple(back),
        [
            VMEM((chip_rows, HEADS * HEAD_DIM), jnp.bfloat16),
            VMEM((chip_rows, width), jnp.float32),
            VMEM((chip_rows, mels), jnp.float32),
        ],
    )
    other = across(send, 1, count)
    first = jnp.where(is_first > 0.5, keep, other)
    second = jnp.where(is_first > 0.5, other, keep)
    guided = first + guidance[0] * (first - second)
    velocity = jnp.where(live > 0.5, guided, 0.0)
    progress = step_index[0].astype(jnp.float32) / STEPS
    time_now = 1.0 - jnp.cos(0.5 * jnp.pi * progress)
    return (velocity, latent + (1.0 - time_now) * velocity)


def solution(mesh):
    return jax.shard_map(
        per_device,
        mesh=mesh,
        in_specs=(
            P(None, ("clip", "seq"), None),
            P(("clip", "seq"), None),
            P("clip"),
            P(),
            P(),
            P(),
            P(),
            P(),
            P(),
            P(),
        ),
        out_specs=(P(("clip", "seq"), None), P(("clip", "seq"), None)),
        check_vma=False,
    )
```

profile of v0, /device:TPU:0, one launch (start us, length us, event | category | flops | bytes accessed | tf_op | source)
XLA Modules:
  0.0 58.1 jit_solution(8824104863944581707)
XLA Ops:
  0.6 0.9 %constant_dynamic-slice_fusion = bf16[2,16,1536]{2,1,0:T(8,128)(2,1)S(1)} fusion(bf16[2,56,1536]{2,1,0:T(8,128)(2,1)} %hidden_hbm.1, s32[]{:T(128)S(6)} %select_n.45), kind=kLoop, calls=%fused_computation.15 | loop fusion | bytes 196612 | tf_op jit(solution)/shard_map/dynamic_slice | solution.py:475
  1.5 3.0 %collective-permute-start.1 = (bf16[2,16,1536]{2,1,0:T(8,128)(2,1)S(1)}, bf16[2,16,1536]{2,1,0:T(8,128)(2,1)S(1)}, u32[]{:S(2)}, u32[]{:S(2)}) collective-permute-start(bf16[2,16,1536]{2,1,0:T(8,128)(2,1)S(1)} %constant_dynamic-slice_fusion), channel_id=1, source_target_pairs={{1,2},{2,1},{3,4},{4,3},{5,6},{6,5},{7,8},{8,7},{9,10},{10,9},{11,... | collective-permute-start | bytes 294920 | tf_op jit(solution)/shard_map/ppermute | solution.py:477
  4.5 0.9 %dynamic-slice_bitcast_fusion = bf16[56,1536]{1,0:T(8,128)(2,1)S(1)} fusion(bf16[2,56,1536]{2,1,0:T(8,128)(2,1)} %hidden_hbm.1, s32[]{:T(128)S(6)} %select_n.44), kind=kLoop, calls=%fused_computation | loop fusion | bytes 344068 | tf_op jit(solution)/shard_map/squeeze | solution.py:476
  5.4 0.2 collective-permute-start
  5.7 0.3 fusion
  6.6 0.5 collective-permute-done.1.near_ref
  7.1 0.1 collective-permute-start.2
  7.2 0.1 pad_add_fusion.info_ref
  7.3 1.6 %shard_map.113 = (bf16[56,1536]{1,0:T(8,128)(2,1)S(1)}, f32[31,1536]{1,0:T(8,128)S(1)}, f32[5,1536]{1,0:T(8,128)S(1)}, f32[56,100]{1,0:T(8,128)S(1)}, f32[56,100]{1,0:T(8,128)S(1)}) custom-call(s32[3]{0:T(128)S(1)} %pad_add_fusion.info_ref, bf16[2,56,1536]{2,1,0:T(8,128)(2,1)} %hidden_hbm.1, f32[31,1536]{1,0:T(8,128)} %taps_hbm.1, f32[5,1536]{1,0:T(8,128)} %mod_hbm.1), custom_call_target="tpu_custom_call" | custom-call | tf_op jit(solution)/shard_map/pallas_call | solution.py:294
  8.9 0.0 collective-permute-done.partner_ref
  8.9 0.0 collective-permute-done.2.far_ref
  8.9 4.3 %shard_map.114 = (f32[112,1536]{1,0:T(8,128)S(1)}, bf16[112,1536]{1,0:T(8,128)(2,1)S(1)}, bf16[1536,3072]{1,0:T(8,128)(2,1)S(1)}) custom-call(s32[3]{0:T(128)S(1)} %pad_add_fusion.info_ref, bf16[56,1536]{1,0:T(8,128)(2,1)S(1)} %get-tuple-element.28.own_ref, bf16[56,1536]{1,0:T(8,128)(2,1)S(1)} %collective-permute-done.partner_ref, ...), custom_call_target="tpu_custom_call" | custom-call | tf_op jit(solution)/shard_map/pallas_call | solution.py:294
  13.2 1.2 %shard_map.118 = (bf16[3,112,128]{2,1,0:T(8,128)(2,1)S(1)}, bf16[3,112,128]{2,1,0:T(8,128)(2,1)S(1)}) custom-call(s32[3]{0:T(128)S(1)} %pad_add_fusion.info_ref, bf16[112,1536]{1,0:T(8,128)(2,1)S(1)} %get-tuple-element.32.normed_ref, bf16[1536,3072]{1,0:T(8,128)(2,1)S(1)} %get-tuple-element.33.weight_ref, f32[112,128]{1,0:T(8,128)S(1)} %get-tuple-element.53.cos_ref, ...), custom_call_target="tpu_custom_call" | custom-call | tf_op jit(solution)/shard_map/pallas_call | solution.py:294
  14.4 4.5 %collective-permute-start.8 = (bf16[3,112,128]{2,1,0:T(8,128)(2,1)S(1)}, bf16[3,112,128]{2,1,0:T(8,128)(2,1)S(1)}, u32[]{:S(2)}, u32[]{:S(2)}) collective-permute-start(bf16[3,112,128]{2,1,0:T(8,128)(2,1)S(1)} %get-tuple-element.40), channel_id=1, source_target_pairs={{0,12},{1,13},{2,14},{3,15},{4,8},{5,9},{6,10},{7,11},{8,4},{9,5},... | collective-permute-start | bytes 258056 | tf_op jit(solution)/shard_map/ppermute | solution.py:334
  19.0 1.2 %collective-permute-start.9 = (bf16[3,112,128]{2,1,0:T(8,128)(2,1)S(1)}, bf16[3,112,128]{2,1,0:T(8,128)(2,1)S(1)}, u32[]{:S(2)}, u32[]{:S(2)}) collective-permute-start(bf16[3,112,128]{2,1,0:T(8,128)(2,1)S(1)} %get-tuple-element.41), channel_id=1, source_target_pairs={{0,14},{1,15},{2,12},{3,13},{4,10},{5,11},{6,8},{7,9},{8,6},{9,7},... | collective-permute-start | bytes 258056 | tf_op jit(solution)/shard_map/ppermute | solution.py:334
  20.2 1.2 %shard_map.117 = (bf16[3,112,128]{2,1,0:T(8,128)(2,1)S(1)}, bf16[3,112,128]{2,1,0:T(8,128)(2,1)S(1)}) custom-call(s32[3]{0:T(128)S(1)} %pad_add_fusion.info_ref, bf16[112,1536]{1,0:T(8,128)(2,1)S(1)} %get-tuple-element.32.normed_ref, bf16[1536,3072]{1,0:T(8,128)(2,1)S(1)} %get-tuple-element.33.weight_ref, f32[112,128]{1,0:T(8,128)S(1)} %get-tuple-element.53.cos_ref, ...), custom_call_target="tpu_custom_call" | custom-call | tf_op jit(solution)/shard_map/pallas_call | solution.py:294
  21.4 0.0 copy-start
  21.4 0.0 copy-start.1
  21.4 1.2 %shard_map.116 = (bf16[3,112,128]{2,1,0:T(8,128)(2,1)S(1)}, bf16[3,112,128]{2,1,0:T(8,128)(2,1)S(1)}) custom-call(s32[3]{0:T(128)S(1)} %pad_add_fusion.info_ref, bf16[112,1536]{1,0:T(8,128)(2,1)S(1)} %get-tuple-element.32.normed_ref, bf16[1536,3072]{1,0:T(8,128)(2,1)S(1)} %get-tuple-element.33.weight_ref, f32[112,128]{1,0:T(8,128)S(1)} %get-tuple-element.53.cos_ref, ...), custom_call_target="tpu_custom_call" | custom-call | tf_op jit(solution)/shard_map/pallas_call | solution.py:294
  22.6 0.0 copy-start.2
  22.6 1.2 %shard_map.115 = (bf16[3,112,128]{2,1,0:T(8,128)(2,1)S(1)}, bf16[3,112,128]{2,1,0:T(8,128)(2,1)S(1)}) custom-call(s32[3]{0:T(128)S(1)} %pad_add_fusion.info_ref, bf16[112,1536]{1,0:T(8,128)(2,1)S(1)} %get-tuple-element.32.normed_ref, bf16[1536,3072]{1,0:T(8,128)(2,1)S(1)} %get-tuple-element.33.weight_ref, f32[112,128]{1,0:T(8,128)S(1)} %get-tuple-element.53.cos_ref, ...), custom_call_target="tpu_custom_call" | custom-call | tf_op jit(solution)/shard_map/pallas_call | solution.py:294
  23.8 0.9 %collective-permute-start.6 = (bf16[3,112,128]{2,1,0:T(8,128)(2,1)S(1)}, bf16[3,112,128]{2,1,0:T(8,128)(2,1)S(1)}, u32[]{:S(2)}, u32[]{:S(2)}) collective-permute-start(bf16[3,112,128]{2,1,0:T(8,128)(2,1)S(1)} %get-tuple-element.38), channel_id=1, source_target_pairs={{0,8},{1,9},{2,10},{3,11},{4,12},{5,13},{6,14},{7,15},{8,0},{9,1},... | collective-permute-start | bytes 258056 | tf_op jit(solution)/shard_map/ppermute | solution.py:334
  24.6 1.9 %collective-permute-start.7 = (bf16[3,112,128]{2,1,0:T(8,128)(2,1)S(1)}, bf16[3,112,128]{2,1,0:T(8,128)(2,1)S(1)}, u32[]{:S(2)}, u32[]{:S(2)}) collective-permute-start(bf16[3,112,128]{2,1,0:T(8,128)(2,1)S(1)} %get-tuple-element.39), channel_id=1, source_target_pairs={{0,10},{1,11},{2,8},{3,9},{4,14},{5,15},{6,12},{7,13},{8,2},{9,3},... | collective-permute-start | bytes 258056 | tf_op jit(solution)/shard_map/ppermute | solution.py:334
  26.5 1.5 %collective-permute-start.4 = (bf16[3,112,128]{2,1,0:T(8,128)(2,1)S(1)}, bf16[3,112,128]{2,1,0:T(8,128)(2,1)S(1)}, u32[]{:S(2)}, u32[]{:S(2)}) collective-permute-start(bf16[3,112,128]{2,1,0:T(8,128)(2,1)S(1)} %get-tuple-element.36), channel_id=1, source_target_pairs={{0,4},{1,5},{2,6},{3,7},{4,0},{5,1},{6,2},{7,3},{8,12},{9,13},{10,... | collective-permute-start | bytes 258056 | tf_op jit(solution)/shard_map/ppermute | solution.py:334
  28.0 0.0 collective-permute-done.8.refs_6_.refs_3_
  28.0 1.6 %collective-permute-start.5 = (bf16[3,112,128]{2,1,0:T(8,128)(2,1)S(1)}, bf16[3,112,128]{2,1,0:T(8,128)(2,1)S(1)}, u32[]{:S(2)}, u32[]{:S(2)}) collective-permute-start(bf16[3,112,128]{2,1,0:T(8,128)(2,1)S(1)} %get-tuple-element.37), channel_id=1, source_target_pairs={{0,6},{1,7},{2,4},{3,5},{4,2},{5,3},{6,0},{7,1},{8,14},{9,15},{10,... | collective-permute-start | bytes 258056 | tf_op jit(solution)/shard_map/ppermute | solution.py:334
  29.7 0.0 collective-permute-done.9.refs_7_
  29.7 0.3 collective-permute-start.3
  30.0 2.0 %collective-permute-done.6.refs_4_.refs_2_ = bf16[3,112,128]{2,1,0:T(8,128)(2,1)S(1)} collective-permute-done((bf16[3,112,128]{2,1,0:T(8,128)(2,1)S(1)}, bf16[3,112,128]{2,1,0:T(8,128)(2,1)S(1)}, u32[]{:S(2)}, u32[]{:S(2)}) %collective-permute-start.6) | collective-permute-done | bytes 86048 | tf_op jit(solution)/shard_map/ppermute | solution.py:334
  32.0 3.2 %collective-permute-done.7.refs_5_ = bf16[3,112,128]{2,1,0:T(8,128)(2,1)S(1)} collective-permute-done((bf16[3,112,128]{2,1,0:T(8,128)(2,1)S(1)}, bf16[3,112,128]{2,1,0:T(8,128)(2,1)S(1)}, u32[]{:S(2)}, u32[]{:S(2)}) %collective-permute-start.7) | collective-permute-done | bytes 86048 | tf_op jit(solution)/shard_map/ppermute | solution.py:334
  35.2 0.0 collective-permute-done.4.refs_2_.refs_1_
  35.2 1.4 %collective-permute-done.5.refs_3_ = bf16[3,112,128]{2,1,0:T(8,128)(2,1)S(1)} collective-permute-done((bf16[3,112,128]{2,1,0:T(8,128)(2,1)S(1)}, bf16[3,112,128]{2,1,0:T(8,128)(2,1)S(1)}, u32[]{:S(2)}, u32[]{:S(2)}) %collective-permute-start.5) | collective-permute-done | bytes 86048 | tf_op jit(solution)/shard_map/ppermute | solution.py:334
  36.6 0.3 collective-permute-done.3.refs_1_
  36.8 2.4 %shard_map.119 = (bf16[4,112,128]{2,1,0:T(8,128)(2,1)S(1)}, bf16[896,256]{1,0:T(8,128)(2,1)S(1)}, bf16[896,128]{1,0:T(8,128)(2,1)S(1)}) custom-call(s32[3]{0:T(128)S(1)} %pad_add_fusion.info_ref, bf16[3,112,128]{2,1,0:T(8,128)(2,1)S(1)} %get-tuple-element.34.refs_0_, bf16[3,112,128]{2,1,0:T(8,128)(2,1)S(1)} %collective-permute-done.3.refs_1_, ...), custom_call_target="tpu_custom_call" | custom-call | tf_op jit(solution)/shard_map/pallas_call | solution.py:294
  39.2 1.2 %collective-permute-start.10 = (bf16[4,112,128]{2,1,0:T(8,128)(2,1)S(1)}, bf16[4,112,128]{2,1,0:T(8,128)(2,1)S(1)}, u32[]{:S(2)}, u32[]{:S(2)}) collective-permute-start(bf16[4,112,128]{2,1,0:T(8,128)(2,1)S(1)} %get-tuple-element.44), channel_id=1, source_target_pairs={{0,2},{1,3},{2,0},{3,1},{4,6},{5,7},{6,4},{7,5},{8,10},{9,11},{10,... | collective-permute-start | bytes 344072 | tf_op jit(solution)/shard_map/ppermute | solution.py:334
  40.4 2.3 %shard_map.120.own_ref.refs_0_ = bf16[4,112,128]{2,1,0:T(8,128)(2,1)S(1)} custom-call(s32[3]{0:T(128)S(1)} %pad_add_fusion.info_ref, bf16[896,256]{1,0:T(8,128)(2,1)S(1)} %get-tuple-element.42.keys, bf16[896,128]{1,0:T(8,128)(2,1)S(1)} %get-tuple-element.43.values, bf16[3,112,128]{2,1,0:T(8,128)(2,1)S(1)} %get-tuple-element.34.refs_0_, ...), custom_call_target="tpu_custom_call" | custom-call | tf_op jit(solution)/shard_map/pallas_call | solution.py:294
  42.7 1.4 %collective-permute-done.10.got_ref.refs_1_ = bf16[4,112,128]{2,1,0:T(8,128)(2,1)S(1)} collective-permute-done((bf16[4,112,128]{2,1,0:T(8,128)(2,1)S(1)}, bf16[4,112,128]{2,1,0:T(8,128)(2,1)S(1)}, u32[]{:S(2)}, u32[]{:S(2)}) %collective-permute-start.10) | collective-permute-done | bytes 114720 | tf_op jit(solution)/shard_map/ppermute | solution.py:334
  44.1 0.6 shard_map.121
  44.6 0.1 collective-permute-start.11
  44.7 3.3 %collective-permute-start.12 = (bf16[2,112,128]{2,1,0:T(8,128)(2,1)S(1)}, bf16[2,112,128]{2,1,0:T(8,128)(2,1)S(1)}, u32[]{:S(2)}, u32[]{:S(2)}) collective-permute-start(bf16[2,112,128]{2,1,0:T(8,128)(2,1)S(1)} %get-tuple-element.46), channel_id=1, source_target_pairs={{0,8},{1,9},{2,10},{3,11},{4,12},{5,13},{6,14},{7,15},{8,0},{9,1},... | collective-permute-start | bytes 172040 | tf_op jit(solution)/shard_map/ppermute | solution.py:334
  48.0 1.1 %collective-permute-start.13 = (bf16[2,112,128]{2,1,0:T(8,128)(2,1)S(1)}, bf16[2,112,128]{2,1,0:T(8,128)(2,1)S(1)}, u32[]{:S(2)}, u32[]{:S(2)}) collective-permute-start(bf16[2,112,128]{2,1,0:T(8,128)(2,1)S(1)} %get-tuple-element.47), channel_id=1, source_target_pairs={{0,12},{1,13},{2,14},{3,15},{4,8},{5,9},{6,10},{7,11},{8,4},{9,5},... | collective-permute-start | bytes 172040 | tf_op jit(solution)/shard_map/ppermute | solution.py:334
  49.1 0.0 collective-permute-done.11.refs_2_
  49.1 2.2 %collective-permute-done.12.refs_3_ = bf16[2,112,128]{2,1,0:T(8,128)(2,1)S(1)} collective-permute-done((bf16[2,112,128]{2,1,0:T(8,128)(2,1)S(1)}, bf16[2,112,128]{2,1,0:T(8,128)(2,1)S(1)}, u32[]{:S(2)}, u32[]{:S(2)}) %collective-permute-start.12) | collective-permute-done | bytes 57376 | tf_op jit(solution)/shard_map/ppermute | solution.py:334
  51.3 2.7 %collective-permute-done.13.refs_4_ = bf16[2,112,128]{2,1,0:T(8,128)(2,1)S(1)} collective-permute-done((bf16[2,112,128]{2,1,0:T(8,128)(2,1)S(1)}, bf16[2,112,128]{2,1,0:T(8,128)(2,1)S(1)}, u32[]{:S(2)}, u32[]{:S(2)}) %collective-permute-start.13) | collective-permute-done | bytes 57376 | tf_op jit(solution)/shard_map/ppermute | solution.py:334
  54.0 2.0 %shard_map.122 = (f32[56,100]{1,0:T(8,128)S(1)}, f32[56,100]{1,0:T(8,128)S(1)}) custom-call(s32[3]{0:T(128)S(1)} %pad_add_fusion.info_ref, f32[112,1536]{1,0:T(8,128)S(1)} %get-tuple-element.31.residual, bf16[100,1536]{1,0:T(8,128)(2,1)S(1)} %bitcast.8, f32[5,1536]{1,0:T(8,128)S(1)} %get-tuple-element.30.mod_ref, bf16[1024,1536]{1,0:T(8,128)(2,1)S(1)} %copy-done, ...), custom_call_target="tpu_custom_call" | custom-call | tf_op jit(solution)/shard_map/pallas_call | solution.py:294
  56.0 0.1 collective-permute-start.14
  57.5 0.0 collective-permute-done.14
  57.5 0.6 %multiply_add_fusion = (f32[56,100]{1,0:T(8,128)}, f32[56,100]{1,0:T(8,128)}) fusion(f32[56,100]{1,0:T(8,128)S(1)} %copy-done.2, f32[]{:T(128)} %bitcast.5, f32[56,100]{1,0:T(8,128)S(1)} %collective-permute-done.14, f32[56,100]{1,0:T(8,128)S(1)} %get-tuple-element.48, f32[]{:T(128)} %bitcast.7, f32[56,100]{1,0:T(8,128)S(1)} %get-tuple-element.27, ...), kind=kLoop, calls=%fused_computation.4 | loop fusion | flops 56000 | bytes 156808 | tf_op jit(solution)/shard_map/add | solution.py:528
  (5 shorter events, 0.0 us)
Async XLA Ops:
  1.5 5.6 %collective-permute-start.1 = (bf16[2,16,1536]{2,1,0:T(8,128)(2,1)S(1)}, bf16[2,16,1536]{2,1,0:T(8,128)(2,1)S(1)}, u32[]{:S(2)}, u32[]{:S(2)}) collective-permute-start(bf16[2,16,1536]{2,1,0:T(8,128)(2,1)S(1)} %constant_dynamic-slice_fusion), channel_id=1, source_target_pairs={{1,2},{2,1},{3,4},{4,3},{5,6},{6,5},{7,8},{8,7},{9,10},{10,9},{11,... | collective-permute-start | bytes 294920 | tf_op jit(solution)/shard_map/ppermute | solution.py:477
  5.4 3.4 %collective-permute-start = (bf16[56,1536]{1,0:T(8,128)(2,1)S(1)}, bf16[56,1536]{1,0:T(8,128)(2,1)S(1)}, u32[]{:S(2)}, u32[]{:S(2)}) collective-permute-start(bf16[56,1536]{1,0:T(8,128)(2,1)S(1)} %dynamic-slice_bitcast_fusion), channel_id=1, source_target_pairs={{0,1},{1,0},{2,3},{3,2},{4,5},{5,4},{6,7},{7,6},{8,9},{9,8},{10,11... | collective-permute-start | bytes 516104 | tf_op jit(solution)/shard_map/ppermute | solution.py:334
  7.1 1.8 %collective-permute-start.2 = (bf16[2,16,1536]{2,1,0:T(8,128)(2,1)S(1)}, bf16[2,16,1536]{2,1,0:T(8,128)(2,1)S(1)}, u32[]{:S(2)}, u32[]{:S(2)}) collective-permute-start(bf16[2,16,1536]{2,1,0:T(8,128)(2,1)S(1)} %collective-permute-done.1.near_ref), channel_id=1, source_target_pairs={{0,1},{1,0},{2,3},{3,2},{4,5},{5,4},{6,7},{7,6},{8,9},{9,8},{10,11... | collective-permute-start | bytes 294920 | tf_op jit(solution)/shard_map/ppermute | solution.py:334
  14.4 13.6 %collective-permute-start.8 = (bf16[3,112,128]{2,1,0:T(8,128)(2,1)S(1)}, bf16[3,112,128]{2,1,0:T(8,128)(2,1)S(1)}, u32[]{:S(2)}, u32[]{:S(2)}) collective-permute-start(bf16[3,112,128]{2,1,0:T(8,128)(2,1)S(1)} %get-tuple-element.40), channel_id=1, source_target_pairs={{0,12},{1,13},{2,14},{3,15},{4,8},{5,9},{6,10},{7,11},{8,4},{9,5},... | collective-permute-start | bytes 258056 | tf_op jit(solution)/shard_map/ppermute | solution.py:334
  19.0 10.7 %collective-permute-start.9 = (bf16[3,112,128]{2,1,0:T(8,128)(2,1)S(1)}, bf16[3,112,128]{2,1,0:T(8,128)(2,1)S(1)}, u32[]{:S(2)}, u32[]{:S(2)}) collective-permute-start(bf16[3,112,128]{2,1,0:T(8,128)(2,1)S(1)} %get-tuple-element.41), channel_id=1, source_target_pairs={{0,14},{1,15},{2,12},{3,13},{4,10},{5,11},{6,8},{7,9},{8,6},{9,7},... | collective-permute-start | bytes 258056 | tf_op jit(solution)/shard_map/ppermute | solution.py:334
  21.4 32.6 %copy-start = (bf16[1024,1536]{1,0:T(8,128)(2,1)S(1)}, bf16[1024,1536]{1,0:T(8,128)(2,1)}, u32[]{:S(2)}) copy-start(bf16[1024,1536]{1,0:T(8,128)(2,1)} %w_out_ref.1) | copy-start | bytes 9437188
  21.4 32.6 %copy-start.1 = (bf16[1536,100]{0,1:T(8,128)(2,1)S(1)}, bf16[1536,100]{0,1:T(8,128)(2,1)}, u32[]{:S(2)}) copy-start(bf16[1536,100]{0,1:T(8,128)(2,1)} %param.19) | copy-start | bytes 921604
  22.6 34.9 %copy-start.2 = (f32[56,100]{1,0:T(8,128)S(1)}, f32[56,100]{1,0:T(8,128)}, u32[]{:S(2)}) copy-start(f32[56,100]{1,0:T(8,128)} %param.11) | copy-start | bytes 67204
  23.8 8.3 %collective-permute-start.6 = (bf16[3,112,128]{2,1,0:T(8,128)(2,1)S(1)}, bf16[3,112,128]{2,1,0:T(8,128)(2,1)S(1)}, u32[]{:S(2)}, u32[]{:S(2)}) collective-permute-start(bf16[3,112,128]{2,1,0:T(8,128)(2,1)S(1)} %get-tuple-element.38), channel_id=1, source_target_pairs={{0,8},{1,9},{2,10},{3,11},{4,12},{5,13},{6,14},{7,15},{8,0},{9,1},... | collective-permute-start | bytes 258056 | tf_op jit(solution)/shard_map/ppermute | solution.py:334
  24.6 10.6 %collective-permute-start.7 = (bf16[3,112,128]{2,1,0:T(8,128)(2,1)S(1)}, bf16[3,112,128]{2,1,0:T(8,128)(2,1)S(1)}, u32[]{:S(2)}, u32[]{:S(2)}) collective-permute-start(bf16[3,112,128]{2,1,0:T(8,128)(2,1)S(1)} %get-tuple-element.39), channel_id=1, source_target_pairs={{0,10},{1,11},{2,8},{3,9},{4,14},{5,15},{6,12},{7,13},{8,2},{9,3},... | collective-permute-start | bytes 258056 | tf_op jit(solution)/shard_map/ppermute | solution.py:334
  26.5 8.7 %collective-permute-start.4 = (bf16[3,112,128]{2,1,0:T(8,128)(2,1)S(1)}, bf16[3,112,128]{2,1,0:T(8,128)(2,1)S(1)}, u32[]{:S(2)}, u32[]{:S(2)}) collective-permute-start(bf16[3,112,128]{2,1,0:T(8,128)(2,1)S(1)} %get-tuple-element.36), channel_id=1, source_target_pairs={{0,4},{1,5},{2,6},{3,7},{4,0},{5,1},{6,2},{7,3},{8,12},{9,13},{10,... | collective-permute-start | bytes 258056 | tf_op jit(solution)/shard_map/ppermute | solution.py:334
  28.0 8.5 %collective-permute-start.5 = (bf16[3,112,128]{2,1,0:T(8,128)(2,1)S(1)}, bf16[3,112,128]{2,1,0:T(8,128)(2,1)S(1)}, u32[]{:S(2)}, u32[]{:S(2)}) collective-permute-start(bf16[3,112,128]{2,1,0:T(8,128)(2,1)S(1)} %get-tuple-element.37), channel_id=1, source_target_pairs={{0,6},{1,7},{2,4},{3,5},{4,2},{5,3},{6,0},{7,1},{8,14},{9,15},{10,... | collective-permute-start | bytes 258056 | tf_op jit(solution)/shard_map/ppermute | solution.py:334
  29.7 7.1 %collective-permute-start.3 = (bf16[3,112,128]{2,1,0:T(8,128)(2,1)S(1)}, bf16[3,112,128]{2,1,0:T(8,128)(2,1)S(1)}, u32[]{:S(2)}, u32[]{:S(2)}) collective-permute-start(bf16[3,112,128]{2,1,0:T(8,128)(2,1)S(1)} %get-tuple-element.35), channel_id=1, source_target_pairs={{0,2},{1,3},{2,0},{3,1},{4,6},{5,7},{6,4},{7,5},{8,10},{9,11},{10,... | collective-permute-start | bytes 258056 | tf_op jit(solution)/shard_map/ppermute | solution.py:334
  39.2 4.9 %collective-permute-start.10 = (bf16[4,112,128]{2,1,0:T(8,128)(2,1)S(1)}, bf16[4,112,128]{2,1,0:T(8,128)(2,1)S(1)}, u32[]{:S(2)}, u32[]{:S(2)}) collective-permute-start(bf16[4,112,128]{2,1,0:T(8,128)(2,1)S(1)} %get-tuple-element.44), channel_id=1, source_target_pairs={{0,2},{1,3},{2,0},{3,1},{4,6},{5,7},{6,4},{7,5},{8,10},{9,11},{10,... | collective-permute-start | bytes 344072 | tf_op jit(solution)/shard_map/ppermute | solution.py:334
  44.6 4.5 %collective-permute-start.11 = (bf16[2,112,128]{2,1,0:T(8,128)(2,1)S(1)}, bf16[2,112,128]{2,1,0:T(8,128)(2,1)S(1)}, u32[]{:S(2)}, u32[]{:S(2)}) collective-permute-start(bf16[2,112,128]{2,1,0:T(8,128)(2,1)S(1)} %get-tuple-element.45), channel_id=1, source_target_pairs={{0,4},{1,5},{2,6},{3,7},{4,0},{5,1},{6,2},{7,3},{8,12},{9,13},{10,... | collective-permute-start | bytes 172040 | tf_op jit(solution)/shard_map/ppermute | solution.py:334
  44.7 6.6 %collective-permute-start.12 = (bf16[2,112,128]{2,1,0:T(8,128)(2,1)S(1)}, bf16[2,112,128]{2,1,0:T(8,128)(2,1)S(1)}, u32[]{:S(2)}, u32[]{:S(2)}) collective-permute-start(bf16[2,112,128]{2,1,0:T(8,128)(2,1)S(1)} %get-tuple-element.46), channel_id=1, source_target_pairs={{0,8},{1,9},{2,10},{3,11},{4,12},{5,13},{6,14},{7,15},{8,0},{9,1},... | collective-permute-start | bytes 172040 | tf_op jit(solution)/shard_map/ppermute | solution.py:334
  48.0 6.0 %collective-permute-start.13 = (bf16[2,112,128]{2,1,0:T(8,128)(2,1)S(1)}, bf16[2,112,128]{2,1,0:T(8,128)(2,1)S(1)}, u32[]{:S(2)}, u32[]{:S(2)}) collective-permute-start(bf16[2,112,128]{2,1,0:T(8,128)(2,1)S(1)} %get-tuple-element.47), channel_id=1, source_target_pairs={{0,12},{1,13},{2,14},{3,15},{4,8},{5,9},{6,10},{7,11},{8,4},{9,5},... | collective-permute-start | bytes 172040 | tf_op jit(solution)/shard_map/ppermute | solution.py:334
  56.0 1.5 %collective-permute-start.14 = (f32[56,100]{1,0:T(8,128)S(1)}, f32[56,100]{1,0:T(8,128)S(1)}, u32[]{:S(2)}, u32[]{:S(2)}) collective-permute-start(f32[56,100]{1,0:T(8,128)S(1)} %get-tuple-element.49), channel_id=1, source_target_pairs={{0,1},{1,0},{2,3},{3,2},{4,5},{5,4},{6,7},{7,6},{8,9},{9,8},{10,11... | collective-permute-start | bytes 67208 | tf_op jit(solution)/shard_map/ppermute | solution.py:334
where the time goes:
time: 58.4 us; the launch traced here: 58.1 us
  starting transfers between devices  21 us (36%)
  Pallas kernels  17.9 us (31%)
  waiting for transfers between devices  13.5 us (23%)
  between operations  2.83 us (5%)
  local copies, waits for them, and re-layouts  1.86 us (3%)
  other arithmetic  1.01 us (2%)
    ppermute x14, starting transfers between devices, across(): return lax.ppermute(value, 'seq', [(i, i ^ apart) for i in range(count)])  18 us
    pallas_call x10, Pallas kernels, call(): pl.pallas_call(kernel, out_shape=out_shape, in_specs=[smem_spec()] + spec...  17.9 us
    ppermute x14, waiting for transfers between devices, across(): return lax.ppermute(value, 'seq', [(i, i ^ apart) for i in range(count)])  13 us
    ppermute x1, starting transfers between devices, per_device(): lax.ppermute(edges, ('clip', 'seq'), facing_pairs(lax.axis_size('clip'),...  2.97 us
  transfers between devices with their start and end apart: 15, of which 8 were waited for; matrix products, arithmetic and copies ran while one was open for 2% of the time, Pallas kernels for 13%

commit v1 on v0

--- a/solution.py
+++ b/solution.py
@@ -189,20 +189,19 @@
             out_refs[2 * at + 1][part] = jnp.where(swap, sides[0], sides[1]).astype(jnp.bfloat16)
 
 
-def gather_keys(info_ref, got_refs, keys, values):
-    _, rows, _ = got_refs[0].shape
-    length, chip = info_ref[LENGTH], info_ref[CHIP]
+def place_keys(info_ref, apart, got_ref, keys, values, first):
+    _, rows, _ = got_ref.shape
+    chip = info_ref[CHIP] ^ apart
     lane = lax.broadcasted_iota(jnp.int32, (rows, LANES), 1)
     row = lax.broadcasted_iota(jnp.int32, (rows, LANES), 0)
-    for apart, got_ref in enumerate(got_refs):
-        here = slice(apart * rows, (apart + 1) * rows)
-        keys[here, :LANES] = got_ref[1]
-        dead = (lane == 0) & (row + (chip ^ apart) * rows >= length)
-        keys[here, LANES:] = jnp.where(dead, NEGATIVE, 0.0).astype(jnp.bfloat16)
-        values[here, :] = got_ref[2]
-
-
-def attend_rows(query_refs, keys, values, out_ref, queries):
+    here = slice(first, first + rows)
+    keys[here, :LANES] = got_ref[1]
+    dead = (lane == 0) & (row + chip * rows >= info_ref[LENGTH])
+    keys[here, LANES:] = jnp.where(dead, NEGATIVE, 0.0).astype(jnp.bfloat16)
+    values[here, :] = got_ref[2]
+
+
+def place_queries(query_refs, queries):
     _, rows, _ = query_refs[0].shape
     low = lax.broadcasted_iota(jnp.int32, (rows, LANES), 1) < HEAD_DIM
     zero = jnp.zeros((rows, LANES), jnp.bfloat16)
@@ -214,36 +213,81 @@
         base = 2 * at * rows
         queries[base : base + rows, :LANES] = jnp.where(low, query, zero)
         queries[base + rows : base + 2 * rows, :LANES] = jnp.where(low, zero, query)
-    for first in range(0, len(query_refs), 2):
-        base = 2 * first * rows
-        scores = lax.dot_general(
-            queries[base : base + 4 * rows, :], keys[...], (((1,), (1,)), ((), ())),
-            preferred_element_type=jnp.float32,
-        )
+
+
+def score(queries, keys):
+    return lax.dot_general(
+        queries, keys, (((1,), (1,)), ((), ())), preferred_element_type=jnp.float32
+    )
+
+
+def mix(weights, values):
+    return jnp.dot(weights.astype(jnp.bfloat16), values, preferred_element_type=jnp.float32)
+
+
+def store_heads(mixed, out_ref, first):
+    _, rows, _ = out_ref.shape
+    low = lax.broadcasted_iota(jnp.int32, (rows, LANES), 1) < HEAD_DIM
+    for at in range(mixed.shape[0] // (2 * rows)):
+        base = 2 * at * rows
+        out_ref[first + at] = jnp.where(
+            low, mixed[base : base + rows], mixed[base + rows : base + 2 * rows]
+        ).astype(jnp.bfloat16)
+
+
+def attend_rows(keys, values, queries, out_ref, first):
+    _, rows, _ = out_ref.shape
+    total = queries.shape[0]
+    for base in range(0, total, 4 * rows):
+        block = slice(base, min(base + 4 * rows, total))
+        scores = score(queries[block, :], keys[...])
         weights = jnp.exp(scores - jnp.max(scores, axis=1, keepdims=True))
         weight_sum = jnp.sum(weights, axis=1, keepdims=True)
-        mixed = jnp.dot(
-            weights.astype(jnp.bfloat16), values[...], preferred_element_type=jnp.float32
-        )
-        mixed = mixed / weight_sum
-        for side in range(2):
-            base = 2 * side * rows
-            out_ref[first + side] = jnp.where(
-                low, mixed[base : base + rows], mixed[base + rows : base + 2 * rows]
-            ).astype(jnp.bfloat16)
-
-
-def attend_first_kernel(info_ref, *refs):
-    chips = len(refs) - 4
+        store_heads(mix(weights, values[...]) / weight_sum, out_ref, first + base // (2 * rows))
+
+
+def attend_early_kernel(info_ref, *refs):
+    chips = len(refs) - 6
     got_refs = refs[:chips]
-    out_ref, keys, values, queries = refs[chips:]
-    gather_keys(info_ref, got_refs, keys, values)
-    attend_rows(got_refs[1::2], keys, values, out_ref, queries)
+    keys, values, queries, mixed_ref, peak_ref, sum_ref = refs[chips:]
+    _, rows, _ = got_refs[0].shape
+    for apart, got_ref in enumerate(got_refs):
+        place_keys(info_ref, apart, got_ref, keys, values, apart * rows)
+    place_queries(got_refs[1::2], queries)
+    scores = score(queries[...], keys[...])
+    peak = jnp.max(scores, axis=1, keepdims=True)
+    weights = jnp.exp(scores - peak)
+    peak_ref[...] = jnp.broadcast_to(peak, peak_ref.shape)
+    sum_ref[...] = jnp.broadcast_to(jnp.sum(weights, axis=1, keepdims=True), sum_ref.shape)
+    mixed_ref[...] = mix(weights, values[...])
+
+
+def attend_last_kernel(
+    info_ref, early_keys, early_values, early_queries, mixed_ref, peak_ref, sum_ref, last_ref,
+    out_ref, keys, values, queries,
+):
+    held, _ = early_values.shape
+    _, rows, _ = last_ref.shape
+    keys[:held, :] = early_keys[...]
+    values[:held, :] = early_values[...]
+    place_keys(info_ref, held // rows, last_ref, keys, values, held)
+    place_queries([last_ref], queries)
+    attend_rows(keys, values, queries, out_ref, out_ref.shape[0] - 1)
+    scores = score(early_queries[...], keys[held:, :])
+    peak = peak_ref[...]
+    joined = jnp.maximum(peak, jnp.max(scores, axis=1, keepdims=True))
+    scale = jnp.exp(peak - joined)
+    weights = jnp.exp(scores - joined[:, : scores.shape[1]])
+    weight_sum = sum_ref[...] * scale + jnp.sum(weights, axis=1, keepdims=True)
+    mixed = mixed_ref[...] * scale + mix(weights, values[held:, :])
+    store_heads(mixed / weight_sum, out_ref, 0)
 
 
 def attend_second_kernel(info_ref, keys, values, *refs):
     del info_ref
-    attend_rows(refs[:-2], keys, values, refs[-2], refs[-1])
+    out_ref, queries = refs[-2:]
+    place_queries(refs[:-2], queries)
+    attend_rows(keys, values, queries, out_ref, 0)
 
 
 def merge_kernel(info_ref, own_ref, got_ref, *out_refs):
@@ -429,23 +473,34 @@
             apart = first + side
             held[apart] = across(made[side], 2 * apart, count) if apart else made[side]
     total, half = chips * rows, chips // 2
-    queries = VMEM((total, 2 * LANES), jnp.bfloat16)
+    early, early_rows = total - rows, 2 * (half - 1) * rows
+    parts = call(
+        attend_early_kernel,
+        (
+            array((early, 2 * LANES), jnp.bfloat16),
+            array((early, LANES), jnp.bfloat16),
+            array((early_rows, 2 * LANES), jnp.bfloat16),
+        )
+        + (array((early_rows, LANES)),) * 3,
+        (info,) + tuple(held[apart] for apart in range(chips - 1)),
+        [],
+    )
     crossing, keys, values = call(
-        attend_first_kernel,
+        attend_last_kernel,
         (
             array((half, rows, LANES), jnp.bfloat16),
             array((total, 2 * LANES), jnp.bfloat16),
             array((total, LANES), jnp.bfloat16),
         ),
-        (info,) + tuple(held[apart] for apart in range(chips)),
-        [queries],
+        (info,) + tuple(parts) + (held[chips - 1],),
+        [VMEM((2 * rows, 2 * LANES), jnp.bfloat16)],
     )
     crossed = across(crossing, 2, count)
     staying = call(
         attend_second_kernel,
         array((half, rows, LANES), jnp.bfloat16),
         (info, keys, values) + tuple(held[apart] for apart in range(0, chips, 2)),
-        [queries],
+        [VMEM((total, 2 * LANES), jnp.bfloat16)],
     )
     joined = call(
         merge_kernel,

time: 58.4 us -> 58 us (level)
  Pallas kernels: 17.9 us -> 19.3 us
  waiting for transfers between devices: 13.5 us -> 12.1 us
    ppermute x14, waiting for transfers between devices: 13 us -> 11.6 us  [across(): return lax.ppermute(value, 'seq', [(i, i ^ apart) for i in range(count)])]
    pallas_call x10 -> x11, Pallas kernels: 17.9 us -> 19.3 us  [call(): pl.pallas_call(kernel, out_shape=out_shape, in_specs=[smem_spec()] + spec...]
  transfers between devices with their start and end apart: 15 -> 15, of which waited for: 8 -> 7; matrix products, arithmetic and copies ran while one was open for 2% -> 2% of each run, Pallas kernels for 13% -> 17%
where the time goes in v1:
time: 58 us; the launch traced here: 57.8 us
  starting transfers between devices  20.7 us (36%)
  Pallas kernels  19.3 us (33%)
  waiting for transfers between devices  12.1 us (21%)
  between operations  2.85 us (5%)
  local copies, waits for them, and re-layouts  1.86 us (3%)
  other arithmetic  1.01 us (2%)
    pallas_call x11, Pallas kernels, call(): pl.pallas_call(kernel, out_shape=out_shape, in_specs=[smem_spec()] + spec...  19.3 us
    ppermute x14, starting transfers between devices, across(): return lax.ppermute(value, 'seq', [(i, i ^ apart) for i in range(count)])  17.7 us
    ppermute x14, waiting for transfers between devices, across(): return lax.ppermute(value, 'seq', [(i, i ^ apart) for i in range(count)])  11.6 us
    ppermute x1, starting transfers between devices, per_device(): lax.ppermute(edges, ('clip', 'seq'), facing_pairs(lax.axis_size('clip'),...  2.97 us
  transfers between devices with their start and end apart: 15, of which 7 were waited for; matrix products, arithmetic and copies ran while one was open for 2% of the time, Pallas kernels for 17%

profile of v1, /device:TPU:0, one launch (start us, length us, event | category | flops | bytes accessed | tf_op | source)
XLA Modules:
  0.0 57.8 jit_solution(12310870158039950019)
XLA Ops:
  0.6 0.9 %constant_dynamic-slice_fusion = bf16[2,16,1536]{2,1,0:T(8,128)(2,1)S(1)} fusion(bf16[2,56,1536]{2,1,0:T(8,128)(2,1)} %hidden_hbm.1, s32[]{:T(128)S(6)} %select_n.45), kind=kLoop, calls=%fused_computation.15 | loop fusion | bytes 196612 | tf_op jit(solution)/shard_map/dynamic_slice | solution.py:530
  1.5 3.0 %collective-permute-start.1 = (bf16[2,16,1536]{2,1,0:T(8,128)(2,1)S(1)}, bf16[2,16,1536]{2,1,0:T(8,128)(2,1)S(1)}, u32[]{:S(2)}, u32[]{:S(2)}) collective-permute-start(bf16[2,16,1536]{2,1,0:T(8,128)(2,1)S(1)} %constant_dynamic-slice_fusion), channel_id=1, source_target_pairs={{1,2},{2,1},{3,4},{4,3},{5,6},{6,5},{7,8},{8,7},{9,10},{10,9},{11,... | collective-permute-start | bytes 294920 | tf_op jit(solution)/shard_map/ppermute | solution.py:532
  4.5 0.9 %dynamic-slice_bitcast_fusion = bf16[56,1536]{1,0:T(8,128)(2,1)S(1)} fusion(bf16[2,56,1536]{2,1,0:T(8,128)(2,1)} %hidden_hbm.1, s32[]{:T(128)S(6)} %select_n.44), kind=kLoop, calls=%fused_computation | loop fusion | bytes 344068 | tf_op jit(solution)/shard_map/squeeze | solution.py:531
  5.4 0.2 collective-permute-start
  5.7 0.3 fusion
  6.6 0.5 collective-permute-done.1.near_ref
  7.1 0.1 collective-permute-start.2
  7.2 0.1 pad_add_fusion.info_ref
  7.3 1.6 %shard_map.113 = (bf16[56,1536]{1,0:T(8,128)(2,1)S(1)}, f32[31,1536]{1,0:T(8,128)S(1)}, f32[5,1536]{1,0:T(8,128)S(1)}, f32[56,100]{1,0:T(8,128)S(1)}, f32[56,100]{1,0:T(8,128)S(1)}) custom-call(s32[3]{0:T(128)S(1)} %pad_add_fusion.info_ref, bf16[2,56,1536]{2,1,0:T(8,128)(2,1)} %hidden_hbm.1, f32[31,1536]{1,0:T(8,128)} %taps_hbm.1, f32[5,1536]{1,0:T(8,128)} %mod_hbm.1), custom_call_target="tpu_custom_call" | custom-call | tf_op jit(solution)/shard_map/pallas_call | solution.py:338
  8.9 0.0 collective-permute-done.partner_ref
  8.9 0.0 collective-permute-done.2.far_ref
  8.9 4.3 %shard_map.114 = (f32[112,1536]{1,0:T(8,128)S(1)}, bf16[112,1536]{1,0:T(8,128)(2,1)S(1)}, bf16[1536,3072]{1,0:T(8,128)(2,1)S(1)}) custom-call(s32[3]{0:T(128)S(1)} %pad_add_fusion.info_ref, bf16[56,1536]{1,0:T(8,128)(2,1)S(1)} %get-tuple-element.34.own_ref, bf16[56,1536]{1,0:T(8,128)(2,1)S(1)} %collective-permute-done.partner_ref, ...), custom_call_target="tpu_custom_call" | custom-call | tf_op jit(solution)/shard_map/pallas_call | solution.py:338
  13.2 1.2 %shard_map.118 = (bf16[3,112,128]{2,1,0:T(8,128)(2,1)S(1)}, bf16[3,112,128]{2,1,0:T(8,128)(2,1)S(1)}) custom-call(s32[3]{0:T(128)S(1)} %pad_add_fusion.info_ref, bf16[112,1536]{1,0:T(8,128)(2,1)S(1)} %get-tuple-element.38.normed_ref, bf16[1536,3072]{1,0:T(8,128)(2,1)S(1)} %get-tuple-element.39.weight_ref, f32[112,128]{1,0:T(8,128)S(1)} %get-tuple-element.65.cos_ref, ...), custom_call_target="tpu_custom_call" | custom-call | tf_op jit(solution)/shard_map/pallas_call | solution.py:338
  14.4 4.5 %collective-permute-start.8 = (bf16[3,112,128]{2,1,0:T(8,128)(2,1)S(1)}, bf16[3,112,128]{2,1,0:T(8,128)(2,1)S(1)}, u32[]{:S(2)}, u32[]{:S(2)}) collective-permute-start(bf16[3,112,128]{2,1,0:T(8,128)(2,1)S(1)} %get-tuple-element.46), channel_id=1, source_target_pairs={{0,12},{1,13},{2,14},{3,15},{4,8},{5,9},{6,10},{7,11},{8,4},{9,5},... | collective-permute-start | bytes 258056 | tf_op jit(solution)/shard_map/ppermute | solution.py:378
  19.0 1.2 %shard_map.117 = (bf16[3,112,128]{2,1,0:T(8,128)(2,1)S(1)}, bf16[3,112,128]{2,1,0:T(8,128)(2,1)S(1)}) custom-call(s32[3]{0:T(128)S(1)} %pad_add_fusion.info_ref, bf16[112,1536]{1,0:T(8,128)(2,1)S(1)} %get-tuple-element.38.normed_ref, bf16[1536,3072]{1,0:T(8,128)(2,1)S(1)} %get-tuple-element.39.weight_ref, f32[112,128]{1,0:T(8,128)S(1)} %get-tuple-element.65.cos_ref, ...), custom_call_target="tpu_custom_call" | custom-call | tf_op jit(solution)/shard_map/pallas_call | solution.py:338
  20.2 0.1 collective-permute-start.6
  20.2 1.2 %shard_map.116 = (bf16[3,112,128]{2,1,0:T(8,128)(2,1)S(1)}, bf16[3,112,128]{2,1,0:T(8,128)(2,1)S(1)}) custom-call(s32[3]{0:T(128)S(1)} %pad_add_fusion.info_ref, bf16[112,1536]{1,0:T(8,128)(2,1)S(1)} %get-tuple-element.38.normed_ref, bf16[1536,3072]{1,0:T(8,128)(2,1)S(1)} %get-tuple-element.39.weight_ref, f32[112,128]{1,0:T(8,128)S(1)} %get-tuple-element.65.cos_ref, ...), custom_call_target="tpu_custom_call" | custom-call | tf_op jit(solution)/shard_map/pallas_call | solution.py:338
  21.4 0.0 copy-start
  21.4 0.0 copy-start.1
  21.5 0.0 copy-start.2
  21.5 1.2 %shard_map.115 = (bf16[3,112,128]{2,1,0:T(8,128)(2,1)S(1)}, bf16[3,112,128]{2,1,0:T(8,128)(2,1)S(1)}) custom-call(s32[3]{0:T(128)S(1)} %pad_add_fusion.info_ref, bf16[112,1536]{1,0:T(8,128)(2,1)S(1)} %get-tuple-element.38.normed_ref, bf16[1536,3072]{1,0:T(8,128)(2,1)S(1)} %get-tuple-element.39.weight_ref, f32[112,128]{1,0:T(8,128)S(1)} %get-tuple-element.65.cos_ref, ...), custom_call_target="tpu_custom_call" | custom-call | tf_op jit(solution)/shard_map/pallas_call | solution.py:338
  22.7 2.9 %collective-permute-start.7 = (bf16[3,112,128]{2,1,0:T(8,128)(2,1)S(1)}, bf16[3,112,128]{2,1,0:T(8,128)(2,1)S(1)}, u32[]{:S(2)}, u32[]{:S(2)}) collective-permute-start(bf16[3,112,128]{2,1,0:T(8,128)(2,1)S(1)} %get-tuple-element.45), channel_id=1, source_target_pairs={{0,10},{1,11},{2,8},{3,9},{4,14},{5,15},{6,12},{7,13},{8,2},{9,3},... | collective-permute-start | bytes 258056 | tf_op jit(solution)/shard_map/ppermute | solution.py:378
  25.5 0.7 %collective-permute-start.4 = (bf16[3,112,128]{2,1,0:T(8,128)(2,1)S(1)}, bf16[3,112,128]{2,1,0:T(8,128)(2,1)S(1)}, u32[]{:S(2)}, u32[]{:S(2)}) collective-permute-start(bf16[3,112,128]{2,1,0:T(8,128)(2,1)S(1)} %get-tuple-element.42), channel_id=1, source_target_pairs={{0,4},{1,5},{2,6},{3,7},{4,0},{5,1},{6,2},{7,3},{8,12},{9,13},{10,... | collective-permute-start | bytes 258056 | tf_op jit(solution)/shard_map/ppermute | solution.py:378
  26.2 2.4 %collective-permute-start.5 = (bf16[3,112,128]{2,1,0:T(8,128)(2,1)S(1)}, bf16[3,112,128]{2,1,0:T(8,128)(2,1)S(1)}, u32[]{:S(2)}, u32[]{:S(2)}) collective-permute-start(bf16[3,112,128]{2,1,0:T(8,128)(2,1)S(1)} %get-tuple-element.43), channel_id=1, source_target_pairs={{0,6},{1,7},{2,4},{3,5},{4,2},{5,3},{6,0},{7,1},{8,14},{9,15},{10,... | collective-permute-start | bytes 258056 | tf_op jit(solution)/shard_map/ppermute | solution.py:378
  28.6 0.0 collective-permute-done.8.refs_6_.refs_3_
  28.6 0.5 collective-permute-start.3
  29.0 0.0 collective-permute-done.6.refs_4_.refs_2_
  29.0 1.9 %collective-permute-start.9 = (bf16[3,112,128]{2,1,0:T(8,128)(2,1)S(1)}, bf16[3,112,128]{2,1,0:T(8,128)(2,1)S(1)}, u32[]{:S(2)}, u32[]{:S(2)}) collective-permute-start(bf16[3,112,128]{2,1,0:T(8,128)(2,1)S(1)} %get-tuple-element.53), channel_id=1, source_target_pairs={{0,14},{1,15},{2,12},{3,13},{4,10},{5,11},{6,8},{7,9},{8,6},{9,7},... | collective-permute-start | bytes 258056 | tf_op jit(solution)/shard_map/ppermute | solution.py:378
  30.9 0.8 %collective-permute-done.7.refs_5_ = bf16[3,112,128]{2,1,0:T(8,128)(2,1)S(1)} collective-permute-done((bf16[3,112,128]{2,1,0:T(8,128)(2,1)S(1)}, bf16[3,112,128]{2,1,0:T(8,128)(2,1)S(1)}, u32[]{:S(2)}, u32[]{:S(2)}) %collective-permute-start.7) | collective-permute-done | bytes 86048 | tf_op jit(solution)/shard_map/ppermute | solution.py:378
  31.7 0.0 collective-permute-done.4.refs_2_.refs_1_
  31.7 4.7 %collective-permute-done.5.refs_3_ = bf16[3,112,128]{2,1,0:T(8,128)(2,1)S(1)} collective-permute-done((bf16[3,112,128]{2,1,0:T(8,128)(2,1)S(1)}, bf16[3,112,128]{2,1,0:T(8,128)(2,1)S(1)}, u32[]{:S(2)}, u32[]{:S(2)}) %collective-permute-start.5) | collective-permute-done | bytes 86048 | tf_op jit(solution)/shard_map/ppermute | solution.py:378
  36.4 0.7 %collective-permute-done.3.refs_1_ = bf16[3,112,128]{2,1,0:T(8,128)(2,1)S(1)} collective-permute-done((bf16[3,112,128]{2,1,0:T(8,128)(2,1)S(1)}, bf16[3,112,128]{2,1,0:T(8,128)(2,1)S(1)}, u32[]{:S(2)}, u32[]{:S(2)}) %collective-permute-start.3) | collective-permute-done | bytes 86048 | tf_op jit(solution)/shard_map/ppermute | solution.py:378
  37.1 2.2 %shard_map.119 = (bf16[784,256]{1,0:T(8,128)(2,1)S(1)}, bf16[784,128]{1,0:T(8,128)(2,1)S(1)}, bf16[672,256]{1,0:T(8,128)(2,1)S(1)}, f32[672,128]{1,0:T(8,128)S(1...) custom-call(s32[3]{0:T(128)S(1)} %pad_add_fusion.info_ref, bf16[3,112,128]{2,1,0:T(8,128)(2,1)S(1)} %get-tuple-element.40.refs_0_, ...), custom_call_target="tpu_custom_call" | custom-call | tf_op jit(solution)/shard_map/pallas_call | solution.py:338
  39.3 0.0 collective-permute-done.9.last_ref
  39.3 1.5 %shard_map.120 = (bf16[4,112,128]{2,1,0:T(8,128)(2,1)S(1)}, bf16[896,256]{1,0:T(8,128)(2,1)S(1)}, bf16[896,128]{1,0:T(8,128)(2,1)S(1)}) custom-call(s32[3]{0:T(128)S(1)} %pad_add_fusion.info_ref, bf16[784,256]{1,0:T(8,128)(2,1)S(1)} %get-tuple-element.47.early_keys, bf16[784,128]{1,0:T(8,128)(2,1)S(1)} %get-tuple-element.48.early_values, ...), custom_call_target="tpu_custom_call" | custom-call | tf_op jit(solution)/shard_map/pallas_call | solution.py:338
  40.9 0.1 collective-permute-start.10
  41.0 2.3 %shard_map.121.own_ref.refs_0_ = bf16[4,112,128]{2,1,0:T(8,128)(2,1)S(1)} custom-call(s32[3]{0:T(128)S(1)} %pad_add_fusion.info_ref, bf16[896,256]{1,0:T(8,128)(2,1)S(1)} %get-tuple-element.54.keys, bf16[896,128]{1,0:T(8,128)(2,1)S(1)} %get-tuple-element.55.values, bf16[3,112,128]{2,1,0:T(8,128)(2,1)S(1)} %get-tuple-element.40.refs_0_, ...), custom_call_target="tpu_custom_call" | custom-call | tf_op jit(solution)/shard_map/pallas_call | solution.py:338
  43.2 2.5 %collective-permute-done.10.got_ref.refs_1_ = bf16[4,112,128]{2,1,0:T(8,128)(2,1)S(1)} collective-permute-done((bf16[4,112,128]{2,1,0:T(8,128)(2,1)S(1)}, bf16[4,112,128]{2,1,0:T(8,128)(2,1)S(1)}, u32[]{:S(2)}, u32[]{:S(2)}) %collective-permute-start.10) | collective-permute-done | bytes 114720 | tf_op jit(solution)/shard_map/ppermute | solution.py:378
  45.7 0.6 shard_map.122
  46.3 0.1 collective-permute-start.11
  46.4 0.6 %collective-permute-start.12 = (bf16[2,112,128]{2,1,0:T(8,128)(2,1)S(1)}, bf16[2,112,128]{2,1,0:T(8,128)(2,1)S(1)}, u32[]{:S(2)}, u32[]{:S(2)}) collective-permute-start(bf16[2,112,128]{2,1,0:T(8,128)(2,1)S(1)} %get-tuple-element.58), channel_id=1, source_target_pairs={{0,8},{1,9},{2,10},{3,11},{4,12},{5,13},{6,14},{7,15},{8,0},{9,1},... | collective-permute-start | bytes 172040 | tf_op jit(solution)/shard_map/ppermute | solution.py:378
  47.0 3.8 %collective-permute-start.13 = (bf16[2,112,128]{2,1,0:T(8,128)(2,1)S(1)}, bf16[2,112,128]{2,1,0:T(8,128)(2,1)S(1)}, u32[]{:S(2)}, u32[]{:S(2)}) collective-permute-start(bf16[2,112,128]{2,1,0:T(8,128)(2,1)S(1)} %get-tuple-element.59), channel_id=1, source_target_pairs={{0,12},{1,13},{2,14},{3,15},{4,8},{5,9},{6,10},{7,11},{8,4},{9,5},... | collective-permute-start | bytes 172040 | tf_op jit(solution)/shard_map/ppermute | solution.py:378
  50.7 0.0 collective-permute-done.11.refs_2_
  50.7 1.2 %collective-permute-done.12.refs_3_ = bf16[2,112,128]{2,1,0:T(8,128)(2,1)S(1)} collective-permute-done((bf16[2,112,128]{2,1,0:T(8,128)(2,1)S(1)}, bf16[2,112,128]{2,1,0:T(8,128)(2,1)S(1)}, u32[]{:S(2)}, u32[]{:S(2)}) %collective-permute-start.12) | collective-permute-done | bytes 57376 | tf_op jit(solution)/shard_map/ppermute | solution.py:378
  52.0 1.6 %collective-permute-done.13.refs_4_ = bf16[2,112,128]{2,1,0:T(8,128)(2,1)S(1)} collective-permute-done((bf16[2,112,128]{2,1,0:T(8,128)(2,1)S(1)}, bf16[2,112,128]{2,1,0:T(8,128)(2,1)S(1)}, u32[]{:S(2)}, u32[]{:S(2)}) %collective-permute-start.13) | collective-permute-done | bytes 57376 | tf_op jit(solution)/shard_map/ppermute | solution.py:378
  53.6 2.0 %shard_map.123 = (f32[56,100]{1,0:T(8,128)S(1)}, f32[56,100]{1,0:T(8,128)S(1)}) custom-call(s32[3]{0:T(128)S(1)} %pad_add_fusion.info_ref, f32[112,1536]{1,0:T(8,128)S(1)} %get-tuple-element.37.residual, bf16[100,1536]{1,0:T(8,128)(2,1)S(1)} %bitcast.8, f32[5,1536]{1,0:T(8,128)S(1)} %get-tuple-element.36.mod_ref, bf16[1024,1536]{1,0:T(8,128)(2,1)S(1)} %copy-done, ...), custom_call_target="tpu_custom_call" | custom-call | tf_op jit(solution)/shard_map/pallas_call | solution.py:338
  55.7 0.1 collective-permute-start.14
  57.1 0.6 %multiply_add_fusion = (f32[56,100]{1,0:T(8,128)}, f32[56,100]{1,0:T(8,128)}) fusion(f32[56,100]{1,0:T(8,128)S(1)} %copy-done.2, f32[]{:T(128)} %bitcast.5, f32[56,100]{1,0:T(8,128)S(1)} %collective-permute-done.14, f32[56,100]{1,0:T(8,128)S(1)} %get-tuple-element.60, f32[]{:T(128)} %bitcast.7, f32[56,100]{1,0:T(8,128)S(1)} %get-tuple-element.33, ...), kind=kLoop, calls=%fused_computation.4 | loop fusion | flops 56000 | bytes 156808 | tf_op jit(solution)/shard_map/add | solution.py:583
  (6 shorter events, 0.0 us)
Async XLA Ops:
  1.5 5.6 %collective-permute-start.1 = (bf16[2,16,1536]{2,1,0:T(8,128)(2,1)S(1)}, bf16[2,16,1536]{2,1,0:T(8,128)(2,1)S(1)}, u32[]{:S(2)}, u32[]{:S(2)}) collective-permute-start(bf16[2,16,1536]{2,1,0:T(8,128)(2,1)S(1)} %constant_dynamic-slice_fusion), channel_id=1, source_target_pairs={{1,2},{2,1},{3,4},{4,3},{5,6},{6,5},{7,8},{8,7},{9,10},{10,9},{11,... | collective-permute-start | bytes 294920 | tf_op jit(solution)/shard_map/ppermute | solution.py:532
  5.4 3.4 %collective-permute-start = (bf16[56,1536]{1,0:T(8,128)(2,1)S(1)}, bf16[56,1536]{1,0:T(8,128)(2,1)S(1)}, u32[]{:S(2)}, u32[]{:S(2)}) collective-permute-start(bf16[56,1536]{1,0:T(8,128)(2,1)S(1)} %dynamic-slice_bitcast_fusion), channel_id=1, source_target_pairs={{0,1},{1,0},{2,3},{3,2},{4,5},{5,4},{6,7},{7,6},{8,9},{9,8},{10,11... | collective-permute-start | bytes 516104 | tf_op jit(solution)/shard_map/ppermute | solution.py:378
  7.1 1.8 %collective-permute-start.2 = (bf16[2,16,1536]{2,1,0:T(8,128)(2,1)S(1)}, bf16[2,16,1536]{2,1,0:T(8,128)(2,1)S(1)}, u32[]{:S(2)}, u32[]{:S(2)}) collective-permute-start(bf16[2,16,1536]{2,1,0:T(8,128)(2,1)S(1)} %collective-permute-done.1.near_ref), channel_id=1, source_target_pairs={{0,1},{1,0},{2,3},{3,2},{4,5},{5,4},{6,7},{7,6},{8,9},{9,8},{10,11... | collective-permute-start | bytes 294920 | tf_op jit(solution)/shard_map/ppermute | solution.py:378
  14.4 14.1 %collective-permute-start.8 = (bf16[3,112,128]{2,1,0:T(8,128)(2,1)S(1)}, bf16[3,112,128]{2,1,0:T(8,128)(2,1)S(1)}, u32[]{:S(2)}, u32[]{:S(2)}) collective-permute-start(bf16[3,112,128]{2,1,0:T(8,128)(2,1)S(1)} %get-tuple-element.46), channel_id=1, source_target_pairs={{0,12},{1,13},{2,14},{3,15},{4,8},{5,9},{6,10},{7,11},{8,4},{9,5},... | collective-permute-start | bytes 258056 | tf_op jit(solution)/shard_map/ppermute | solution.py:378
  20.2 8.9 %collective-permute-start.6 = (bf16[3,112,128]{2,1,0:T(8,128)(2,1)S(1)}, bf16[3,112,128]{2,1,0:T(8,128)(2,1)S(1)}, u32[]{:S(2)}, u32[]{:S(2)}) collective-permute-start(bf16[3,112,128]{2,1,0:T(8,128)(2,1)S(1)} %get-tuple-element.44), channel_id=1, source_target_pairs={{0,8},{1,9},{2,10},{3,11},{4,12},{5,13},{6,14},{7,15},{8,0},{9,1},... | collective-permute-start | bytes 258056 | tf_op jit(solution)/shard_map/ppermute | solution.py:378
  21.4 32.2 %copy-start = (bf16[1024,1536]{1,0:T(8,128)(2,1)S(1)}, bf16[1024,1536]{1,0:T(8,128)(2,1)}, u32[]{:S(2)}) copy-start(bf16[1024,1536]{1,0:T(8,128)(2,1)} %w_out_ref.1) | copy-start | bytes 9437188
  21.4 32.2 %copy-start.1 = (bf16[1536,100]{0,1:T(8,128)(2,1)S(1)}, bf16[1536,100]{0,1:T(8,128)(2,1)}, u32[]{:S(2)}) copy-start(bf16[1536,100]{0,1:T(8,128)(2,1)} %param.19) | copy-start | bytes 921604
  21.5 35.7 %copy-start.2 = (f32[56,100]{1,0:T(8,128)S(1)}, f32[56,100]{1,0:T(8,128)}, u32[]{:S(2)}) copy-start(f32[56,100]{1,0:T(8,128)} %param.11) | copy-start | bytes 67204
  22.7 9.0 %collective-permute-start.7 = (bf16[3,112,128]{2,1,0:T(8,128)(2,1)S(1)}, bf16[3,112,128]{2,1,0:T(8,128)(2,1)S(1)}, u32[]{:S(2)}, u32[]{:S(2)}) collective-permute-start(bf16[3,112,128]{2,1,0:T(8,128)(2,1)S(1)} %get-tuple-element.45), channel_id=1, source_target_pairs={{0,10},{1,11},{2,8},{3,9},{4,14},{5,15},{6,12},{7,13},{8,2},{9,3},... | collective-permute-start | bytes 258056 | tf_op jit(solution)/shard_map/ppermute | solution.py:378
  25.5 6.2 %collective-permute-start.4 = (bf16[3,112,128]{2,1,0:T(8,128)(2,1)S(1)}, bf16[3,112,128]{2,1,0:T(8,128)(2,1)S(1)}, u32[]{:S(2)}, u32[]{:S(2)}) collective-permute-start(bf16[3,112,128]{2,1,0:T(8,128)(2,1)S(1)} %get-tuple-element.42), channel_id=1, source_target_pairs={{0,4},{1,5},{2,6},{3,7},{4,0},{5,1},{6,2},{7,3},{8,12},{9,13},{10,... | collective-permute-start | bytes 258056 | tf_op jit(solution)/shard_map/ppermute | solution.py:378
  26.2 10.3 %collective-permute-start.5 = (bf16[3,112,128]{2,1,0:T(8,128)(2,1)S(1)}, bf16[3,112,128]{2,1,0:T(8,128)(2,1)S(1)}, u32[]{:S(2)}, u32[]{:S(2)}) collective-permute-start(bf16[3,112,128]{2,1,0:T(8,128)(2,1)S(1)} %get-tuple-element.43), channel_id=1, source_target_pairs={{0,6},{1,7},{2,4},{3,5},{4,2},{5,3},{6,0},{7,1},{8,14},{9,15},{10,... | collective-permute-start | bytes 258056 | tf_op jit(solution)/shard_map/ppermute | solution.py:378
  28.6 8.6 %collective-permute-start.3 = (bf16[3,112,128]{2,1,0:T(8,128)(2,1)S(1)}, bf16[3,112,128]{2,1,0:T(8,128)(2,1)S(1)}, u32[]{:S(2)}, u32[]{:S(2)}) collective-permute-start(bf16[3,112,128]{2,1,0:T(8,128)(2,1)S(1)} %get-tuple-element.41), channel_id=1, source_target_pairs={{0,2},{1,3},{2,0},{3,1},{4,6},{5,7},{6,4},{7,5},{8,10},{9,11},{10,... | collective-permute-start | bytes 258056 | tf_op jit(solution)/shard_map/ppermute | solution.py:378
  29.0 10.3 %collective-permute-start.9 = (bf16[3,112,128]{2,1,0:T(8,128)(2,1)S(1)}, bf16[3,112,128]{2,1,0:T(8,128)(2,1)S(1)}, u32[]{:S(2)}, u32[]{:S(2)}) collective-permute-start(bf16[3,112,128]{2,1,0:T(8,128)(2,1)S(1)} %get-tuple-element.53), channel_id=1, source_target_pairs={{0,14},{1,15},{2,12},{3,13},{4,10},{5,11},{6,8},{7,9},{8,6},{9,7},... | collective-permute-start | bytes 258056 | tf_op jit(solution)/shard_map/ppermute | solution.py:378
  40.9 4.9 %collective-permute-start.10 = (bf16[4,112,128]{2,1,0:T(8,128)(2,1)S(1)}, bf16[4,112,128]{2,1,0:T(8,128)(2,1)S(1)}, u32[]{:S(2)}, u32[]{:S(2)}) collective-permute-start(bf16[4,112,128]{2,1,0:T(8,128)(2,1)S(1)} %get-tuple-element.56), channel_id=1, source_target_pairs={{0,2},{1,3},{2,0},{3,1},{4,6},{5,7},{6,4},{7,5},{8,10},{9,11},{10,... | collective-permute-start | bytes 344072 | tf_op jit(solution)/shard_map/ppermute | solution.py:378
  46.3 4.5 %collective-permute-start.11 = (bf16[2,112,128]{2,1,0:T(8,128)(2,1)S(1)}, bf16[2,112,128]{2,1,0:T(8,128)(2,1)S(1)}, u32[]{:S(2)}, u32[]{:S(2)}) collective-permute-start(bf16[2,112,128]{2,1,0:T(8,128)(2,1)S(1)} %get-tuple-element.57), channel_id=1, source_target_pairs={{0,4},{1,5},{2,6},{3,7},{4,0},{5,1},{6,2},{7,3},{8,12},{9,13},{10,... | collective-permute-start | bytes 172040 | tf_op jit(solution)/shard_map/ppermute | solution.py:378
  46.4 5.6 %collective-permute-start.12 = (bf16[2,112,128]{2,1,0:T(8,128)(2,1)S(1)}, bf16[2,112,128]{2,1,0:T(8,128)(2,1)S(1)}, u32[]{:S(2)}, u32[]{:S(2)}) collective-permute-start(bf16[2,112,128]{2,1,0:T(8,128)(2,1)S(1)} %get-tuple-element.58), channel_id=1, source_target_pairs={{0,8},{1,9},{2,10},{3,11},{4,12},{5,13},{6,14},{7,15},{8,0},{9,1},... | collective-permute-start | bytes 172040 | tf_op jit(solution)/shard_map/ppermute | solution.py:378
  47.0 6.7 %collective-permute-start.13 = (bf16[2,112,128]{2,1,0:T(8,128)(2,1)S(1)}, bf16[2,112,128]{2,1,0:T(8,128)(2,1)S(1)}, u32[]{:S(2)}, u32[]{:S(2)}) collective-permute-start(bf16[2,112,128]{2,1,0:T(8,128)(2,1)S(1)} %get-tuple-element.59), channel_id=1, source_target_pairs={{0,12},{1,13},{2,14},{3,15},{4,8},{5,9},{6,10},{7,11},{8,4},{9,5},... | collective-permute-start | bytes 172040 | tf_op jit(solution)/shard_map/ppermute | solution.py:378
  55.7 1.5 %collective-permute-start.14 = (f32[56,100]{1,0:T(8,128)S(1)}, f32[56,100]{1,0:T(8,128)S(1)}, u32[]{:S(2)}, u32[]{:S(2)}) collective-permute-start(f32[56,100]{1,0:T(8,128)S(1)} %get-tuple-element.61), channel_id=1, source_target_pairs={{0,1},{1,0},{2,3},{3,2},{4,5},{5,4},{6,7},{7,6},{8,9},{9,8},{10,11... | collective-permute-start | bytes 67208 | tf_op jit(solution)/shard_map/ppermute | solution.py:378

commit v2 on v1

--- a/solution.py
+++ b/solution.py
@@ -32,13 +32,12 @@
     return pl.BlockSpec(memory_space=SMEM)
 
 
-def rotary_tables(positions):
+def rotary_rates():
     half_dim = HEAD_DIM // 2
     lane = jnp.arange(LANES, dtype=jnp.int32)
     inverse = 10000.0 ** (-(lane % half_dim).astype(jnp.float32) / half_dim)
-    angles = positions.astype(jnp.float32)[:, None] * inverse[None, :]
     sign = jnp.where(lane % HEAD_DIM < half_dim, -1.0, 1.0)
-    return jnp.cos(angles), jnp.sin(angles) * sign[None, :]
+    return jnp.stack([inverse, sign])
 
 
 def hbm_spec():
@@ -80,6 +79,22 @@
         copy.start()
     for copy in copies:
         copy.wait()
+
+
+def start_loads(source, first, target, sems):
+    parts = sems.shape[0]
+    depth = target.shape[0] // parts
+    loads = [
+        pltpu.make_async_copy(
+            source.at[pl.ds(first + part * depth, depth)],
+            target.at[pl.ds(part * depth, depth)],
+            sems.at[part],
+        )
+        for part in range(parts)
+    ]
+    for load in loads:
+        load.start()
+    return loads
 
 
 def stage_kernel(
@@ -96,6 +111,17 @@
     )
 
 
+def load_kernel(info_ref, rates_ref, weight_hbm, weight_ref, cos_ref, sin_ref, sems):
+    rows = cos_ref.shape[0]
+    loads = start_loads(weight_hbm, 0, weight_ref, sems)
+    frame = info_ref[CHIP] * rows + lax.broadcasted_iota(jnp.int32, (rows, LANES), 0)
+    angles = frame.astype(jnp.float32) * rates_ref[0:1, :]
+    cos_ref[...] = jnp.cos(angles)
+    sin_ref[...] = jnp.sin(angles) * rates_ref[1:2, :]
+    for load in loads:
+        load.wait()
+
+
 def front_kernel(
     info_ref, own_ref, partner_ref, near_ref, far_ref, taps_ref, mod_ref, weight_hbm,
     residual_ref, normed_ref, weight_ref, padded, sems,
@@ -104,16 +130,7 @@
     halo = near_ref.shape[1]
     total_rows = 2 * rows
     tiles = width // LANES
-    parts = 8
-    depth = width // parts
-    loads = []
-    for part in range(parts):
-        here = pl.ds(part * depth, depth)
-        loads.append(
-            pltpu.make_async_copy(weight_hbm.at[here], weight_ref.at[here], sems.at[part])
-        )
-    for load in loads:
-        load.start()
+    loads = start_loads(weight_hbm, width - weight_ref.shape[0], weight_ref, sems)
     length, core = info_ref[LENGTH], info_ref[CORE]
     offset = info_ref[CHIP] * total_rows
     span = total_rows + 2 * halo
@@ -156,9 +173,12 @@
         load.wait()
 
 
-def project_kernel(firsts, origin, info_ref, normed_ref, weight_ref, cos_ref, sin_ref, *out_refs):
+def project_kernel(
+    firsts, origin, info_ref, normed_ref, top_ref, rest_ref, cos_ref, sin_ref, *out_refs
+):
     rows = normed_ref.shape[0]
-    attn = weight_ref.shape[1] // 3
+    attn = rest_ref.shape[1] // 3
+    top = top_ref.shape[0]
     wide = 2 * LANES
     half = HEAD_DIM // 2
     cosine, sine = cos_ref[...], sin_ref[...]
@@ -169,10 +189,11 @@
         pair = (chip ^ apart) >> 1
         for part in range(3):
             start = part * attn + pair * wide
+            lanes = pl.ds(pl.multiple_of(start, wide), wide)
             both = jnp.dot(
-                normed_ref[...],
-                weight_ref[:, pl.ds(pl.multiple_of(start, wide), wide)],
-                preferred_element_type=jnp.float32,
+                normed_ref[:, :top], top_ref[:, lanes], preferred_element_type=jnp.float32
+            ) + jnp.dot(
+                normed_ref[:, top:], rest_ref[:, lanes], preferred_element_type=jnp.float32
             )
             sides = []
             for side in range(2):
@@ -225,17 +246,17 @@
     return jnp.dot(weights.astype(jnp.bfloat16), values, preferred_element_type=jnp.float32)
 
 
-def store_heads(mixed, out_ref, first):
+def store_heads(mixed, out_ref, places):
     _, rows, _ = out_ref.shape
     low = lax.broadcasted_iota(jnp.int32, (rows, LANES), 1) < HEAD_DIM
     for at in range(mixed.shape[0] // (2 * rows)):
         base = 2 * at * rows
-        out_ref[first + at] = jnp.where(
+        out_ref[places[at]] = jnp.where(
             low, mixed[base : base + rows], mixed[base + rows : base + 2 * rows]
         ).astype(jnp.bfloat16)
 
 
-def attend_rows(keys, values, queries, out_ref, first):
+def attend_rows(keys, values, queries, out_ref, places):
     _, rows, _ = out_ref.shape
     total = queries.shape[0]
     for base in range(0, total, 4 * rows):
@@ -243,17 +264,17 @@
         scores = score(queries[block, :], keys[...])
         weights = jnp.exp(scores - jnp.max(scores, axis=1, keepdims=True))
         weight_sum = jnp.sum(weights, axis=1, keepdims=True)
-        store_heads(mix(weights, values[...]) / weight_sum, out_ref, first + base // (2 * rows))
-
-
-def attend_early_kernel(info_ref, *refs):
-    chips = len(refs) - 6
-    got_refs = refs[:chips]
-    keys, values, queries, mixed_ref, peak_ref, sum_ref = refs[chips:]
+        mixed = mix(weights, values[...]) / weight_sum
+        store_heads(mixed, out_ref, places[base // (2 * rows) :])
+
+
+def attend_early_kernel(aparts, info_ref, *refs):
+    got_refs = refs[: len(aparts)]
+    keys, values, queries, mixed_ref, peak_ref, sum_ref = refs[len(aparts) :]
     _, rows, _ = got_refs[0].shape
-    for apart, got_ref in enumerate(got_refs):
-        place_keys(info_ref, apart, got_ref, keys, values, apart * rows)
-    place_queries(got_refs[1::2], queries)
+    for at, apart in enumerate(aparts):
+        place_keys(info_ref, apart, got_refs[at], keys, values, at * rows)
+    place_queries([ref for apart, ref in zip(aparts, got_refs) if apart % 2], queries)
     scores = score(queries[...], keys[...])
     peak = jnp.max(scores, axis=1, keepdims=True)
     weights = jnp.exp(scores - peak)
@@ -263,31 +284,35 @@
 
 
 def attend_last_kernel(
-    info_ref, early_keys, early_values, early_queries, mixed_ref, peak_ref, sum_ref, last_ref,
-    out_ref, keys, values, queries,
+    aparts, places, info_ref, early_keys, early_values, early_queries, mixed_ref, peak_ref, sum_ref,
+    *refs,
 ):
+    got_refs = refs[: len(aparts)]
+    out_ref, keys, values, queries = refs[len(aparts) :]
+    early_places, last_places = places
     held, _ = early_values.shape
-    _, rows, _ = last_ref.shape
+    _, rows, _ = got_refs[0].shape
     keys[:held, :] = early_keys[...]
     values[:held, :] = early_values[...]
-    place_keys(info_ref, held // rows, last_ref, keys, values, held)
-    place_queries([last_ref], queries)
-    attend_rows(keys, values, queries, out_ref, out_ref.shape[0] - 1)
+    for at, apart in enumerate(aparts):
+        place_keys(info_ref, apart, got_refs[at], keys, values, held + at * rows)
+    place_queries([ref for apart, ref in zip(aparts, got_refs) if apart % 2], queries)
+    attend_rows(keys, values, queries, out_ref, last_places)
     scores = score(early_queries[...], keys[held:, :])
-    peak = peak_ref[...]
+    peak = peak_ref[:, :1]
     joined = jnp.maximum(peak, jnp.max(scores, axis=1, keepdims=True))
     scale = jnp.exp(peak - joined)
-    weights = jnp.exp(scores - joined[:, : scores.shape[1]])
-    weight_sum = sum_ref[...] * scale + jnp.sum(weights, axis=1, keepdims=True)
+    weights = jnp.exp(scores - joined)
+    weight_sum = sum_ref[:, :1] * scale + jnp.sum(weights, axis=1, keepdims=True)
     mixed = mixed_ref[...] * scale + mix(weights, values[held:, :])
-    store_heads(mixed / weight_sum, out_ref, 0)
+    store_heads(mixed / weight_sum, out_ref, early_places)
 
 
 def attend_second_kernel(info_ref, keys, values, *refs):
     del info_ref
     out_ref, queries = refs[-2:]
     place_queries(refs[:-2], queries)
-    attend_rows(keys, values, queries, out_ref, 0)
+    attend_rows(keys, values, queries, out_ref, list(range(out_ref.shape[0])))
 
 
 def merge_kernel(info_ref, own_ref, got_ref, *out_refs):
@@ -354,7 +379,7 @@
     return call(
         functools.partial(project_kernel, tuple(firsts), origin),
         (shape,) * (2 * len(firsts)),
-        (info, normed, w_qkv) + tables,
+        (info, normed) + w_qkv + tables,
         [],
     )
 
@@ -460,7 +485,11 @@
 
 def send_order(chips):
     far = list(range(chips // 2, chips, 2))
-    return far[:1] + list(range(2, chips // 2, 2)) + far[1:] + [0]
+    return far[:1] + [0] + far[1:] + list(range(2, chips // 2, 2))
+
+
+def late_sends(chips):
+    return list(range(2, chips // 2)) + [chips - 1]
 
 
 def attend_chips(normed, w_qkv, tables, info, count):
@@ -473,27 +502,32 @@
             apart = first + side
             held[apart] = across(made[side], 2 * apart, count) if apart else made[side]
     total, half = chips * rows, chips // 2
-    early, early_rows = total - rows, 2 * (half - 1) * rows
+    late = late_sends(chips)
+    soon = [apart for apart in range(chips) if apart not in late]
+    odd_soon = [apart for apart in soon if apart % 2]
+    odd_late = [apart for apart in late if apart % 2]
+    early, early_rows = len(soon) * rows, 2 * len(odd_soon) * rows
     parts = call(
-        attend_early_kernel,
+        functools.partial(attend_early_kernel, tuple(soon)),
         (
             array((early, 2 * LANES), jnp.bfloat16),
             array((early, LANES), jnp.bfloat16),
             array((early_rows, 2 * LANES), jnp.bfloat16),
         )
         + (array((early_rows, LANES)),) * 3,
-        (info,) + tuple(held[apart] for apart in range(chips - 1)),
+        (info,) + tuple(held[apart] for apart in soon),
         [],
     )
+    places = tuple(tuple(apart // 2 for apart in odds) for odds in (odd_soon, odd_late))
     crossing, keys, values = call(
-        attend_last_kernel,
+        functools.partial(attend_last_kernel, tuple(late), places),
         (
             array((half, rows, LANES), jnp.bfloat16),
             array((total, 2 * LANES), jnp.bfloat16),
             array((total, LANES), jnp.bfloat16),
         ),
-        (info,) + tuple(parts) + (held[chips - 1],),
-        [VMEM((2 * rows, 2 * LANES), jnp.bfloat16)],
+        (info,) + tuple(parts) + tuple(held[apart] for apart in late),
+        [VMEM((2 * len(odd_late) * rows, 2 * LANES), jnp.bfloat16)],
     )
     crossed = across(crossing, 2, count)
     staying = call(
@@ -545,18 +579,31 @@
         [pltpu.SemaphoreType.DMA((3,))],
         hbm=(1, 2, 3),
     )
-    tables = rotary_tables(chip * chip_rows + jnp.arange(chip_rows, dtype=jnp.int32))
+    top = min(2 * LANES, width // 2)
+    weight_top, *tables = call(
+        load_kernel,
+        (
+            array((top, w_qkv.shape[1]), jnp.bfloat16),
+            array((chip_rows, LANES)),
+            array((chip_rows, LANES)),
+        ),
+        (info, rotary_rates(), w_qkv),
+        [pltpu.SemaphoreType.DMA((2,))],
+        hbm=(2,),
+    )
+    tables = tuple(tables)
     residual, normed, weight = call(
         front_kernel,
         (
             array((chip_rows, width)),
             array((chip_rows, width), jnp.bfloat16),
-            array(w_qkv.shape, jnp.bfloat16),
+            array((width - top, w_qkv.shape[1]), jnp.bfloat16),
         ),
         (info, own, partner, near, far, taps, mods, w_qkv),
         [VMEM((chip_rows + 2 * HALO, LANES), jnp.float32), pltpu.SemaphoreType.DMA((8,))],
         hbm=(7,),
     )
+    weight = (weight_top, weight)
     if chips_hold_groups(count):
         back, blocks = attend_chips(normed, weight, tables, info, count)
     else:

time: 58 us -> 57 us (0.983)
  waiting for transfers between devices: 12.1 us -> 9.61 us
  Pallas kernels: 19.3 us -> 21.1 us
    ppermute x14, waiting for transfers between devices: 11.6 us -> 9.6 us  [across(): return lax.ppermute(value, 'seq', [(i, i ^ apart) for i in range(count)])]
    pallas_call x11 -> x12, Pallas kernels: 19.3 us -> 21.1 us  [call(): pl.pallas_call(kernel, out_shape=out_shape, in_specs=[smem_spec()] + spec...]
  transfers between devices with their start and end apart: 15 -> 15, of which waited for: 7 -> 7; matrix products, arithmetic and copies ran while one was open for 2% -> 2% of each run, Pallas kernels for 17% -> 19%
where the time goes in v2:
time: 57 us; the launch traced here: 56.8 us
  Pallas kernels  21.1 us (37%)
  starting transfers between devices  20.6 us (36%)
  waiting for transfers between devices  9.61 us (17%)
  between operations  2.85 us (5%)
  local copies, waits for them, and re-layouts  1.86 us (3%)
  other arithmetic  0.73 us (1%)
    pallas_call x12, Pallas kernels, call(): pl.pallas_call(kernel, out_shape=out_shape, in_specs=[smem_spec()] + spec...  21.1 us
    ppermute x14, starting transfers between devices, across(): return lax.ppermute(value, 'seq', [(i, i ^ apart) for i in range(count)])  17.7 us
    ppermute x14, waiting for transfers between devices, across(): return lax.ppermute(value, 'seq', [(i, i ^ apart) for i in range(count)])  9.6 us
    ppermute x1, starting transfers between devices, per_device(): lax.ppermute(edges, ('clip', 'seq'), facing_pairs(lax.axis_size('clip'),...  2.97 us
  transfers between devices with their start and end apart: 15, of which 7 were waited for; matrix products, arithmetic and copies ran while one was open for 2% of the time, Pallas kernels for 19%

profile of v2, /device:TPU:0, one launch (start us, length us, event | category | flops | bytes accessed | tf_op | source)
XLA Modules:
  0.0 56.8 jit_solution(1275357436121518333)
XLA Ops:
  0.6 0.9 %constant_dynamic-slice_fusion = bf16[2,16,1536]{2,1,0:T(8,128)(2,1)S(1)} fusion(bf16[2,56,1536]{2,1,0:T(8,128)(2,1)} %hidden_hbm.1, s32[]{:T(128)S(6)} %select_n.54), kind=kLoop, calls=%fused_computation.12 | loop fusion | bytes 196612 | tf_op jit(solution)/shard_map/dynamic_slice | solution.py:564
  1.5 3.0 %collective-permute-start.1 = (bf16[2,16,1536]{2,1,0:T(8,128)(2,1)S(1)}, bf16[2,16,1536]{2,1,0:T(8,128)(2,1)S(1)}, u32[]{:S(2)}, u32[]{:S(2)}) collective-permute-start(bf16[2,16,1536]{2,1,0:T(8,128)(2,1)S(1)} %constant_dynamic-slice_fusion), channel_id=1, source_target_pairs={{1,2},{2,1},{3,4},{4,3},{5,6},{6,5},{7,8},{8,7},{9,10},{10,9},{11,... | collective-permute-start | bytes 294920 | tf_op jit(solution)/shard_map/ppermute | solution.py:566
  4.5 0.9 %dynamic-slice_bitcast_fusion = bf16[56,1536]{1,0:T(8,128)(2,1)S(1)} fusion(bf16[2,56,1536]{2,1,0:T(8,128)(2,1)} %hidden_hbm.1, s32[]{:T(128)S(6)} %select_n.53), kind=kLoop, calls=%fused_computation | loop fusion | bytes 344068 | tf_op jit(solution)/shard_map/squeeze | solution.py:565
  5.4 0.2 collective-permute-start
  6.3 0.1 pad_add_fusion.info_ref
  6.4 1.6 %shard_map.113 = (bf16[56,1536]{1,0:T(8,128)(2,1)S(1)}, f32[31,1536]{1,0:T(8,128)S(1)}, f32[5,1536]{1,0:T(8,128)S(1)}, f32[56,100]{1,0:T(8,128)S(1)}, f32[56,100]{1,0:T(8,128)S(1)}) custom-call(s32[3]{0:T(128)S(1)} %pad_add_fusion.info_ref, bf16[2,56,1536]{2,1,0:T(8,128)(2,1)} %hidden_hbm.1, f32[31,1536]{1,0:T(8,128)} %taps_hbm.1, f32[5,1536]{1,0:T(8,128)} %mod_hbm.1), custom_call_target="tpu_custom_call" | custom-call | tf_op jit(solution)/shard_map/pallas_call | solution.py:363
  8.0 0.0 collective-permute-done.1.near_ref
  8.0 0.4 collective-permute-start.2
  8.4 1.9 %shard_map.115 = (bf16[256,3072]{1,0:T(8,128)(2,1)S(1)}, f32[112,128]{1,0:T(8,128)S(1)}, f32[112,128]{1,0:T(8,128)S(1)}) custom-call(s32[3]{0:T(128)S(1)} %pad_add_fusion.info_ref, f32[2,128]{1,0:T(2,128)S(1)} %pad_maximum_fusion.rates_ref, bf16[1536,3072]{1,0:T(8,128)(2,1)} %weight_hbm.3), custom_call_target="tpu_custom_call" | custom-call | tf_op jit(solution)/shard_map/pallas_call | solution.py:363
  10.4 0.0 collective-permute-done.partner_ref
  10.4 0.0 collective-permute-done.2.far_ref
  10.4 3.9 %shard_map.114 = (f32[112,1536]{1,0:T(8,128)S(1)}, bf16[112,1536]{1,0:T(8,128)(2,1)S(1)}, bf16[1280,3072]{1,0:T(8,128)(2,1)S(1)}) custom-call(s32[3]{0:T(128)S(1)} %pad_add_fusion.info_ref, bf16[56,1536]{1,0:T(8,128)(2,1)S(1)} %get-tuple-element.37.own_ref, bf16[56,1536]{1,0:T(8,128)(2,1)S(1)} %collective-permute-done.partner_ref, ...), custom_call_target="tpu_custom_call" | custom-call | tf_op jit(solution)/shard_map/pallas_call | solution.py:363
  14.3 1.2 %shard_map.118 = (bf16[3,112,128]{2,1,0:T(8,128)(2,1)S(1)}, bf16[3,112,128]{2,1,0:T(8,128)(2,1)S(1)}) custom-call(s32[3]{0:T(128)S(1)} %pad_add_fusion.info_ref, bf16[112,1536]{1,0:T(8,128)(2,1)S(1)} %get-tuple-element.41.normed_ref, bf16[256,3072]{1,0:T(8,128)(2,1)S(1)} %get-tuple-element.42.top_ref, bf16[1280,3072]{1,0:T(8,128)(2,1)S(1)} %get-tuple-element.43.rest_ref, ...), custom_call_target="tpu_custom_call" | custom-call | tf_op jit(solution)/shard_map/pallas_call | solution.py:363
  15.5 3.3 %collective-permute-start.6 = (bf16[3,112,128]{2,1,0:T(8,128)(2,1)S(1)}, bf16[3,112,128]{2,1,0:T(8,128)(2,1)S(1)}, u32[]{:S(2)}, u32[]{:S(2)}) collective-permute-start(bf16[3,112,128]{2,1,0:T(8,128)(2,1)S(1)} %get-tuple-element.50), channel_id=1, source_target_pairs={{0,12},{1,13},{2,14},{3,15},{4,8},{5,9},{6,10},{7,11},{8,4},{9,5},... | collective-permute-start | bytes 258056 | tf_op jit(solution)/shard_map/ppermute | solution.py:403
  18.8 1.2 %shard_map.117 = (bf16[3,112,128]{2,1,0:T(8,128)(2,1)S(1)}, bf16[3,112,128]{2,1,0:T(8,128)(2,1)S(1)}) custom-call(s32[3]{0:T(128)S(1)} %pad_add_fusion.info_ref, bf16[112,1536]{1,0:T(8,128)(2,1)S(1)} %get-tuple-element.41.normed_ref, bf16[256,3072]{1,0:T(8,128)(2,1)S(1)} %get-tuple-element.42.top_ref, bf16[1280,3072]{1,0:T(8,128)(2,1)S(1)} %get-tuple-element.43.rest_ref, ...), custom_call_target="tpu_custom_call" | custom-call | tf_op jit(solution)/shard_map/pallas_call | solution.py:363
  19.9 0.1 collective-permute-start.4
  20.0 1.2 %shard_map.120 = (bf16[3,112,128]{2,1,0:T(8,128)(2,1)S(1)}, bf16[3,112,128]{2,1,0:T(8,128)(2,1)S(1)}) custom-call(s32[3]{0:T(128)S(1)} %pad_add_fusion.info_ref, bf16[112,1536]{1,0:T(8,128)(2,1)S(1)} %get-tuple-element.41.normed_ref, bf16[256,3072]{1,0:T(8,128)(2,1)S(1)} %get-tuple-element.42.top_ref, bf16[1280,3072]{1,0:T(8,128)(2,1)S(1)} %get-tuple-element.43.rest_ref, ...), custom_call_target="tpu_custom_call" | custom-call | tf_op jit(solution)/shard_map/pallas_call | solution.py:363
  21.2 0.0 copy-start
  21.2 0.0 copy-start.1
  21.2 0.0 copy-start.2
  21.2 1.2 %shard_map.116 = (bf16[3,112,128]{2,1,0:T(8,128)(2,1)S(1)}, bf16[3,112,128]{2,1,0:T(8,128)(2,1)S(1)}) custom-call(s32[3]{0:T(128)S(1)} %pad_add_fusion.info_ref, bf16[112,1536]{1,0:T(8,128)(2,1)S(1)} %get-tuple-element.41.normed_ref, bf16[256,3072]{1,0:T(8,128)(2,1)S(1)} %get-tuple-element.42.top_ref, bf16[1280,3072]{1,0:T(8,128)(2,1)S(1)} %get-tuple-element.43.rest_ref, ...), custom_call_target="tpu_custom_call" | custom-call | tf_op jit(solution)/shard_map/pallas_call | solution.py:363
  22.4 1.2 %collective-permute-start.7 = (bf16[3,112,128]{2,1,0:T(8,128)(2,1)S(1)}, bf16[3,112,128]{2,1,0:T(8,128)(2,1)S(1)}, u32[]{:S(2)}, u32[]{:S(2)}) collective-permute-start(bf16[3,112,128]{2,1,0:T(8,128)(2,1)S(1)} %get-tuple-element.57), channel_id=1, source_target_pairs={{0,4},{1,5},{2,6},{3,7},{4,0},{5,1},{6,2},{7,3},{8,12},{9,13},{10,... | collective-permute-start | bytes 258056 | tf_op jit(solution)/shard_map/ppermute | solution.py:403
  23.6 2.3 %collective-permute-start.5 = (bf16[3,112,128]{2,1,0:T(8,128)(2,1)S(1)}, bf16[3,112,128]{2,1,0:T(8,128)(2,1)S(1)}, u32[]{:S(2)}, u32[]{:S(2)}) collective-permute-start(bf16[3,112,128]{2,1,0:T(8,128)(2,1)S(1)} %get-tuple-element.49), channel_id=1, source_target_pairs={{0,10},{1,11},{2,8},{3,9},{4,14},{5,15},{6,12},{7,13},{8,2},{9,3},... | collective-permute-start | bytes 258056 | tf_op jit(solution)/shard_map/ppermute | solution.py:403
  25.9 1.0 %collective-permute-start.3 = (bf16[3,112,128]{2,1,0:T(8,128)(2,1)S(1)}, bf16[3,112,128]{2,1,0:T(8,128)(2,1)S(1)}, u32[]{:S(2)}, u32[]{:S(2)}) collective-permute-start(bf16[3,112,128]{2,1,0:T(8,128)(2,1)S(1)} %get-tuple-element.47), channel_id=1, source_target_pairs={{0,2},{1,3},{2,0},{3,1},{4,6},{5,7},{6,4},{7,5},{8,10},{9,11},{10,... | collective-permute-start | bytes 258056 | tf_op jit(solution)/shard_map/ppermute | solution.py:403
  26.9 0.0 collective-permute-done.6.refs_4_.refs_3_
  26.9 2.3 %collective-permute-start.8 = (bf16[3,112,128]{2,1,0:T(8,128)(2,1)S(1)}, bf16[3,112,128]{2,1,0:T(8,128)(2,1)S(1)}, u32[]{:S(2)}, u32[]{:S(2)}) collective-permute-start(bf16[3,112,128]{2,1,0:T(8,128)(2,1)S(1)} %get-tuple-element.58), channel_id=1, source_target_pairs={{0,6},{1,7},{2,4},{3,5},{4,2},{5,3},{6,0},{7,1},{8,14},{9,15},{10,... | collective-permute-start | bytes 258056 | tf_op jit(solution)/shard_map/ppermute | solution.py:403
  29.2 0.0 collective-permute-done.4.refs_2_
  29.2 1.1 %collective-permute-start.9 = (bf16[3,112,128]{2,1,0:T(8,128)(2,1)S(1)}, bf16[3,112,128]{2,1,0:T(8,128)(2,1)S(1)}, u32[]{:S(2)}, u32[]{:S(2)}) collective-permute-start(bf16[3,112,128]{2,1,0:T(8,128)(2,1)S(1)} %get-tuple-element.59), channel_id=1, source_target_pairs={{0,14},{1,15},{2,12},{3,13},{4,10},{5,11},{6,8},{7,9},{8,6},{9,7},... | collective-permute-start | bytes 258056 | tf_op jit(solution)/shard_map/ppermute | solution.py:403
  30.4 0.2 collective-permute-done.5.refs_3_
  30.6 2.7 %collective-permute-done.3.refs_1_ = bf16[3,112,128]{2,1,0:T(8,128)(2,1)S(1)} collective-permute-done((bf16[3,112,128]{2,1,0:T(8,128)(2,1)S(1)}, bf16[3,112,128]{2,1,0:T(8,128)(2,1)S(1)}, u32[]{:S(2)}, u32[]{:S(2)}) %collective-permute-start.3) | collective-permute-done | bytes 86048 | tf_op jit(solution)/shard_map/ppermute | solution.py:403
  33.2 1.4 %shard_map.119 = (bf16[560,256]{1,0:T(8,128)(2,1)S(1)}, bf16[560,128]{1,0:T(8,128)(2,1)S(1)}, bf16[448,256]{1,0:T(8,128)(2,1)S(1)}, f32[448,128]{1,0:T(8,128)S(1...) custom-call(s32[3]{0:T(128)S(1)} %pad_add_fusion.info_ref, bf16[3,112,128]{2,1,0:T(8,128)(2,1)S(1)} %get-tuple-element.46.refs_0_, ...), custom_call_target="tpu_custom_call" | custom-call | tf_op jit(solution)/shard_map/pallas_call | solution.py:363
  34.7 0.0 collective-permute-done.7.refs_0_.refs_1_
  34.7 1.7 %collective-permute-done.9.refs_2_ = bf16[3,112,128]{2,1,0:T(8,128)(2,1)S(1)} collective-permute-done((bf16[3,112,128]{2,1,0:T(8,128)(2,1)S(1)}, bf16[3,112,128]{2,1,0:T(8,128)(2,1)S(1)}, u32[]{:S(2)}, u32[]{:S(2)}) %collective-permute-start.9) | collective-permute-done | bytes 86048 | tf_op jit(solution)/shard_map/ppermute | solution.py:403
  36.4 2.7 %shard_map.121 = (bf16[4,112,128]{2,1,0:T(8,128)(2,1)S(1)}, bf16[896,256]{1,0:T(8,128)(2,1)S(1)}, bf16[896,128]{1,0:T(8,128)(2,1)S(1)}) custom-call(s32[3]{0:T(128)S(1)} %pad_add_fusion.info_ref, bf16[560,256]{1,0:T(8,128)(2,1)S(1)} %get-tuple-element.51.early_keys, bf16[560,128]{1,0:T(8,128)(2,1)S(1)} %get-tuple-element.52.early_values, ...), custom_call_target="tpu_custom_call" | custom-call | tf_op jit(solution)/shard_map/pallas_call | solution.py:363
  39.1 1.2 %collective-permute-start.10 = (bf16[4,112,128]{2,1,0:T(8,128)(2,1)S(1)}, bf16[4,112,128]{2,1,0:T(8,128)(2,1)S(1)}, u32[]{:S(2)}, u32[]{:S(2)}) collective-permute-start(bf16[4,112,128]{2,1,0:T(8,128)(2,1)S(1)} %get-tuple-element.62), channel_id=1, source_target_pairs={{0,2},{1,3},{2,0},{3,1},{4,6},{5,7},{6,4},{7,5},{8,10},{9,11},{10,... | collective-permute-start | bytes 344072 | tf_op jit(solution)/shard_map/ppermute | solution.py:403
  40.3 2.3 %shard_map.122.own_ref.refs_0_ = bf16[4,112,128]{2,1,0:T(8,128)(2,1)S(1)} custom-call(s32[3]{0:T(128)S(1)} %pad_add_fusion.info_ref, bf16[896,256]{1,0:T(8,128)(2,1)S(1)} %get-tuple-element.60.keys, bf16[896,128]{1,0:T(8,128)(2,1)S(1)} %get-tuple-element.61.values, bf16[3,112,128]{2,1,0:T(8,128)(2,1)S(1)} %get-tuple-element.46.refs_0_, ...), custom_call_target="tpu_custom_call" | custom-call | tf_op jit(solution)/shard_map/pallas_call | solution.py:363
  42.6 1.3 %collective-permute-done.10.got_ref.refs_1_ = bf16[4,112,128]{2,1,0:T(8,128)(2,1)S(1)} collective-permute-done((bf16[4,112,128]{2,1,0:T(8,128)(2,1)S(1)}, bf16[4,112,128]{2,1,0:T(8,128)(2,1)S(1)}, u32[]{:S(2)}, u32[]{:S(2)}) %collective-permute-start.10) | collective-permute-done | bytes 114720 | tf_op jit(solution)/shard_map/ppermute | solution.py:403
  43.9 0.6 shard_map.123
  44.5 1.9 %collective-permute-start.11 = (bf16[2,112,128]{2,1,0:T(8,128)(2,1)S(1)}, bf16[2,112,128]{2,1,0:T(8,128)(2,1)S(1)}, u32[]{:S(2)}, u32[]{:S(2)}) collective-permute-start(bf16[2,112,128]{2,1,0:T(8,128)(2,1)S(1)} %get-tuple-element.63), channel_id=1, source_target_pairs={{0,4},{1,5},{2,6},{3,7},{4,0},{5,1},{6,2},{7,3},{8,12},{9,13},{10,... | collective-permute-start | bytes 172040 | tf_op jit(solution)/shard_map/ppermute | solution.py:403
  46.4 0.1 collective-permute-start.12
  46.5 2.4 %collective-permute-start.13 = (bf16[2,112,128]{2,1,0:T(8,128)(2,1)S(1)}, bf16[2,112,128]{2,1,0:T(8,128)(2,1)S(1)}, u32[]{:S(2)}, u32[]{:S(2)}) collective-permute-start(bf16[2,112,128]{2,1,0:T(8,128)(2,1)S(1)} %get-tuple-element.65), channel_id=1, source_target_pairs={{0,12},{1,13},{2,14},{3,15},{4,8},{5,9},{6,10},{7,11},{8,4},{9,5},... | collective-permute-start | bytes 172040 | tf_op jit(solution)/shard_map/ppermute | solution.py:403
  49.0 0.4 collective-permute-done.11.refs_2_
  49.4 2.4 %collective-permute-done.12.refs_3_ = bf16[2,112,128]{2,1,0:T(8,128)(2,1)S(1)} collective-permute-done((bf16[2,112,128]{2,1,0:T(8,128)(2,1)S(1)}, bf16[2,112,128]{2,1,0:T(8,128)(2,1)S(1)}, u32[]{:S(2)}, u32[]{:S(2)}) %collective-permute-start.12) | collective-permute-done | bytes 57376 | tf_op jit(solution)/shard_map/ppermute | solution.py:403
  51.7 0.9 %collective-permute-done.13.refs_4_ = bf16[2,112,128]{2,1,0:T(8,128)(2,1)S(1)} collective-permute-done((bf16[2,112,128]{2,1,0:T(8,128)(2,1)S(1)}, bf16[2,112,128]{2,1,0:T(8,128)(2,1)S(1)}, u32[]{:S(2)}, u32[]{:S(2)}) %collective-permute-start.13) | collective-permute-done | bytes 57376 | tf_op jit(solution)/shard_map/ppermute | solution.py:403
  52.6 2.0 %shard_map.124 = (f32[56,100]{1,0:T(8,128)S(1)}, f32[56,100]{1,0:T(8,128)S(1)}) custom-call(s32[3]{0:T(128)S(1)} %pad_add_fusion.info_ref, f32[112,1536]{1,0:T(8,128)S(1)} %get-tuple-element.40.residual, bf16[100,1536]{1,0:T(8,128)(2,1)S(1)} %bitcast.8, f32[5,1536]{1,0:T(8,128)S(1)} %get-tuple-element.39.mod_ref, bf16[1024,1536]{1,0:T(8,128)(2,1)S(1)} %copy-done, ...), custom_call_target="tpu_custom_call" | custom-call | tf_op jit(solution)/shard_map/pallas_call | solution.py:363
  54.7 0.1 collective-permute-start.14
  56.1 0.0 collective-permute-done.14
  56.2 0.6 %multiply_add_fusion = (f32[56,100]{1,0:T(8,128)}, f32[56,100]{1,0:T(8,128)}) fusion(f32[56,100]{1,0:T(8,128)S(1)} %copy-done.2, f32[]{:T(128)} %bitcast.5, f32[56,100]{1,0:T(8,128)S(1)} %collective-permute-done.14, f32[56,100]{1,0:T(8,128)S(1)} %get-tuple-element.66, f32[]{:T(128)} %bitcast.7, f32[56,100]{1,0:T(8,128)S(1)} %get-tuple-element.36, ...), kind=kLoop, calls=%fused_computation.1 | loop fusion | flops 56000 | bytes 156808 | tf_op jit(solution)/shard_map/add | solution.py:630
  (6 shorter events, 0.0 us)
Async XLA Ops:
  1.5 6.4 %collective-permute-start.1 = (bf16[2,16,1536]{2,1,0:T(8,128)(2,1)S(1)}, bf16[2,16,1536]{2,1,0:T(8,128)(2,1)S(1)}, u32[]{:S(2)}, u32[]{:S(2)}) collective-permute-start(bf16[2,16,1536]{2,1,0:T(8,128)(2,1)S(1)} %constant_dynamic-slice_fusion), channel_id=1, source_target_pairs={{1,2},{2,1},{3,4},{4,3},{5,6},{6,5},{7,8},{8,7},{9,10},{10,9},{11,... | collective-permute-start | bytes 294920 | tf_op jit(solution)/shard_map/ppermute | solution.py:566
  5.4 4.9 %collective-permute-start = (bf16[56,1536]{1,0:T(8,128)(2,1)S(1)}, bf16[56,1536]{1,0:T(8,128)(2,1)S(1)}, u32[]{:S(2)}, u32[]{:S(2)}) collective-permute-start(bf16[56,1536]{1,0:T(8,128)(2,1)S(1)} %dynamic-slice_bitcast_fusion), channel_id=1, source_target_pairs={{0,1},{1,0},{2,3},{3,2},{4,5},{5,4},{6,7},{7,6},{8,9},{9,8},{10,11... | collective-permute-start | bytes 516104 | tf_op jit(solution)/shard_map/ppermute | solution.py:403
  8.0 2.4 %collective-permute-start.2 = (bf16[2,16,1536]{2,1,0:T(8,128)(2,1)S(1)}, bf16[2,16,1536]{2,1,0:T(8,128)(2,1)S(1)}, u32[]{:S(2)}, u32[]{:S(2)}) collective-permute-start(bf16[2,16,1536]{2,1,0:T(8,128)(2,1)S(1)} %collective-permute-done.1.near_ref), channel_id=1, source_target_pairs={{0,1},{1,0},{2,3},{3,2},{4,5},{5,4},{6,7},{7,6},{8,9},{9,8},{10,11... | collective-permute-start | bytes 294920 | tf_op jit(solution)/shard_map/ppermute | solution.py:403
  15.5 11.5 %collective-permute-start.6 = (bf16[3,112,128]{2,1,0:T(8,128)(2,1)S(1)}, bf16[3,112,128]{2,1,0:T(8,128)(2,1)S(1)}, u32[]{:S(2)}, u32[]{:S(2)}) collective-permute-start(bf16[3,112,128]{2,1,0:T(8,128)(2,1)S(1)} %get-tuple-element.50), channel_id=1, source_target_pairs={{0,12},{1,13},{2,14},{3,15},{4,8},{5,9},{6,10},{7,11},{8,4},{9,5},... | collective-permute-start | bytes 258056 | tf_op jit(solution)/shard_map/ppermute | solution.py:403
  19.9 9.3 %collective-permute-start.4 = (bf16[3,112,128]{2,1,0:T(8,128)(2,1)S(1)}, bf16[3,112,128]{2,1,0:T(8,128)(2,1)S(1)}, u32[]{:S(2)}, u32[]{:S(2)}) collective-permute-start(bf16[3,112,128]{2,1,0:T(8,128)(2,1)S(1)} %get-tuple-element.48), channel_id=1, source_target_pairs={{0,8},{1,9},{2,10},{3,11},{4,12},{5,13},{6,14},{7,15},{8,0},{9,1},... | collective-permute-start | bytes 258056 | tf_op jit(solution)/shard_map/ppermute | solution.py:403
  21.2 31.4 %copy-start = (bf16[1024,1536]{1,0:T(8,128)(2,1)S(1)}, bf16[1024,1536]{1,0:T(8,128)(2,1)}, u32[]{:S(2)}) copy-start(bf16[1024,1536]{1,0:T(8,128)(2,1)} %w_out_ref.1) | copy-start | bytes 9437188
  21.2 31.4 %copy-start.1 = (bf16[1536,100]{0,1:T(8,128)(2,1)S(1)}, bf16[1536,100]{0,1:T(8,128)(2,1)}, u32[]{:S(2)}) copy-start(bf16[1536,100]{0,1:T(8,128)(2,1)} %param.19) | copy-start | bytes 921604
  21.2 34.9 %copy-start.2 = (f32[56,100]{1,0:T(8,128)S(1)}, f32[56,100]{1,0:T(8,128)}, u32[]{:S(2)}) copy-start(f32[56,100]{1,0:T(8,128)} %param.11) | copy-start | bytes 67204
  22.4 12.3 %collective-permute-start.7 = (bf16[3,112,128]{2,1,0:T(8,128)(2,1)S(1)}, bf16[3,112,128]{2,1,0:T(8,128)(2,1)S(1)}, u32[]{:S(2)}, u32[]{:S(2)}) collective-permute-start(bf16[3,112,128]{2,1,0:T(8,128)(2,1)S(1)} %get-tuple-element.57), channel_id=1, source_target_pairs={{0,4},{1,5},{2,6},{3,7},{4,0},{5,1},{6,2},{7,3},{8,12},{9,13},{10,... | collective-permute-start | bytes 258056 | tf_op jit(solution)/shard_map/ppermute | solution.py:403
  23.6 7.0 %collective-permute-start.5 = (bf16[3,112,128]{2,1,0:T(8,128)(2,1)S(1)}, bf16[3,112,128]{2,1,0:T(8,128)(2,1)S(1)}, u32[]{:S(2)}, u32[]{:S(2)}) collective-permute-start(bf16[3,112,128]{2,1,0:T(8,128)(2,1)S(1)} %get-tuple-element.49), channel_id=1, source_target_pairs={{0,10},{1,11},{2,8},{3,9},{4,14},{5,15},{6,12},{7,13},{8,2},{9,3},... | collective-permute-start | bytes 258056 | tf_op jit(solution)/shard_map/ppermute | solution.py:403
  25.9 7.3 %collective-permute-start.3 = (bf16[3,112,128]{2,1,0:T(8,128)(2,1)S(1)}, bf16[3,112,128]{2,1,0:T(8,128)(2,1)S(1)}, u32[]{:S(2)}, u32[]{:S(2)}) collective-permute-start(bf16[3,112,128]{2,1,0:T(8,128)(2,1)S(1)} %get-tuple-element.47), channel_id=1, source_target_pairs={{0,2},{1,3},{2,0},{3,1},{4,6},{5,7},{6,4},{7,5},{8,10},{9,11},{10,... | collective-permute-start | bytes 258056 | tf_op jit(solution)/shard_map/ppermute | solution.py:403
  26.9 7.8 %collective-permute-start.8 = (bf16[3,112,128]{2,1,0:T(8,128)(2,1)S(1)}, bf16[3,112,128]{2,1,0:T(8,128)(2,1)S(1)}, u32[]{:S(2)}, u32[]{:S(2)}) collective-permute-start(bf16[3,112,128]{2,1,0:T(8,128)(2,1)S(1)} %get-tuple-element.58), channel_id=1, source_target_pairs={{0,6},{1,7},{2,4},{3,5},{4,2},{5,3},{6,0},{7,1},{8,14},{9,15},{10,... | collective-permute-start | bytes 258056 | tf_op jit(solution)/shard_map/ppermute | solution.py:403
  29.2 7.2 %collective-permute-start.9 = (bf16[3,112,128]{2,1,0:T(8,128)(2,1)S(1)}, bf16[3,112,128]{2,1,0:T(8,128)(2,1)S(1)}, u32[]{:S(2)}, u32[]{:S(2)}) collective-permute-start(bf16[3,112,128]{2,1,0:T(8,128)(2,1)S(1)} %get-tuple-element.59), channel_id=1, source_target_pairs={{0,14},{1,15},{2,12},{3,13},{4,10},{5,11},{6,8},{7,9},{8,6},{9,7},... | collective-permute-start | bytes 258056 | tf_op jit(solution)/shard_map/ppermute | solution.py:403
  39.1 4.8 %collective-permute-start.10 = (bf16[4,112,128]{2,1,0:T(8,128)(2,1)S(1)}, bf16[4,112,128]{2,1,0:T(8,128)(2,1)S(1)}, u32[]{:S(2)}, u32[]{:S(2)}) collective-permute-start(bf16[4,112,128]{2,1,0:T(8,128)(2,1)S(1)} %get-tuple-element.62), channel_id=1, source_target_pairs={{0,2},{1,3},{2,0},{3,1},{4,6},{5,7},{6,4},{7,5},{8,10},{9,11},{10,... | collective-permute-start | bytes 344072 | tf_op jit(solution)/shard_map/ppermute | solution.py:403
  44.5 4.9 %collective-permute-start.11 = (bf16[2,112,128]{2,1,0:T(8,128)(2,1)S(1)}, bf16[2,112,128]{2,1,0:T(8,128)(2,1)S(1)}, u32[]{:S(2)}, u32[]{:S(2)}) collective-permute-start(bf16[2,112,128]{2,1,0:T(8,128)(2,1)S(1)} %get-tuple-element.63), channel_id=1, source_target_pairs={{0,4},{1,5},{2,6},{3,7},{4,0},{5,1},{6,2},{7,3},{8,12},{9,13},{10,... | collective-permute-start | bytes 172040 | tf_op jit(solution)/shard_map/ppermute | solution.py:403
  46.4 5.3 %collective-permute-start.12 = (bf16[2,112,128]{2,1,0:T(8,128)(2,1)S(1)}, bf16[2,112,128]{2,1,0:T(8,128)(2,1)S(1)}, u32[]{:S(2)}, u32[]{:S(2)}) collective-permute-start(bf16[2,112,128]{2,1,0:T(8,128)(2,1)S(1)} %get-tuple-element.64), channel_id=1, source_target_pairs={{0,8},{1,9},{2,10},{3,11},{4,12},{5,13},{6,14},{7,15},{8,0},{9,1},... | collective-permute-start | bytes 172040 | tf_op jit(solution)/shard_map/ppermute | solution.py:403
  46.5 6.1 %collective-permute-start.13 = (bf16[2,112,128]{2,1,0:T(8,128)(2,1)S(1)}, bf16[2,112,128]{2,1,0:T(8,128)(2,1)S(1)}, u32[]{:S(2)}, u32[]{:S(2)}) collective-permute-start(bf16[2,112,128]{2,1,0:T(8,128)(2,1)S(1)} %get-tuple-element.65), channel_id=1, source_target_pairs={{0,12},{1,13},{2,14},{3,15},{4,8},{5,9},{6,10},{7,11},{8,4},{9,5},... | collective-permute-start | bytes 172040 | tf_op jit(solution)/shard_map/ppermute | solution.py:403
  54.7 1.5 %collective-permute-start.14 = (f32[56,100]{1,0:T(8,128)S(1)}, f32[56,100]{1,0:T(8,128)S(1)}, u32[]{:S(2)}, u32[]{:S(2)}) collective-permute-start(f32[56,100]{1,0:T(8,128)S(1)} %get-tuple-element.67), channel_id=1, source_target_pairs={{0,1},{1,0},{2,3},{3,2},{4,5},{5,4},{6,7},{7,6},{8,9},{9,8},{10,11... | collective-permute-start | bytes 67208 | tf_op jit(solution)/shard_map/ppermute | solution.py:403

commit v3 on v1

--- a/solution.py
+++ b/solution.py
@@ -97,9 +97,10 @@
 
 
 def front_kernel(
-    info_ref, own_ref, partner_ref, near_ref, far_ref, taps_ref, mod_ref, weight_hbm,
-    residual_ref, normed_ref, weight_ref, padded, sems,
+    firsts, info_ref, own_ref, partner_ref, near_ref, far_ref, taps_ref, mod_ref, cos_ref, sin_ref,
+    weight_hbm, residual_ref, normed_ref, weight_ref, *refs,
 ):
+    *out_refs, padded, sems = refs
     rows, width = own_ref.shape
     halo = near_ref.shape[1]
     total_rows = 2 * rows
@@ -154,16 +155,17 @@
     row_norm(lambda tile: residual_ref[:, tile_lanes(tile)], store, tiles, mod_ref, 0, total)
     for load in loads:
         load.wait()
-
-
-def project_kernel(firsts, origin, info_ref, normed_ref, weight_ref, cos_ref, sin_ref, *out_refs):
+    chip = info_ref[CHIP]
+    project_pairs(firsts, chip, normed_ref, weight_ref, cos_ref, sin_ref, out_refs)
+
+
+def project_pairs(firsts, chip, normed_ref, weight_ref, cos_ref, sin_ref, out_refs):
     rows = normed_ref.shape[0]
     attn = weight_ref.shape[1] // 3
     wide = 2 * LANES
     half = HEAD_DIM // 2
     cosine, sine = cos_ref[...], sin_ref[...]
     lower = lax.broadcasted_iota(jnp.int32, (rows, LANES), 1) % HEAD_DIM < half
-    chip = info_ref[CHIP] if origin is None else origin
     swap = jnp.full((rows, LANES), chip & 1, jnp.int32) > 0
     for at, apart in enumerate(firsts):
         pair = (chip ^ apart) >> 1
@@ -189,6 +191,11 @@
             out_refs[2 * at + 1][part] = jnp.where(swap, sides[0], sides[1]).astype(jnp.bfloat16)
 
 
+def project_kernel(firsts, origin, info_ref, normed_ref, weight_ref, cos_ref, sin_ref, *out_refs):
+    chip = info_ref[CHIP] if origin is None else origin
+    project_pairs(firsts, chip, normed_ref, weight_ref, cos_ref, sin_ref, out_refs)
+
+
 def place_keys(info_ref, apart, got_ref, keys, values, first):
     _, rows, _ = got_ref.shape
     chip = info_ref[CHIP] ^ apart
@@ -463,12 +470,13 @@
     return far[:1] + list(range(2, chips // 2, 2)) + far[1:] + [0]
 
 
-def attend_chips(normed, w_qkv, tables, info, count):
+def attend_chips(made, normed, w_qkv, tables, info, count):
     rows = normed.shape[0]
     chips = count // 2
     held = {}
     for first in send_order(chips):
-        made = project(normed, w_qkv, tables, info, [first])
+        if held:
+            made = project(normed, w_qkv, tables, info, [first])
         for side in range(2):
             apart = first + side
             held[apart] = across(made[side], 2 * apart, count) if apart else made[side]
@@ -522,6 +530,7 @@
 ):
     copies, rows, width = hidden.shape
     count = lax.axis_size("seq")
+    chips = count // 2
     index = lax.axis_index("seq").astype(jnp.int32)
     chip, core = index >> 1, index & 1
     chip_rows = 2 * rows
@@ -546,19 +555,22 @@
         hbm=(1, 2, 3),
     )
     tables = rotary_tables(chip * chip_rows + jnp.arange(chip_rows, dtype=jnp.int32))
-    residual, normed, weight = call(
-        front_kernel,
+    firsts = tuple(send_order(chips)[:1]) if chips_hold_groups(count) else ()
+    group = array((3, chip_rows, LANES), jnp.bfloat16)
+    residual, normed, weight, *made = call(
+        functools.partial(front_kernel, firsts),
         (
             array((chip_rows, width)),
             array((chip_rows, width), jnp.bfloat16),
             array(w_qkv.shape, jnp.bfloat16),
-        ),
-        (info, own, partner, near, far, taps, mods, w_qkv),
+        )
+        + (group,) * (2 * len(firsts)),
+        (info, own, partner, near, far, taps, mods) + tables + (w_qkv,),
         [VMEM((chip_rows + 2 * HALO, LANES), jnp.float32), pltpu.SemaphoreType.DMA((8,))],
-        hbm=(7,),
+        hbm=(9,),
     )
     if chips_hold_groups(count):
-        back, blocks = attend_chips(normed, weight, tables, info, count)
+        back, blocks = attend_chips(made, normed, weight, tables, info, count)
     else:
         back = [attend_any(normed, weight, tables, info, lengths[0], count)]
         blocks = [(0, group, None) for group in range(back[0].shape[0])]

time: 58 us -> 59.9 us (1.033)
  waiting for transfers between devices: 12.1 us -> 13.9 us
  Pallas kernels: 19.3 us -> 18.7 us
  starting transfers between devices: 20.7 us -> 21.3 us
    ppermute x14, waiting for transfers between devices: 11.6 us -> 13.5 us  [across(): return lax.ppermute(value, 'seq', [(i, i ^ apart) for i in range(count)])]
    pallas_call x11 -> x10, Pallas kernels: 19.3 us -> 18.7 us  [call(): pl.pallas_call(kernel, out_shape=out_shape, in_specs=[smem_spec()] + spec...]
  transfers between devices with their start and end apart: 15 -> 15, of which waited for: 7 -> 7; matrix products, arithmetic and copies ran while one was open for 2% -> 2% of each run, Pallas kernels for 17% -> 14%
where the time goes in v3:
time: 59.9 us; the launch traced here: 59.6 us
  starting transfers between devices  21.3 us (36%)
  Pallas kernels  18.7 us (31%)
  waiting for transfers between devices  13.9 us (23%)
  between operations  2.83 us (5%)
  local copies, waits for them, and re-layouts  1.86 us (3%)
  other arithmetic  1.01 us (2%)
    pallas_call x10, Pallas kernels, call(): pl.pallas_call(kernel, out_shape=out_shape, in_specs=[smem_spec()] + spec...  18.7 us
    ppermute x14, starting transfers between devices, across(): return lax.ppermute(value, 'seq', [(i, i ^ apart) for i in range(count)])  18.3 us
    ppermute x14, waiting for transfers between devices, across(): return lax.ppermute(value, 'seq', [(i, i ^ apart) for i in range(count)])  13.5 us
    ppermute x1, starting transfers between devices, per_device(): lax.ppermute(edges, ('clip', 'seq'), facing_pairs(lax.axis_size('clip'),...  2.97 us
  transfers between devices with their start and end apart: 15, of which 7 were waited for; matrix products, arithmetic and copies ran while one was open for 2% of the time, Pallas kernels for 14%

profile of v3, /device:TPU:0, one launch (start us, length us, event | category | flops | bytes accessed | tf_op | source)
XLA Modules:
  0.0 59.6 jit_solution(16120808149747423211)
XLA Ops:
  0.6 0.9 %constant_dynamic-slice_fusion = bf16[2,16,1536]{2,1,0:T(8,128)(2,1)S(1)} fusion(bf16[2,56,1536]{2,1,0:T(8,128)(2,1)} %hidden_hbm.1, s32[]{:T(128)S(6)} %select_n.45), kind=kLoop, calls=%fused_computation.15 | loop fusion | bytes 196612 | tf_op jit(solution)/shard_map/dynamic_slice | solution.py:539
  1.5 3.0 %collective-permute-start.1 = (bf16[2,16,1536]{2,1,0:T(8,128)(2,1)S(1)}, bf16[2,16,1536]{2,1,0:T(8,128)(2,1)S(1)}, u32[]{:S(2)}, u32[]{:S(2)}) collective-permute-start(bf16[2,16,1536]{2,1,0:T(8,128)(2,1)S(1)} %constant_dynamic-slice_fusion), channel_id=1, source_target_pairs={{1,2},{2,1},{3,4},{4,3},{5,6},{6,5},{7,8},{8,7},{9,10},{10,9},{11,... | collective-permute-start | bytes 294920 | tf_op jit(solution)/shard_map/ppermute | solution.py:541
  4.5 0.9 %dynamic-slice_bitcast_fusion = bf16[56,1536]{1,0:T(8,128)(2,1)S(1)} fusion(bf16[2,56,1536]{2,1,0:T(8,128)(2,1)} %hidden_hbm.1, s32[]{:T(128)S(6)} %select_n.44), kind=kLoop, calls=%fused_computation | loop fusion | bytes 344068 | tf_op jit(solution)/shard_map/squeeze | solution.py:540
  5.4 0.2 collective-permute-start
  5.7 0.3 fusion
  6.6 0.5 collective-permute-done.1.near_ref
  7.1 0.1 collective-permute-start.2
  7.2 0.1 pad_add_fusion.info_ref
  7.3 1.6 %shard_map.113 = (bf16[56,1536]{1,0:T(8,128)(2,1)S(1)}, f32[31,1536]{1,0:T(8,128)S(1)}, f32[5,1536]{1,0:T(8,128)S(1)}, f32[56,100]{1,0:T(8,128)S(1)}, f32[56,100]{1,0:T(8,128)S(1)}) custom-call(s32[3]{0:T(128)S(1)} %pad_add_fusion.info_ref, bf16[2,56,1536]{2,1,0:T(8,128)(2,1)} %hidden_hbm.1, f32[31,1536]{1,0:T(8,128)} %taps_hbm.1, f32[5,1536]{1,0:T(8,128)} %mod_hbm.1), custom_call_target="tpu_custom_call" | custom-call | tf_op jit(solution)/shard_map/pallas_call | solution.py:345
  8.9 0.0 collective-permute-done.partner_ref
  8.9 0.0 collective-permute-done.2.far_ref
  8.9 4.9 %shard_map.114 = (f32[112,1536]{1,0:T(8,128)S(1)}, bf16[112,1536]{1,0:T(8,128)(2,1)S(1)}, bf16[1536,3072]{1,0:T(8,128)(2,1)S(1)}, bf16[3,112,128]{2,1,0:T(8,128)(2,1)S(1)}, bf16[3,112,128]{2,1,0:T(8,128)(2,1)S(1)}) custom-call(s32[3]{0:T(128)S(1)} %pad_add_fusion.info_ref, bf16[56,1536]{1,0:T(8,128)(2,1)S(1)} %get-tuple-element.34.own_ref, ...), custom_call_target="tpu_custom_call" | custom-call | tf_op jit(solution)/shard_map/pallas_call | solution.py:345
  13.9 1.2 %shard_map.117 = (bf16[3,112,128]{2,1,0:T(8,128)(2,1)S(1)}, bf16[3,112,128]{2,1,0:T(8,128)(2,1)S(1)}) custom-call(s32[3]{0:T(128)S(1)} %pad_add_fusion.info_ref, bf16[112,1536]{1,0:T(8,128)(2,1)S(1)} %get-tuple-element.38.normed_ref, bf16[1536,3072]{1,0:T(8,128)(2,1)S(1)} %get-tuple-element.39.weight_ref, f32[112,128]{1,0:T(8,128)S(1)} %get-tuple-element.65.cos_ref, ...), custom_call_target="tpu_custom_call" | custom-call | tf_op jit(solution)/shard_map/pallas_call | solution.py:345
  15.1 4.6 %collective-permute-start.8 = (bf16[3,112,128]{2,1,0:T(8,128)(2,1)S(1)}, bf16[3,112,128]{2,1,0:T(8,128)(2,1)S(1)}, u32[]{:S(2)}, u32[]{:S(2)}) collective-permute-start(bf16[3,112,128]{2,1,0:T(8,128)(2,1)S(1)} %get-tuple-element.46), channel_id=1, source_target_pairs={{0,12},{1,13},{2,14},{3,15},{4,8},{5,9},{6,10},{7,11},{8,4},{9,5},... | collective-permute-start | bytes 258056 | tf_op jit(solution)/shard_map/ppermute | solution.py:385
  19.6 1.2 %shard_map.116 = (bf16[3,112,128]{2,1,0:T(8,128)(2,1)S(1)}, bf16[3,112,128]{2,1,0:T(8,128)(2,1)S(1)}) custom-call(s32[3]{0:T(128)S(1)} %pad_add_fusion.info_ref, bf16[112,1536]{1,0:T(8,128)(2,1)S(1)} %get-tuple-element.38.normed_ref, bf16[1536,3072]{1,0:T(8,128)(2,1)S(1)} %get-tuple-element.39.weight_ref, f32[112,128]{1,0:T(8,128)S(1)} %get-tuple-element.65.cos_ref, ...), custom_call_target="tpu_custom_call" | custom-call | tf_op jit(solution)/shard_map/pallas_call | solution.py:345
  20.8 0.0 copy-start
  20.8 0.0 copy-start.1
  20.9 0.0 copy-start.2
  20.9 0.1 collective-permute-start.4
  20.9 1.2 %shard_map.115 = (bf16[3,112,128]{2,1,0:T(8,128)(2,1)S(1)}, bf16[3,112,128]{2,1,0:T(8,128)(2,1)S(1)}) custom-call(s32[3]{0:T(128)S(1)} %pad_add_fusion.info_ref, bf16[112,1536]{1,0:T(8,128)(2,1)S(1)} %get-tuple-element.38.normed_ref, bf16[1536,3072]{1,0:T(8,128)(2,1)S(1)} %get-tuple-element.39.weight_ref, f32[112,128]{1,0:T(8,128)S(1)} %get-tuple-element.65.cos_ref, ...), custom_call_target="tpu_custom_call" | custom-call | tf_op jit(solution)/shard_map/pallas_call | solution.py:345
  22.1 2.0 %collective-permute-start.5 = (bf16[3,112,128]{2,1,0:T(8,128)(2,1)S(1)}, bf16[3,112,128]{2,1,0:T(8,128)(2,1)S(1)}, u32[]{:S(2)}, u32[]{:S(2)}) collective-permute-start(bf16[3,112,128]{2,1,0:T(8,128)(2,1)S(1)} %get-tuple-element.43), channel_id=1, source_target_pairs={{0,6},{1,7},{2,4},{3,5},{4,2},{5,3},{6,0},{7,1},{8,14},{9,15},{10,... | collective-permute-start | bytes 258056 | tf_op jit(solution)/shard_map/ppermute | solution.py:385
  24.1 1.6 %collective-permute-start.3 = (bf16[3,112,128]{2,1,0:T(8,128)(2,1)S(1)}, bf16[3,112,128]{2,1,0:T(8,128)(2,1)S(1)}, u32[]{:S(2)}, u32[]{:S(2)}) collective-permute-start(bf16[3,112,128]{2,1,0:T(8,128)(2,1)S(1)} %get-tuple-element.41), channel_id=1, source_target_pairs={{0,2},{1,3},{2,0},{3,1},{4,6},{5,7},{6,4},{7,5},{8,10},{9,11},{10,... | collective-permute-start | bytes 258056 | tf_op jit(solution)/shard_map/ppermute | solution.py:385
  25.7 0.0 collective-permute-start.6
  25.7 0.0 collective-permute-done.8.refs_6_.refs_3_
  25.7 2.8 %collective-permute-start.7 = (bf16[3,112,128]{2,1,0:T(8,128)(2,1)S(1)}, bf16[3,112,128]{2,1,0:T(8,128)(2,1)S(1)}, u32[]{:S(2)}, u32[]{:S(2)}) collective-permute-start(bf16[3,112,128]{2,1,0:T(8,128)(2,1)S(1)} %get-tuple-element.45), channel_id=1, source_target_pairs={{0,10},{1,11},{2,8},{3,9},{4,14},{5,15},{6,12},{7,13},{8,2},{9,3},... | collective-permute-start | bytes 258056 | tf_op jit(solution)/shard_map/ppermute | solution.py:385
  28.5 0.0 collective-permute-done.4.refs_2_.refs_1_
  28.5 1.0 %collective-permute-start.9 = (bf16[3,112,128]{2,1,0:T(8,128)(2,1)S(1)}, bf16[3,112,128]{2,1,0:T(8,128)(2,1)S(1)}, u32[]{:S(2)}, u32[]{:S(2)}) collective-permute-start(bf16[3,112,128]{2,1,0:T(8,128)(2,1)S(1)} %get-tuple-element.53), channel_id=1, source_target_pairs={{0,14},{1,15},{2,12},{3,13},{4,10},{5,11},{6,8},{7,9},{8,6},{9,7},... | collective-permute-start | bytes 258056 | tf_op jit(solution)/shard_map/ppermute | solution.py:385
  29.5 0.0 collective-permute-done.5.refs_3_
  29.5 0.1 collective-permute-done.3.refs_1_
  29.5 5.4 %collective-permute-done.6.refs_4_.refs_2_ = bf16[3,112,128]{2,1,0:T(8,128)(2,1)S(1)} collective-permute-done((bf16[3,112,128]{2,1,0:T(8,128)(2,1)S(1)}, bf16[3,112,128]{2,1,0:T(8,128)(2,1)S(1)}, u32[]{:S(2)}, u32[]{:S(2)}) %collective-permute-start.6) | collective-permute-done | bytes 86048 | tf_op jit(solution)/shard_map/ppermute | solution.py:385
  35.0 2.8 %collective-permute-done.7.refs_5_ = bf16[3,112,128]{2,1,0:T(8,128)(2,1)S(1)} collective-permute-done((bf16[3,112,128]{2,1,0:T(8,128)(2,1)S(1)}, bf16[3,112,128]{2,1,0:T(8,128)(2,1)S(1)}, u32[]{:S(2)}, u32[]{:S(2)}) %collective-permute-start.7) | collective-permute-done | bytes 86048 | tf_op jit(solution)/shard_map/ppermute | solution.py:385
  37.8 2.2 %shard_map.118 = (bf16[784,256]{1,0:T(8,128)(2,1)S(1)}, bf16[784,128]{1,0:T(8,128)(2,1)S(1)}, bf16[672,256]{1,0:T(8,128)(2,1)S(1)}, f32[672,128]{1,0:T(8,128)S(1...) custom-call(s32[3]{0:T(128)S(1)} %pad_add_fusion.info_ref, bf16[3,112,128]{2,1,0:T(8,128)(2,1)S(1)} %get-tuple-element.40.refs_0_, ...), custom_call_target="tpu_custom_call" | custom-call | tf_op jit(solution)/shard_map/pallas_call | solution.py:345
  39.9 0.0 collective-permute-done.9.last_ref
  40.0 1.5 %shard_map.119 = (bf16[4,112,128]{2,1,0:T(8,128)(2,1)S(1)}, bf16[896,256]{1,0:T(8,128)(2,1)S(1)}, bf16[896,128]{1,0:T(8,128)(2,1)S(1)}) custom-call(s32[3]{0:T(128)S(1)} %pad_add_fusion.info_ref, bf16[784,256]{1,0:T(8,128)(2,1)S(1)} %get-tuple-element.47.early_keys, bf16[784,128]{1,0:T(8,128)(2,1)S(1)} %get-tuple-element.48.early_values, ...), custom_call_target="tpu_custom_call" | custom-call | tf_op jit(solution)/shard_map/pallas_call | solution.py:345
  41.5 1.5 %collective-permute-start.10 = (bf16[4,112,128]{2,1,0:T(8,128)(2,1)S(1)}, bf16[4,112,128]{2,1,0:T(8,128)(2,1)S(1)}, u32[]{:S(2)}, u32[]{:S(2)}) collective-permute-start(bf16[4,112,128]{2,1,0:T(8,128)(2,1)S(1)} %get-tuple-element.56), channel_id=1, source_target_pairs={{0,2},{1,3},{2,0},{3,1},{4,6},{5,7},{6,4},{7,5},{8,10},{9,11},{10,... | collective-permute-start | bytes 344072 | tf_op jit(solution)/shard_map/ppermute | solution.py:385
  43.0 2.3 %shard_map.120.own_ref.refs_0_ = bf16[4,112,128]{2,1,0:T(8,128)(2,1)S(1)} custom-call(s32[3]{0:T(128)S(1)} %pad_add_fusion.info_ref, bf16[896,256]{1,0:T(8,128)(2,1)S(1)} %get-tuple-element.54.keys, bf16[896,128]{1,0:T(8,128)(2,1)S(1)} %get-tuple-element.55.values, bf16[3,112,128]{2,1,0:T(8,128)(2,1)S(1)} %get-tuple-element.40.refs_0_, ...), custom_call_target="tpu_custom_call" | custom-call | tf_op jit(solution)/shard_map/pallas_call | solution.py:345
  45.3 1.3 %collective-permute-done.10.got_ref.refs_1_ = bf16[4,112,128]{2,1,0:T(8,128)(2,1)S(1)} collective-permute-done((bf16[4,112,128]{2,1,0:T(8,128)(2,1)S(1)}, bf16[4,112,128]{2,1,0:T(8,128)(2,1)S(1)}, u32[]{:S(2)}, u32[]{:S(2)}) %collective-permute-start.10) | collective-permute-done | bytes 114720 | tf_op jit(solution)/shard_map/ppermute | solution.py:385
  46.5 0.6 shard_map.121
  47.1 0.3 collective-permute-start.11
  47.4 2.1 %collective-permute-start.12 = (bf16[2,112,128]{2,1,0:T(8,128)(2,1)S(1)}, bf16[2,112,128]{2,1,0:T(8,128)(2,1)S(1)}, u32[]{:S(2)}, u32[]{:S(2)}) collective-permute-start(bf16[2,112,128]{2,1,0:T(8,128)(2,1)S(1)} %get-tuple-element.58), channel_id=1, source_target_pairs={{0,8},{1,9},{2,10},{3,11},{4,12},{5,13},{6,14},{7,15},{8,0},{9,1},... | collective-permute-start | bytes 172040 | tf_op jit(solution)/shard_map/ppermute | solution.py:385
  49.5 2.1 %collective-permute-start.13 = (bf16[2,112,128]{2,1,0:T(8,128)(2,1)S(1)}, bf16[2,112,128]{2,1,0:T(8,128)(2,1)S(1)}, u32[]{:S(2)}, u32[]{:S(2)}) collective-permute-start(bf16[2,112,128]{2,1,0:T(8,128)(2,1)S(1)} %get-tuple-element.59), channel_id=1, source_target_pairs={{0,12},{1,13},{2,14},{3,15},{4,8},{5,9},{6,10},{7,11},{8,4},{9,5},... | collective-permute-start | bytes 172040 | tf_op jit(solution)/shard_map/ppermute | solution.py:385
  51.6 0.0 collective-permute-done.11.refs_2_
  51.6 1.4 %collective-permute-done.12.refs_3_ = bf16[2,112,128]{2,1,0:T(8,128)(2,1)S(1)} collective-permute-done((bf16[2,112,128]{2,1,0:T(8,128)(2,1)S(1)}, bf16[2,112,128]{2,1,0:T(8,128)(2,1)S(1)}, u32[]{:S(2)}, u32[]{:S(2)}) %collective-permute-start.12) | collective-permute-done | bytes 57376 | tf_op jit(solution)/shard_map/ppermute | solution.py:385
  52.9 2.5 %collective-permute-done.13.refs_4_ = bf16[2,112,128]{2,1,0:T(8,128)(2,1)S(1)} collective-permute-done((bf16[2,112,128]{2,1,0:T(8,128)(2,1)S(1)}, bf16[2,112,128]{2,1,0:T(8,128)(2,1)S(1)}, u32[]{:S(2)}, u32[]{:S(2)}) %collective-permute-start.13) | collective-permute-done | bytes 57376 | tf_op jit(solution)/shard_map/ppermute | solution.py:385
  55.5 2.0 %shard_map.122 = (f32[56,100]{1,0:T(8,128)S(1)}, f32[56,100]{1,0:T(8,128)S(1)}) custom-call(s32[3]{0:T(128)S(1)} %pad_add_fusion.info_ref, f32[112,1536]{1,0:T(8,128)S(1)} %get-tuple-element.37.residual, bf16[100,1536]{1,0:T(8,128)(2,1)S(1)} %bitcast.8, f32[5,1536]{1,0:T(8,128)S(1)} %get-tuple-element.36.mod_ref, bf16[1024,1536]{1,0:T(8,128)(2,1)S(1)} %copy-done, ...), custom_call_target="tpu_custom_call" | custom-call | tf_op jit(solution)/shard_map/pallas_call | solution.py:345
  57.5 0.1 collective-permute-start.14
  59.0 0.0 collective-permute-done.14
  59.0 0.6 %multiply_add_fusion = (f32[56,100]{1,0:T(8,128)}, f32[56,100]{1,0:T(8,128)}) fusion(f32[56,100]{1,0:T(8,128)S(1)} %copy-done.2, f32[]{:T(128)} %bitcast.5, f32[56,100]{1,0:T(8,128)S(1)} %collective-permute-done.14, f32[56,100]{1,0:T(8,128)S(1)} %get-tuple-element.60, f32[]{:T(128)} %bitcast.7, f32[56,100]{1,0:T(8,128)S(1)} %get-tuple-element.33, ...), kind=kLoop, calls=%fused_computation.4 | loop fusion | flops 56000 | bytes 156808 | tf_op jit(solution)/shard_map/add | solution.py:595
  (5 shorter events, 0.0 us)
Async XLA Ops:
  1.5 5.6 %collective-permute-start.1 = (bf16[2,16,1536]{2,1,0:T(8,128)(2,1)S(1)}, bf16[2,16,1536]{2,1,0:T(8,128)(2,1)S(1)}, u32[]{:S(2)}, u32[]{:S(2)}) collective-permute-start(bf16[2,16,1536]{2,1,0:T(8,128)(2,1)S(1)} %constant_dynamic-slice_fusion), channel_id=1, source_target_pairs={{1,2},{2,1},{3,4},{4,3},{5,6},{6,5},{7,8},{8,7},{9,10},{10,9},{11,... | collective-permute-start | bytes 294920 | tf_op jit(solution)/shard_map/ppermute | solution.py:541
  5.4 3.4 %collective-permute-start = (bf16[56,1536]{1,0:T(8,128)(2,1)S(1)}, bf16[56,1536]{1,0:T(8,128)(2,1)S(1)}, u32[]{:S(2)}, u32[]{:S(2)}) collective-permute-start(bf16[56,1536]{1,0:T(8,128)(2,1)S(1)} %dynamic-slice_bitcast_fusion), channel_id=1, source_target_pairs={{0,1},{1,0},{2,3},{3,2},{4,5},{5,4},{6,7},{7,6},{8,9},{9,8},{10,11... | collective-permute-start | bytes 516104 | tf_op jit(solution)/shard_map/ppermute | solution.py:385
  7.1 1.8 %collective-permute-start.2 = (bf16[2,16,1536]{2,1,0:T(8,128)(2,1)S(1)}, bf16[2,16,1536]{2,1,0:T(8,128)(2,1)S(1)}, u32[]{:S(2)}, u32[]{:S(2)}) collective-permute-start(bf16[2,16,1536]{2,1,0:T(8,128)(2,1)S(1)} %collective-permute-done.1.near_ref), channel_id=1, source_target_pairs={{0,1},{1,0},{2,3},{3,2},{4,5},{5,4},{6,7},{7,6},{8,9},{9,8},{10,11... | collective-permute-start | bytes 294920 | tf_op jit(solution)/shard_map/ppermute | solution.py:385
  15.1 10.6 %collective-permute-start.8 = (bf16[3,112,128]{2,1,0:T(8,128)(2,1)S(1)}, bf16[3,112,128]{2,1,0:T(8,128)(2,1)S(1)}, u32[]{:S(2)}, u32[]{:S(2)}) collective-permute-start(bf16[3,112,128]{2,1,0:T(8,128)(2,1)S(1)} %get-tuple-element.46), channel_id=1, source_target_pairs={{0,12},{1,13},{2,14},{3,15},{4,8},{5,9},{6,10},{7,11},{8,4},{9,5},... | collective-permute-start | bytes 258056 | tf_op jit(solution)/shard_map/ppermute | solution.py:385
  20.8 34.6 %copy-start = (bf16[1024,1536]{1,0:T(8,128)(2,1)S(1)}, bf16[1024,1536]{1,0:T(8,128)(2,1)}, u32[]{:S(2)}) copy-start(bf16[1024,1536]{1,0:T(8,128)(2,1)} %w_out_ref.1) | copy-start | bytes 9437188
  20.8 34.6 %copy-start.1 = (bf16[1536,100]{0,1:T(8,128)(2,1)S(1)}, bf16[1536,100]{0,1:T(8,128)(2,1)}, u32[]{:S(2)}) copy-start(bf16[1536,100]{0,1:T(8,128)(2,1)} %param.19) | copy-start | bytes 921604
  20.9 38.1 %copy-start.2 = (f32[56,100]{1,0:T(8,128)S(1)}, f32[56,100]{1,0:T(8,128)}, u32[]{:S(2)}) copy-start(f32[56,100]{1,0:T(8,128)} %param.11) | copy-start | bytes 67204
  20.9 7.6 %collective-permute-start.4 = (bf16[3,112,128]{2,1,0:T(8,128)(2,1)S(1)}, bf16[3,112,128]{2,1,0:T(8,128)(2,1)S(1)}, u32[]{:S(2)}, u32[]{:S(2)}) collective-permute-start(bf16[3,112,128]{2,1,0:T(8,128)(2,1)S(1)} %get-tuple-element.42), channel_id=1, source_target_pairs={{0,4},{1,5},{2,6},{3,7},{4,0},{5,1},{6,2},{7,3},{8,12},{9,13},{10,... | collective-permute-start | bytes 258056 | tf_op jit(solution)/shard_map/ppermute | solution.py:385
  22.1 7.4 %collective-permute-start.5 = (bf16[3,112,128]{2,1,0:T(8,128)(2,1)S(1)}, bf16[3,112,128]{2,1,0:T(8,128)(2,1)S(1)}, u32[]{:S(2)}, u32[]{:S(2)}) collective-permute-start(bf16[3,112,128]{2,1,0:T(8,128)(2,1)S(1)} %get-tuple-element.43), channel_id=1, source_target_pairs={{0,6},{1,7},{2,4},{3,5},{4,2},{5,3},{6,0},{7,1},{8,14},{9,15},{10,... | collective-permute-start | bytes 258056 | tf_op jit(solution)/shard_map/ppermute | solution.py:385
  24.1 5.4 %collective-permute-start.3 = (bf16[3,112,128]{2,1,0:T(8,128)(2,1)S(1)}, bf16[3,112,128]{2,1,0:T(8,128)(2,1)S(1)}, u32[]{:S(2)}, u32[]{:S(2)}) collective-permute-start(bf16[3,112,128]{2,1,0:T(8,128)(2,1)S(1)} %get-tuple-element.41), channel_id=1, source_target_pairs={{0,2},{1,3},{2,0},{3,1},{4,6},{5,7},{6,4},{7,5},{8,10},{9,11},{10,... | collective-permute-start | bytes 258056 | tf_op jit(solution)/shard_map/ppermute | solution.py:385
  25.7 9.3 %collective-permute-start.6 = (bf16[3,112,128]{2,1,0:T(8,128)(2,1)S(1)}, bf16[3,112,128]{2,1,0:T(8,128)(2,1)S(1)}, u32[]{:S(2)}, u32[]{:S(2)}) collective-permute-start(bf16[3,112,128]{2,1,0:T(8,128)(2,1)S(1)} %get-tuple-element.44), channel_id=1, source_target_pairs={{0,8},{1,9},{2,10},{3,11},{4,12},{5,13},{6,14},{7,15},{8,0},{9,1},... | collective-permute-start | bytes 258056 | tf_op jit(solution)/shard_map/ppermute | solution.py:385
  25.7 12.1 %collective-permute-start.7 = (bf16[3,112,128]{2,1,0:T(8,128)(2,1)S(1)}, bf16[3,112,128]{2,1,0:T(8,128)(2,1)S(1)}, u32[]{:S(2)}, u32[]{:S(2)}) collective-permute-start(bf16[3,112,128]{2,1,0:T(8,128)(2,1)S(1)} %get-tuple-element.45), channel_id=1, source_target_pairs={{0,10},{1,11},{2,8},{3,9},{4,14},{5,15},{6,12},{7,13},{8,2},{9,3},... | collective-permute-start | bytes 258056 | tf_op jit(solution)/shard_map/ppermute | solution.py:385
  28.5 11.4 %collective-permute-start.9 = (bf16[3,112,128]{2,1,0:T(8,128)(2,1)S(1)}, bf16[3,112,128]{2,1,0:T(8,128)(2,1)S(1)}, u32[]{:S(2)}, u32[]{:S(2)}) collective-permute-start(bf16[3,112,128]{2,1,0:T(8,128)(2,1)S(1)} %get-tuple-element.53), channel_id=1, source_target_pairs={{0,14},{1,15},{2,12},{3,13},{4,10},{5,11},{6,8},{7,9},{8,6},{9,7},... | collective-permute-start | bytes 258056 | tf_op jit(solution)/shard_map/ppermute | solution.py:385
  41.5 5.0 %collective-permute-start.10 = (bf16[4,112,128]{2,1,0:T(8,128)(2,1)S(1)}, bf16[4,112,128]{2,1,0:T(8,128)(2,1)S(1)}, u32[]{:S(2)}, u32[]{:S(2)}) collective-permute-start(bf16[4,112,128]{2,1,0:T(8,128)(2,1)S(1)} %get-tuple-element.56), channel_id=1, source_target_pairs={{0,2},{1,3},{2,0},{3,1},{4,6},{5,7},{6,4},{7,5},{8,10},{9,11},{10,... | collective-permute-start | bytes 344072 | tf_op jit(solution)/shard_map/ppermute | solution.py:385
  47.1 4.5 %collective-permute-start.11 = (bf16[2,112,128]{2,1,0:T(8,128)(2,1)S(1)}, bf16[2,112,128]{2,1,0:T(8,128)(2,1)S(1)}, u32[]{:S(2)}, u32[]{:S(2)}) collective-permute-start(bf16[2,112,128]{2,1,0:T(8,128)(2,1)S(1)} %get-tuple-element.57), channel_id=1, source_target_pairs={{0,4},{1,5},{2,6},{3,7},{4,0},{5,1},{6,2},{7,3},{8,12},{9,13},{10,... | collective-permute-start | bytes 172040 | tf_op jit(solution)/shard_map/ppermute | solution.py:385
  47.4 5.5 %collective-permute-start.12 = (bf16[2,112,128]{2,1,0:T(8,128)(2,1)S(1)}, bf16[2,112,128]{2,1,0:T(8,128)(2,1)S(1)}, u32[]{:S(2)}, u32[]{:S(2)}) collective-permute-start(bf16[2,112,128]{2,1,0:T(8,128)(2,1)S(1)} %get-tuple-element.58), channel_id=1, source_target_pairs={{0,8},{1,9},{2,10},{3,11},{4,12},{5,13},{6,14},{7,15},{8,0},{9,1},... | collective-permute-start | bytes 172040 | tf_op jit(solution)/shard_map/ppermute | solution.py:385
  49.5 6.0 %collective-permute-start.13 = (bf16[2,112,128]{2,1,0:T(8,128)(2,1)S(1)}, bf16[2,112,128]{2,1,0:T(8,128)(2,1)S(1)}, u32[]{:S(2)}, u32[]{:S(2)}) collective-permute-start(bf16[2,112,128]{2,1,0:T(8,128)(2,1)S(1)} %get-tuple-element.59), channel_id=1, source_target_pairs={{0,12},{1,13},{2,14},{3,15},{4,8},{5,9},{6,10},{7,11},{8,4},{9,5},... | collective-permute-start | bytes 172040 | tf_op jit(solution)/shard_map/ppermute | solution.py:385
  57.5 1.5 %collective-permute-start.14 = (f32[56,100]{1,0:T(8,128)S(1)}, f32[56,100]{1,0:T(8,128)S(1)}, u32[]{:S(2)}, u32[]{:S(2)}) collective-permute-start(f32[56,100]{1,0:T(8,128)S(1)} %get-tuple-element.61), channel_id=1, source_target_pairs={{0,1},{1,0},{2,3},{3,2},{4,5},{5,4},{6,7},{7,6},{8,9},{9,8},{10,11... | collective-permute-start | bytes 67208 | tf_op jit(solution)/shard_map/ppermute | solution.py:385

commit v4 on v3

--- a/solution.py
+++ b/solution.py
@@ -97,7 +97,7 @@
 
 
 def front_kernel(
-    firsts, info_ref, own_ref, partner_ref, near_ref, far_ref, taps_ref, mod_ref, cos_ref, sin_ref,
+    first_pair, info_ref, own_ref, partner_ref, near_ref, far_ref, taps_ref, mod_ref, cos_ref, sin_ref,
     weight_hbm, residual_ref, normed_ref, weight_ref, *refs,
 ):
     *out_refs, padded, sems = refs
@@ -105,7 +105,7 @@
     halo = near_ref.shape[1]
     total_rows = 2 * rows
     tiles = width // LANES
-    parts = 8
+    parts = sems.shape[0]
     depth = width // parts
     loads = []
     for part in range(parts):
@@ -153,47 +153,72 @@
         normed_ref[:, lanes] = value.astype(jnp.bfloat16)
 
     row_norm(lambda tile: residual_ref[:, tile_lanes(tile)], store, tiles, mod_ref, 0, total)
-    for load in loads:
-        load.wait()
-    chip = info_ref[CHIP]
-    project_pairs(firsts, chip, normed_ref, weight_ref, cos_ref, sin_ref, out_refs)
-
-
-def project_pairs(firsts, chip, normed_ref, weight_ref, cos_ref, sin_ref, out_refs):
-    rows = normed_ref.shape[0]
-    attn = weight_ref.shape[1] // 3
+    if first_pair is None:
+        for load in loads:
+            load.wait()
+    else:
+        project_landing(
+            first_pair, info_ref[CHIP], loads, normed_ref, weight_ref, cos_ref, sin_ref, out_refs
+        )
+
+
+def pair_lanes(chip, apart, part, attn):
     wide = 2 * LANES
+    start = part * attn + ((chip ^ apart) >> 1) * wide
+    return pl.ds(pl.multiple_of(start, wide), wide)
+
+
+def store_pair(products, chip, cos_ref, sin_ref, out_refs):
+    rows = cos_ref.shape[0]
     half = HEAD_DIM // 2
     cosine, sine = cos_ref[...], sin_ref[...]
     lower = lax.broadcasted_iota(jnp.int32, (rows, LANES), 1) % HEAD_DIM < half
     swap = jnp.full((rows, LANES), chip & 1, jnp.int32) > 0
-    for at, apart in enumerate(firsts):
-        pair = (chip ^ apart) >> 1
+    for part, both in enumerate(products):
+        sides = []
+        for side in range(2):
+            value = both[:, side * LANES : (side + 1) * LANES]
+            if part < 2:
+                swapped = jnp.where(
+                    lower, pltpu.roll(value, LANES - half, 1), pltpu.roll(value, half, 1)
+                )
+                value = value * cosine + swapped * sine
+            if part == 0:
+                value = value * HEAD_DIM**-0.5
+            sides.append(value)
+        out_refs[0][part] = jnp.where(swap, sides[1], sides[0]).astype(jnp.bfloat16)
+        out_refs[1][part] = jnp.where(swap, sides[0], sides[1]).astype(jnp.bfloat16)
+
+
+def project_landing(apart, chip, loads, normed_ref, weight_ref, cos_ref, sin_ref, out_refs):
+    depth = weight_ref.shape[0] // len(loads)
+    attn = weight_ref.shape[1] // 3
+    products = [jnp.zeros((normed_ref.shape[0], 2 * LANES), jnp.float32)] * 3
+    for at, load in enumerate(loads):
+        load.wait()
+        here = slice(at * depth, (at + 1) * depth)
         for part in range(3):
-            start = part * attn + pair * wide
-            both = jnp.dot(
-                normed_ref[...],
-                weight_ref[:, pl.ds(pl.multiple_of(start, wide), wide)],
+            products[part] = products[part] + jnp.dot(
+                normed_ref[:, here],
+                weight_ref[here, pair_lanes(chip, apart, part, attn)],
                 preferred_element_type=jnp.float32,
             )
-            sides = []
-            for side in range(2):
-                value = both[:, side * LANES : (side + 1) * LANES]
-                if part < 2:
-                    swapped = jnp.where(
-                        lower, pltpu.roll(value, LANES - half, 1), pltpu.roll(value, half, 1)
-                    )
-                    value = value * cosine + swapped * sine
-                if part == 0:
-                    value = value * HEAD_DIM**-0.5
-                sides.append(value)
-            out_refs[2 * at][part] = jnp.where(swap, sides[1], sides[0]).astype(jnp.bfloat16)
-            out_refs[2 * at + 1][part] = jnp.where(swap, sides[0], sides[1]).astype(jnp.bfloat16)
+    store_pair(products, chip, cos_ref, sin_ref, out_refs)
 
 
 def project_kernel(firsts, origin, info_ref, normed_ref, weight_ref, cos_ref, sin_ref, *out_refs):
     chip = info_ref[CHIP] if origin is None else origin
-    project_pairs(firsts, chip, normed_ref, weight_ref, cos_ref, sin_ref, out_refs)
+    attn = weight_ref.shape[1] // 3
+    for at, apart in enumerate(firsts):
+        products = [
+            jnp.dot(
+                normed_ref[...],
+                weight_ref[:, pair_lanes(chip, apart, part, attn)],
+                preferred_element_type=jnp.float32,
+            )
+            for part in range(3)
+        ]
+        store_pair(products, chip, cos_ref, sin_ref, out_refs[2 * at : 2 * at + 2])
 
 
 def place_keys(info_ref, apart, got_ref, keys, values, first):
@@ -555,18 +580,21 @@
         hbm=(1, 2, 3),
     )
     tables = rotary_tables(chip * chip_rows + jnp.arange(chip_rows, dtype=jnp.int32))
-    firsts = tuple(send_order(chips)[:1]) if chips_hold_groups(count) else ()
+    first_pair = send_order(chips)[0] if chips_hold_groups(count) else None
     group = array((3, chip_rows, LANES), jnp.bfloat16)
     residual, normed, weight, *made = call(
-        functools.partial(front_kernel, firsts),
+        functools.partial(front_kernel, first_pair),
         (
             array((chip_rows, width)),
             array((chip_rows, width), jnp.bfloat16),
             array(w_qkv.shape, jnp.bfloat16),
         )
-        + (group,) * (2 * len(firsts)),
+        + (group,) * (0 if first_pair is None else 2),
         (info, own, partner, near, far, taps, mods) + tables + (w_qkv,),
-        [VMEM((chip_rows + 2 * HALO, LANES), jnp.float32), pltpu.SemaphoreType.DMA((8,))],
+        [
+            VMEM((chip_rows + 2 * HALO, LANES), jnp.float32),
+            pltpu.SemaphoreType.DMA((width // (2 * LANES),)),
+        ],
         hbm=(9,),
     )
     if chips_hold_groups(count):

time: 59.9 us -> 59.6 us (level)
  no operation moved by 1% of the time
where the time goes in v4:
time: 59.6 us; the launch traced here: 59.4 us
  starting transfers between devices  21.2 us (36%)
  Pallas kernels  18.4 us (31%)
  waiting for transfers between devices  14 us (23%)
  between operations  2.83 us (5%)
  local copies, waits for them, and re-layouts  1.86 us (3%)
  other arithmetic  1.01 us (2%)
    pallas_call x10, Pallas kernels, call(): pl.pallas_call(kernel, out_shape=out_shape, in_specs=[smem_spec()] + spec...  18.4 us
    ppermute x14, starting transfers between devices, across(): return lax.ppermute(value, 'seq', [(i, i ^ apart) for i in range(count)])  18.3 us
    ppermute x14, waiting for transfers between devices, across(): return lax.ppermute(value, 'seq', [(i, i ^ apart) for i in range(count)])  13.5 us
    ppermute x1, starting transfers between devices, per_device(): lax.ppermute(edges, ('clip', 'seq'), facing_pairs(lax.axis_size('clip'),...  2.97 us
  transfers between devices with their start and end apart: 15, of which 7 were waited for; matrix products, arithmetic and copies ran while one was open for 2% of the time, Pallas kernels for 14%

profile of v4, /device:TPU:0, one launch (start us, length us, event | category | flops | bytes accessed | tf_op | source)
XLA Modules:
  0.0 59.4 jit_solution(15751124375660368993)
XLA Ops:
  0.6 0.9 %constant_dynamic-slice_fusion = bf16[2,16,1536]{2,1,0:T(8,128)(2,1)S(1)} fusion(bf16[2,56,1536]{2,1,0:T(8,128)(2,1)} %hidden_hbm.1, s32[]{:T(128)S(6)} %select_n.45), kind=kLoop, calls=%fused_computation.15 | loop fusion | bytes 196612 | tf_op jit(solution)/shard_map/dynamic_slice | solution.py:564
  1.5 3.0 %collective-permute-start.1 = (bf16[2,16,1536]{2,1,0:T(8,128)(2,1)S(1)}, bf16[2,16,1536]{2,1,0:T(8,128)(2,1)S(1)}, u32[]{:S(2)}, u32[]{:S(2)}) collective-permute-start(bf16[2,16,1536]{2,1,0:T(8,128)(2,1)S(1)} %constant_dynamic-slice_fusion), channel_id=1, source_target_pairs={{1,2},{2,1},{3,4},{4,3},{5,6},{6,5},{7,8},{8,7},{9,10},{10,9},{11,... | collective-permute-start | bytes 294920 | tf_op jit(solution)/shard_map/ppermute | solution.py:566
  4.5 0.9 %dynamic-slice_bitcast_fusion = bf16[56,1536]{1,0:T(8,128)(2,1)S(1)} fusion(bf16[2,56,1536]{2,1,0:T(8,128)(2,1)} %hidden_hbm.1, s32[]{:T(128)S(6)} %select_n.44), kind=kLoop, calls=%fused_computation | loop fusion | bytes 344068 | tf_op jit(solution)/shard_map/squeeze | solution.py:565
  5.4 0.2 collective-permute-start
  5.7 0.3 fusion
  6.6 0.5 collective-permute-done.1.near_ref
  7.1 0.1 collective-permute-start.2
  7.2 0.1 pad_add_fusion.info_ref
  7.3 1.6 %shard_map.113 = (bf16[56,1536]{1,0:T(8,128)(2,1)S(1)}, f32[31,1536]{1,0:T(8,128)S(1)}, f32[5,1536]{1,0:T(8,128)S(1)}, f32[56,100]{1,0:T(8,128)S(1)}, f32[56,100]{1,0:T(8,128)S(1)}) custom-call(s32[3]{0:T(128)S(1)} %pad_add_fusion.info_ref, bf16[2,56,1536]{2,1,0:T(8,128)(2,1)} %hidden_hbm.1, f32[31,1536]{1,0:T(8,128)} %taps_hbm.1, f32[5,1536]{1,0:T(8,128)} %mod_hbm.1), custom_call_target="tpu_custom_call" | custom-call | tf_op jit(solution)/shard_map/pallas_call | solution.py:370
  8.9 0.0 collective-permute-done.partner_ref
  8.9 0.0 collective-permute-done.2.far_ref
  8.9 4.7 %shard_map.114 = (f32[112,1536]{1,0:T(8,128)S(1)}, bf16[112,1536]{1,0:T(8,128)(2,1)S(1)}, bf16[1536,3072]{1,0:T(8,128)(2,1)S(1)}, bf16[3,112,128]{2,1,0:T(8,128)(2,1)S(1)}, bf16[3,112,128]{2,1,0:T(8,128)(2,1)S(1)}) custom-call(s32[3]{0:T(128)S(1)} %pad_add_fusion.info_ref, bf16[56,1536]{1,0:T(8,128)(2,1)S(1)} %get-tuple-element.34.own_ref, ...), custom_call_target="tpu_custom_call" | custom-call | tf_op jit(solution)/shard_map/pallas_call | solution.py:370
  13.6 1.2 %shard_map.117 = (bf16[3,112,128]{2,1,0:T(8,128)(2,1)S(1)}, bf16[3,112,128]{2,1,0:T(8,128)(2,1)S(1)}) custom-call(s32[3]{0:T(128)S(1)} %pad_add_fusion.info_ref, bf16[112,1536]{1,0:T(8,128)(2,1)S(1)} %get-tuple-element.38.normed_ref, bf16[1536,3072]{1,0:T(8,128)(2,1)S(1)} %get-tuple-element.39.weight_ref, f32[112,128]{1,0:T(8,128)S(1)} %get-tuple-element.65.cos_ref, ...), custom_call_target="tpu_custom_call" | custom-call | tf_op jit(solution)/shard_map/pallas_call | solution.py:370
  14.8 4.5 %collective-permute-start.8 = (bf16[3,112,128]{2,1,0:T(8,128)(2,1)S(1)}, bf16[3,112,128]{2,1,0:T(8,128)(2,1)S(1)}, u32[]{:S(2)}, u32[]{:S(2)}) collective-permute-start(bf16[3,112,128]{2,1,0:T(8,128)(2,1)S(1)} %get-tuple-element.46), channel_id=1, source_target_pairs={{0,12},{1,13},{2,14},{3,15},{4,8},{5,9},{6,10},{7,11},{8,4},{9,5},... | collective-permute-start | bytes 258056 | tf_op jit(solution)/shard_map/ppermute | solution.py:410
  19.3 1.2 %shard_map.116 = (bf16[3,112,128]{2,1,0:T(8,128)(2,1)S(1)}, bf16[3,112,128]{2,1,0:T(8,128)(2,1)S(1)}) custom-call(s32[3]{0:T(128)S(1)} %pad_add_fusion.info_ref, bf16[112,1536]{1,0:T(8,128)(2,1)S(1)} %get-tuple-element.38.normed_ref, bf16[1536,3072]{1,0:T(8,128)(2,1)S(1)} %get-tuple-element.39.weight_ref, f32[112,128]{1,0:T(8,128)S(1)} %get-tuple-element.65.cos_ref, ...), custom_call_target="tpu_custom_call" | custom-call | tf_op jit(solution)/shard_map/pallas_call | solution.py:370
  20.5 0.0 copy-start
  20.6 0.0 copy-start.1
  20.6 0.0 copy-start.2
  20.6 0.1 collective-permute-start.4
  20.7 1.2 %shard_map.115 = (bf16[3,112,128]{2,1,0:T(8,128)(2,1)S(1)}, bf16[3,112,128]{2,1,0:T(8,128)(2,1)S(1)}) custom-call(s32[3]{0:T(128)S(1)} %pad_add_fusion.info_ref, bf16[112,1536]{1,0:T(8,128)(2,1)S(1)} %get-tuple-element.38.normed_ref, bf16[1536,3072]{1,0:T(8,128)(2,1)S(1)} %get-tuple-element.39.weight_ref, f32[112,128]{1,0:T(8,128)S(1)} %get-tuple-element.65.cos_ref, ...), custom_call_target="tpu_custom_call" | custom-call | tf_op jit(solution)/shard_map/pallas_call | solution.py:370
  21.8 2.0 %collective-permute-start.5 = (bf16[3,112,128]{2,1,0:T(8,128)(2,1)S(1)}, bf16[3,112,128]{2,1,0:T(8,128)(2,1)S(1)}, u32[]{:S(2)}, u32[]{:S(2)}) collective-permute-start(bf16[3,112,128]{2,1,0:T(8,128)(2,1)S(1)} %get-tuple-element.43), channel_id=1, source_target_pairs={{0,6},{1,7},{2,4},{3,5},{4,2},{5,3},{6,0},{7,1},{8,14},{9,15},{10,... | collective-permute-start | bytes 258056 | tf_op jit(solution)/shard_map/ppermute | solution.py:410
  23.8 1.6 %collective-permute-start.3 = (bf16[3,112,128]{2,1,0:T(8,128)(2,1)S(1)}, bf16[3,112,128]{2,1,0:T(8,128)(2,1)S(1)}, u32[]{:S(2)}, u32[]{:S(2)}) collective-permute-start(bf16[3,112,128]{2,1,0:T(8,128)(2,1)S(1)} %get-tuple-element.41), channel_id=1, source_target_pairs={{0,2},{1,3},{2,0},{3,1},{4,6},{5,7},{6,4},{7,5},{8,10},{9,11},{10,... | collective-permute-start | bytes 258056 | tf_op jit(solution)/shard_map/ppermute | solution.py:410
  25.4 0.0 collective-permute-start.6
  25.4 0.0 collective-permute-done.8.refs_6_.refs_3_
  25.4 2.8 %collective-permute-start.7 = (bf16[3,112,128]{2,1,0:T(8,128)(2,1)S(1)}, bf16[3,112,128]{2,1,0:T(8,128)(2,1)S(1)}, u32[]{:S(2)}, u32[]{:S(2)}) collective-permute-start(bf16[3,112,128]{2,1,0:T(8,128)(2,1)S(1)} %get-tuple-element.45), channel_id=1, source_target_pairs={{0,10},{1,11},{2,8},{3,9},{4,14},{5,15},{6,12},{7,13},{8,2},{9,3},... | collective-permute-start | bytes 258056 | tf_op jit(solution)/shard_map/ppermute | solution.py:410
  28.2 0.0 collective-permute-done.4.refs_2_.refs_1_
  28.2 1.0 %collective-permute-start.9 = (bf16[3,112,128]{2,1,0:T(8,128)(2,1)S(1)}, bf16[3,112,128]{2,1,0:T(8,128)(2,1)S(1)}, u32[]{:S(2)}, u32[]{:S(2)}) collective-permute-start(bf16[3,112,128]{2,1,0:T(8,128)(2,1)S(1)} %get-tuple-element.53), channel_id=1, source_target_pairs={{0,14},{1,15},{2,12},{3,13},{4,10},{5,11},{6,8},{7,9},{8,6},{9,7},... | collective-permute-start | bytes 258056 | tf_op jit(solution)/shard_map/ppermute | solution.py:410
  29.2 0.0 collective-permute-done.5.refs_3_
  29.2 0.1 collective-permute-done.3.refs_1_
  29.2 5.4 %collective-permute-done.6.refs_4_.refs_2_ = bf16[3,112,128]{2,1,0:T(8,128)(2,1)S(1)} collective-permute-done((bf16[3,112,128]{2,1,0:T(8,128)(2,1)S(1)}, bf16[3,112,128]{2,1,0:T(8,128)(2,1)S(1)}, u32[]{:S(2)}, u32[]{:S(2)}) %collective-permute-start.6) | collective-permute-done | bytes 86048 | tf_op jit(solution)/shard_map/ppermute | solution.py:410
  34.7 2.8 %collective-permute-done.7.refs_5_ = bf16[3,112,128]{2,1,0:T(8,128)(2,1)S(1)} collective-permute-done((bf16[3,112,128]{2,1,0:T(8,128)(2,1)S(1)}, bf16[3,112,128]{2,1,0:T(8,128)(2,1)S(1)}, u32[]{:S(2)}, u32[]{:S(2)}) %collective-permute-start.7) | collective-permute-done | bytes 86048 | tf_op jit(solution)/shard_map/ppermute | solution.py:410
  37.5 2.2 %shard_map.118 = (bf16[784,256]{1,0:T(8,128)(2,1)S(1)}, bf16[784,128]{1,0:T(8,128)(2,1)S(1)}, bf16[672,256]{1,0:T(8,128)(2,1)S(1)}, f32[672,128]{1,0:T(8,128)S(1...) custom-call(s32[3]{0:T(128)S(1)} %pad_add_fusion.info_ref, bf16[3,112,128]{2,1,0:T(8,128)(2,1)S(1)} %get-tuple-element.40.refs_0_, ...), custom_call_target="tpu_custom_call" | custom-call | tf_op jit(solution)/shard_map/pallas_call | solution.py:370
  39.7 0.0 collective-permute-done.9.last_ref
  39.7 1.5 %shard_map.119 = (bf16[4,112,128]{2,1,0:T(8,128)(2,1)S(1)}, bf16[896,256]{1,0:T(8,128)(2,1)S(1)}, bf16[896,128]{1,0:T(8,128)(2,1)S(1)}) custom-call(s32[3]{0:T(128)S(1)} %pad_add_fusion.info_ref, bf16[784,256]{1,0:T(8,128)(2,1)S(1)} %get-tuple-element.47.early_keys, bf16[784,128]{1,0:T(8,128)(2,1)S(1)} %get-tuple-element.48.early_values, ...), custom_call_target="tpu_custom_call" | custom-call | tf_op jit(solution)/shard_map/pallas_call | solution.py:370
  41.2 1.5 %collective-permute-start.10 = (bf16[4,112,128]{2,1,0:T(8,128)(2,1)S(1)}, bf16[4,112,128]{2,1,0:T(8,128)(2,1)S(1)}, u32[]{:S(2)}, u32[]{:S(2)}) collective-permute-start(bf16[4,112,128]{2,1,0:T(8,128)(2,1)S(1)} %get-tuple-element.56), channel_id=1, source_target_pairs={{0,2},{1,3},{2,0},{3,1},{4,6},{5,7},{6,4},{7,5},{8,10},{9,11},{10,... | collective-permute-start | bytes 344072 | tf_op jit(solution)/shard_map/ppermute | solution.py:410
  42.7 2.3 %shard_map.120.own_ref.refs_0_ = bf16[4,112,128]{2,1,0:T(8,128)(2,1)S(1)} custom-call(s32[3]{0:T(128)S(1)} %pad_add_fusion.info_ref, bf16[896,256]{1,0:T(8,128)(2,1)S(1)} %get-tuple-element.54.keys, bf16[896,128]{1,0:T(8,128)(2,1)S(1)} %get-tuple-element.55.values, bf16[3,112,128]{2,1,0:T(8,128)(2,1)S(1)} %get-tuple-element.40.refs_0_, ...), custom_call_target="tpu_custom_call" | custom-call | tf_op jit(solution)/shard_map/pallas_call | solution.py:370
  45.0 1.2 %collective-permute-done.10.got_ref.refs_1_ = bf16[4,112,128]{2,1,0:T(8,128)(2,1)S(1)} collective-permute-done((bf16[4,112,128]{2,1,0:T(8,128)(2,1)S(1)}, bf16[4,112,128]{2,1,0:T(8,128)(2,1)S(1)}, u32[]{:S(2)}, u32[]{:S(2)}) %collective-permute-start.10) | collective-permute-done | bytes 114720 | tf_op jit(solution)/shard_map/ppermute | solution.py:410
  46.3 0.6 shard_map.121
  46.8 0.3 collective-permute-start.11
  47.1 2.1 %collective-permute-start.12 = (bf16[2,112,128]{2,1,0:T(8,128)(2,1)S(1)}, bf16[2,112,128]{2,1,0:T(8,128)(2,1)S(1)}, u32[]{:S(2)}, u32[]{:S(2)}) collective-permute-start(bf16[2,112,128]{2,1,0:T(8,128)(2,1)S(1)} %get-tuple-element.58), channel_id=1, source_target_pairs={{0,8},{1,9},{2,10},{3,11},{4,12},{5,13},{6,14},{7,15},{8,0},{9,1},... | collective-permute-start | bytes 172040 | tf_op jit(solution)/shard_map/ppermute | solution.py:410
  49.2 2.1 %collective-permute-start.13 = (bf16[2,112,128]{2,1,0:T(8,128)(2,1)S(1)}, bf16[2,112,128]{2,1,0:T(8,128)(2,1)S(1)}, u32[]{:S(2)}, u32[]{:S(2)}) collective-permute-start(bf16[2,112,128]{2,1,0:T(8,128)(2,1)S(1)} %get-tuple-element.59), channel_id=1, source_target_pairs={{0,12},{1,13},{2,14},{3,15},{4,8},{5,9},{6,10},{7,11},{8,4},{9,5},... | collective-permute-start | bytes 172040 | tf_op jit(solution)/shard_map/ppermute | solution.py:410
  51.3 0.0 collective-permute-done.11.refs_2_
  51.3 1.4 %collective-permute-done.12.refs_3_ = bf16[2,112,128]{2,1,0:T(8,128)(2,1)S(1)} collective-permute-done((bf16[2,112,128]{2,1,0:T(8,128)(2,1)S(1)}, bf16[2,112,128]{2,1,0:T(8,128)(2,1)S(1)}, u32[]{:S(2)}, u32[]{:S(2)}) %collective-permute-start.12) | collective-permute-done | bytes 57376 | tf_op jit(solution)/shard_map/ppermute | solution.py:410
  52.7 2.5 %collective-permute-done.13.refs_4_ = bf16[2,112,128]{2,1,0:T(8,128)(2,1)S(1)} collective-permute-done((bf16[2,112,128]{2,1,0:T(8,128)(2,1)S(1)}, bf16[2,112,128]{2,1,0:T(8,128)(2,1)S(1)}, u32[]{:S(2)}, u32[]{:S(2)}) %collective-permute-start.13) | collective-permute-done | bytes 57376 | tf_op jit(solution)/shard_map/ppermute | solution.py:410
  55.2 2.0 %shard_map.122 = (f32[56,100]{1,0:T(8,128)S(1)}, f32[56,100]{1,0:T(8,128)S(1)}) custom-call(s32[3]{0:T(128)S(1)} %pad_add_fusion.info_ref, f32[112,1536]{1,0:T(8,128)S(1)} %get-tuple-element.37.residual, bf16[100,1536]{1,0:T(8,128)(2,1)S(1)} %bitcast.8, f32[5,1536]{1,0:T(8,128)S(1)} %get-tuple-element.36.mod_ref, bf16[1024,1536]{1,0:T(8,128)(2,1)S(1)} %copy-done, ...), custom_call_target="tpu_custom_call" | custom-call | tf_op jit(solution)/shard_map/pallas_call | solution.py:370
  57.2 0.1 collective-permute-start.14
  58.7 0.0 collective-permute-done.14
  58.7 0.6 %multiply_add_fusion = (f32[56,100]{1,0:T(8,128)}, f32[56,100]{1,0:T(8,128)}) fusion(f32[56,100]{1,0:T(8,128)S(1)} %copy-done.2, f32[]{:T(128)} %bitcast.5, f32[56,100]{1,0:T(8,128)S(1)} %collective-permute-done.14, f32[56,100]{1,0:T(8,128)S(1)} %get-tuple-element.60, f32[]{:T(128)} %bitcast.7, f32[56,100]{1,0:T(8,128)S(1)} %get-tuple-element.33, ...), kind=kLoop, calls=%fused_computation.4 | loop fusion | flops 56000 | bytes 156808 | tf_op jit(solution)/shard_map/add | solution.py:623
  (5 shorter events, 0.0 us)
Async XLA Ops:
  1.5 5.6 %collective-permute-start.1 = (bf16[2,16,1536]{2,1,0:T(8,128)(2,1)S(1)}, bf16[2,16,1536]{2,1,0:T(8,128)(2,1)S(1)}, u32[]{:S(2)}, u32[]{:S(2)}) collective-permute-start(bf16[2,16,1536]{2,1,0:T(8,128)(2,1)S(1)} %constant_dynamic-slice_fusion), channel_id=1, source_target_pairs={{1,2},{2,1},{3,4},{4,3},{5,6},{6,5},{7,8},{8,7},{9,10},{10,9},{11,... | collective-permute-start | bytes 294920 | tf_op jit(solution)/shard_map/ppermute | solution.py:566
  5.4 3.4 %collective-permute-start = (bf16[56,1536]{1,0:T(8,128)(2,1)S(1)}, bf16[56,1536]{1,0:T(8,128)(2,1)S(1)}, u32[]{:S(2)}, u32[]{:S(2)}) collective-permute-start(bf16[56,1536]{1,0:T(8,128)(2,1)S(1)} %dynamic-slice_bitcast_fusion), channel_id=1, source_target_pairs={{0,1},{1,0},{2,3},{3,2},{4,5},{5,4},{6,7},{7,6},{8,9},{9,8},{10,11... | collective-permute-start | bytes 516104 | tf_op jit(solution)/shard_map/ppermute | solution.py:410
  7.1 1.8 %collective-permute-start.2 = (bf16[2,16,1536]{2,1,0:T(8,128)(2,1)S(1)}, bf16[2,16,1536]{2,1,0:T(8,128)(2,1)S(1)}, u32[]{:S(2)}, u32[]{:S(2)}) collective-permute-start(bf16[2,16,1536]{2,1,0:T(8,128)(2,1)S(1)} %collective-permute-done.1.near_ref), channel_id=1, source_target_pairs={{0,1},{1,0},{2,3},{3,2},{4,5},{5,4},{6,7},{7,6},{8,9},{9,8},{10,11... | collective-permute-start | bytes 294920 | tf_op jit(solution)/shard_map/ppermute | solution.py:410
  14.8 10.6 %collective-permute-start.8 = (bf16[3,112,128]{2,1,0:T(8,128)(2,1)S(1)}, bf16[3,112,128]{2,1,0:T(8,128)(2,1)S(1)}, u32[]{:S(2)}, u32[]{:S(2)}) collective-permute-start(bf16[3,112,128]{2,1,0:T(8,128)(2,1)S(1)} %get-tuple-element.46), channel_id=1, source_target_pairs={{0,12},{1,13},{2,14},{3,15},{4,8},{5,9},{6,10},{7,11},{8,4},{9,5},... | collective-permute-start | bytes 258056 | tf_op jit(solution)/shard_map/ppermute | solution.py:410
  20.5 34.7 %copy-start = (bf16[1024,1536]{1,0:T(8,128)(2,1)S(1)}, bf16[1024,1536]{1,0:T(8,128)(2,1)}, u32[]{:S(2)}) copy-start(bf16[1024,1536]{1,0:T(8,128)(2,1)} %w_out_ref.1) | copy-start | bytes 9437188
  20.6 34.6 %copy-start.1 = (bf16[1536,100]{0,1:T(8,128)(2,1)S(1)}, bf16[1536,100]{0,1:T(8,128)(2,1)}, u32[]{:S(2)}) copy-start(bf16[1536,100]{0,1:T(8,128)(2,1)} %param.19) | copy-start | bytes 921604
  20.6 38.1 %copy-start.2 = (f32[56,100]{1,0:T(8,128)S(1)}, f32[56,100]{1,0:T(8,128)}, u32[]{:S(2)}) copy-start(f32[56,100]{1,0:T(8,128)} %param.11) | copy-start | bytes 67204
  20.6 7.7 %collective-permute-start.4 = (bf16[3,112,128]{2,1,0:T(8,128)(2,1)S(1)}, bf16[3,112,128]{2,1,0:T(8,128)(2,1)S(1)}, u32[]{:S(2)}, u32[]{:S(2)}) collective-permute-start(bf16[3,112,128]{2,1,0:T(8,128)(2,1)S(1)} %get-tuple-element.42), channel_id=1, source_target_pairs={{0,4},{1,5},{2,6},{3,7},{4,0},{5,1},{6,2},{7,3},{8,12},{9,13},{10,... | collective-permute-start | bytes 258056 | tf_op jit(solution)/shard_map/ppermute | solution.py:410
  21.8 7.4 %collective-permute-start.5 = (bf16[3,112,128]{2,1,0:T(8,128)(2,1)S(1)}, bf16[3,112,128]{2,1,0:T(8,128)(2,1)S(1)}, u32[]{:S(2)}, u32[]{:S(2)}) collective-permute-start(bf16[3,112,128]{2,1,0:T(8,128)(2,1)S(1)} %get-tuple-element.43), channel_id=1, source_target_pairs={{0,6},{1,7},{2,4},{3,5},{4,2},{5,3},{6,0},{7,1},{8,14},{9,15},{10,... | collective-permute-start | bytes 258056 | tf_op jit(solution)/shard_map/ppermute | solution.py:410
  23.8 5.4 %collective-permute-start.3 = (bf16[3,112,128]{2,1,0:T(8,128)(2,1)S(1)}, bf16[3,112,128]{2,1,0:T(8,128)(2,1)S(1)}, u32[]{:S(2)}, u32[]{:S(2)}) collective-permute-start(bf16[3,112,128]{2,1,0:T(8,128)(2,1)S(1)} %get-tuple-element.41), channel_id=1, source_target_pairs={{0,2},{1,3},{2,0},{3,1},{4,6},{5,7},{6,4},{7,5},{8,10},{9,11},{10,... | collective-permute-start | bytes 258056 | tf_op jit(solution)/shard_map/ppermute | solution.py:410
  25.4 9.3 %collective-permute-start.6 = (bf16[3,112,128]{2,1,0:T(8,128)(2,1)S(1)}, bf16[3,112,128]{2,1,0:T(8,128)(2,1)S(1)}, u32[]{:S(2)}, u32[]{:S(2)}) collective-permute-start(bf16[3,112,128]{2,1,0:T(8,128)(2,1)S(1)} %get-tuple-element.44), channel_id=1, source_target_pairs={{0,8},{1,9},{2,10},{3,11},{4,12},{5,13},{6,14},{7,15},{8,0},{9,1},... | collective-permute-start | bytes 258056 | tf_op jit(solution)/shard_map/ppermute | solution.py:410
  25.4 12.1 %collective-permute-start.7 = (bf16[3,112,128]{2,1,0:T(8,128)(2,1)S(1)}, bf16[3,112,128]{2,1,0:T(8,128)(2,1)S(1)}, u32[]{:S(2)}, u32[]{:S(2)}) collective-permute-start(bf16[3,112,128]{2,1,0:T(8,128)(2,1)S(1)} %get-tuple-element.45), channel_id=1, source_target_pairs={{0,10},{1,11},{2,8},{3,9},{4,14},{5,15},{6,12},{7,13},{8,2},{9,3},... | collective-permute-start | bytes 258056 | tf_op jit(solution)/shard_map/ppermute | solution.py:410
  28.2 11.5 %collective-permute-start.9 = (bf16[3,112,128]{2,1,0:T(8,128)(2,1)S(1)}, bf16[3,112,128]{2,1,0:T(8,128)(2,1)S(1)}, u32[]{:S(2)}, u32[]{:S(2)}) collective-permute-start(bf16[3,112,128]{2,1,0:T(8,128)(2,1)S(1)} %get-tuple-element.53), channel_id=1, source_target_pairs={{0,14},{1,15},{2,12},{3,13},{4,10},{5,11},{6,8},{7,9},{8,6},{9,7},... | collective-permute-start | bytes 258056 | tf_op jit(solution)/shard_map/ppermute | solution.py:410
  41.2 5.0 %collective-permute-start.10 = (bf16[4,112,128]{2,1,0:T(8,128)(2,1)S(1)}, bf16[4,112,128]{2,1,0:T(8,128)(2,1)S(1)}, u32[]{:S(2)}, u32[]{:S(2)}) collective-permute-start(bf16[4,112,128]{2,1,0:T(8,128)(2,1)S(1)} %get-tuple-element.56), channel_id=1, source_target_pairs={{0,2},{1,3},{2,0},{3,1},{4,6},{5,7},{6,4},{7,5},{8,10},{9,11},{10,... | collective-permute-start | bytes 344072 | tf_op jit(solution)/shard_map/ppermute | solution.py:410
  46.8 4.5 %collective-permute-start.11 = (bf16[2,112,128]{2,1,0:T(8,128)(2,1)S(1)}, bf16[2,112,128]{2,1,0:T(8,128)(2,1)S(1)}, u32[]{:S(2)}, u32[]{:S(2)}) collective-permute-start(bf16[2,112,128]{2,1,0:T(8,128)(2,1)S(1)} %get-tuple-element.57), channel_id=1, source_target_pairs={{0,4},{1,5},{2,6},{3,7},{4,0},{5,1},{6,2},{7,3},{8,12},{9,13},{10,... | collective-permute-start | bytes 172040 | tf_op jit(solution)/shard_map/ppermute | solution.py:410
  47.1 5.6 %collective-permute-start.12 = (bf16[2,112,128]{2,1,0:T(8,128)(2,1)S(1)}, bf16[2,112,128]{2,1,0:T(8,128)(2,1)S(1)}, u32[]{:S(2)}, u32[]{:S(2)}) collective-permute-start(bf16[2,112,128]{2,1,0:T(8,128)(2,1)S(1)} %get-tuple-element.58), channel_id=1, source_target_pairs={{0,8},{1,9},{2,10},{3,11},{4,12},{5,13},{6,14},{7,15},{8,0},{9,1},... | collective-permute-start | bytes 172040 | tf_op jit(solution)/shard_map/ppermute | solution.py:410
  49.2 6.0 %collective-permute-start.13 = (bf16[2,112,128]{2,1,0:T(8,128)(2,1)S(1)}, bf16[2,112,128]{2,1,0:T(8,128)(2,1)S(1)}, u32[]{:S(2)}, u32[]{:S(2)}) collective-permute-start(bf16[2,112,128]{2,1,0:T(8,128)(2,1)S(1)} %get-tuple-element.59), channel_id=1, source_target_pairs={{0,12},{1,13},{2,14},{3,15},{4,8},{5,9},{6,10},{7,11},{8,4},{9,5},... | collective-permute-start | bytes 172040 | tf_op jit(solution)/shard_map/ppermute | solution.py:410
  57.2 1.5 %collective-permute-start.14 = (f32[56,100]{1,0:T(8,128)S(1)}, f32[56,100]{1,0:T(8,128)S(1)}, u32[]{:S(2)}, u32[]{:S(2)}) collective-permute-start(f32[56,100]{1,0:T(8,128)S(1)} %get-tuple-element.61), channel_id=1, source_target_pairs={{0,1},{1,0},{2,3},{3,2},{4,5},{5,4},{6,7},{7,6},{8,9},{9,8},{10,11... | collective-permute-start | bytes 67208 | tf_op jit(solution)/shard_map/ppermute | solution.py:410

commit v5 on v4

--- a/solution.py
+++ b/solution.py
@@ -233,16 +233,17 @@
     values[here, :] = got_ref[2]
 
 
-def place_queries(query_refs, queries):
+def place_queries(query_refs, queries, first=0):
     _, rows, _ = query_refs[0].shape
     low = lax.broadcasted_iota(jnp.int32, (rows, LANES), 1) < HEAD_DIM
     zero = jnp.zeros((rows, LANES), jnp.bfloat16)
-    queries[:, LANES:] = jnp.where(
-        lax.broadcasted_iota(jnp.int32, (queries.shape[0], LANES), 1) == 0, 1.0, 0.0
+    one = jnp.where(
+        lax.broadcasted_iota(jnp.int32, (2 * rows, LANES), 1) == 0, 1.0, 0.0
     ).astype(jnp.bfloat16)
     for at, query_ref in enumerate(query_refs):
         query = query_ref[0]
-        base = 2 * at * rows
+        base = 2 * (first + at) * rows
+        queries[base : base + 2 * rows, LANES:] = one
         queries[base : base + rows, :LANES] = jnp.where(low, query, zero)
         queries[base + rows : base + 2 * rows, :LANES] = jnp.where(low, zero, query)
 
@@ -257,17 +258,17 @@
     return jnp.dot(weights.astype(jnp.bfloat16), values, preferred_element_type=jnp.float32)
 
 
-def store_heads(mixed, out_ref, first):
+def store_heads(mixed, out_ref, places):
     _, rows, _ = out_ref.shape
     low = lax.broadcasted_iota(jnp.int32, (rows, LANES), 1) < HEAD_DIM
     for at in range(mixed.shape[0] // (2 * rows)):
         base = 2 * at * rows
-        out_ref[first + at] = jnp.where(
+        out_ref[places[at]] = jnp.where(
             low, mixed[base : base + rows], mixed[base + rows : base + 2 * rows]
         ).astype(jnp.bfloat16)
 
 
-def attend_rows(keys, values, queries, out_ref, first):
+def attend_rows(keys, values, queries, out_ref, places):
     _, rows, _ = out_ref.shape
     total = queries.shape[0]
     for base in range(0, total, 4 * rows):
@@ -275,36 +276,49 @@
         scores = score(queries[block, :], keys[...])
         weights = jnp.exp(scores - jnp.max(scores, axis=1, keepdims=True))
         weight_sum = jnp.sum(weights, axis=1, keepdims=True)
-        store_heads(mix(weights, values[...]) / weight_sum, out_ref, first + base // (2 * rows))
-
-
-def attend_early_kernel(info_ref, *refs):
-    chips = len(refs) - 6
-    got_refs = refs[:chips]
-    keys, values, queries, mixed_ref, peak_ref, sum_ref = refs[chips:]
+        mixed = mix(weights, values[...]) / weight_sum
+        store_heads(mixed, out_ref, places[base // (2 * rows) :])
+
+
+def place_chips(info_ref, aparts, first, got_refs, keys, values, queries, first_query):
     _, rows, _ = got_refs[0].shape
-    for apart, got_ref in enumerate(got_refs):
-        place_keys(info_ref, apart, got_ref, keys, values, apart * rows)
-    place_queries(got_refs[1::2], queries)
-    scores = score(queries[...], keys[...])
+    for at, apart in enumerate(aparts):
+        place_keys(info_ref, apart, got_refs[at], keys, values, (first + at) * rows)
+    odd = [ref for apart, ref in zip(aparts, got_refs) if apart % 2]
+    place_queries(odd, queries, first_query)
+
+
+def prepare_kernel(aparts, info_ref, *refs):
+    got_refs = refs[: len(aparts)]
+    keys, values, queries = refs[len(aparts) :]
+    place_chips(info_ref, aparts, 0, got_refs, keys, values, queries, 0)
+
+
+def attend_early_kernel(aparts, first, first_query, info_ref, keys_in, values_in, queries_in, *refs):
+    del keys_in, values_in, queries_in
+    got_refs = refs[: len(aparts)]
+    keys, values, queries, mixed_ref, peak_ref, sum_ref = refs[len(aparts) :]
+    _, rows, _ = got_refs[0].shape
+    place_chips(info_ref, aparts, first, got_refs, keys, values, queries, first_query)
+    held = (first + len(aparts)) * rows
+    scores = score(queries[...], keys[:held, :])
     peak = jnp.max(scores, axis=1, keepdims=True)
     weights = jnp.exp(scores - peak)
     peak_ref[...] = jnp.broadcast_to(peak, peak_ref.shape)
     sum_ref[...] = jnp.broadcast_to(jnp.sum(weights, axis=1, keepdims=True), sum_ref.shape)
-    mixed_ref[...] = mix(weights, values[...])
+    mixed_ref[...] = mix(weights, values[:held, :])
 
 
 def attend_last_kernel(
-    info_ref, early_keys, early_values, early_queries, mixed_ref, peak_ref, sum_ref, last_ref,
-    out_ref, keys, values, queries,
+    apart, places, info_ref, keys_in, values_in, early_queries, mixed_ref, peak_ref, sum_ref,
+    last_ref, out_ref, keys, values, queries,
 ):
-    held, _ = early_values.shape
+    del keys_in, values_in
     _, rows, _ = last_ref.shape
-    keys[:held, :] = early_keys[...]
-    values[:held, :] = early_values[...]
-    place_keys(info_ref, held // rows, last_ref, keys, values, held)
+    held = keys.shape[0] - rows
+    place_keys(info_ref, apart, last_ref, keys, values, held)
     place_queries([last_ref], queries)
-    attend_rows(keys, values, queries, out_ref, out_ref.shape[0] - 1)
+    attend_rows(keys, values, queries, out_ref, (apart // 2,))
     scores = score(early_queries[...], keys[held:, :])
     peak = peak_ref[...]
     joined = jnp.maximum(peak, jnp.max(scores, axis=1, keepdims=True))
@@ -312,14 +326,14 @@
     weights = jnp.exp(scores - joined[:, : scores.shape[1]])
     weight_sum = sum_ref[...] * scale + jnp.sum(weights, axis=1, keepdims=True)
     mixed = mixed_ref[...] * scale + mix(weights, values[held:, :])
-    store_heads(mixed / weight_sum, out_ref, 0)
+    store_heads(mixed / weight_sum, out_ref, places)
 
 
 def attend_second_kernel(info_ref, keys, values, *refs):
     del info_ref
     out_ref, queries = refs[-2:]
     place_queries(refs[:-2], queries)
-    attend_rows(keys, values, queries, out_ref, 0)
+    attend_rows(keys, values, queries, out_ref, tuple(range(out_ref.shape[0])))
 
 
 def merge_kernel(info_ref, own_ref, got_ref, *out_refs):
@@ -361,7 +375,7 @@
     send_ref[...] = speed[pl.ds(pl.multiple_of((1 - core) * half, 8), half), :]
 
 
-def call(kernel, out_shape, inputs, scratch, hbm=()):
+def call(kernel, out_shape, inputs, scratch, hbm=(), aliases=None):
     single = not isinstance(out_shape, tuple)
     specs = [hbm_spec() if at in hbm else vmem_spec() for at in range(1, len(inputs))]
     inputs = list(inputs)
@@ -373,6 +387,7 @@
         in_specs=[smem_spec()] + specs,
         out_specs=vmem_spec() if single else tuple(vmem_spec() for _ in out_shape),
         scratch_shapes=scratch,
+        input_output_aliases=aliases or {},
         compiler_params=pltpu.CompilerParams(vmem_limit_bytes=GRANT),
     )(*inputs)
 
@@ -506,27 +521,37 @@
             apart = first + side
             held[apart] = across(made[side], 2 * apart, count) if apart else made[side]
     total, half = chips * rows, chips // 2
-    early, early_rows = total - rows, 2 * (half - 1) * rows
-    parts = call(
-        attend_early_kernel,
-        (
-            array((early, 2 * LANES), jnp.bfloat16),
-            array((early, LANES), jnp.bfloat16),
-            array((early_rows, 2 * LANES), jnp.bfloat16),
-        )
-        + (array((early_rows, LANES)),) * 3,
-        (info,) + tuple(held[apart] for apart in range(chips - 1)),
+    last = chips - 1
+    soon = (1, last - 1)
+    ready = tuple(apart for apart in range(chips) if apart not in soon + (last,))
+    query_order = tuple(apart for apart in ready + soon if apart % 2)
+    query_rows = 2 * len(query_order) * rows
+    buffers = (
+        array((total, 2 * LANES), jnp.bfloat16),
+        array((total, LANES), jnp.bfloat16),
+        array((query_rows, 2 * LANES), jnp.bfloat16),
+    )
+    placed = call(
+        functools.partial(prepare_kernel, ready),
+        buffers,
+        (info,) + tuple(held[apart] for apart in ready),
         [],
     )
+    ready_odd = sum(apart % 2 for apart in ready)
+    keys, values, early_queries, *parts = call(
+        functools.partial(attend_early_kernel, soon, len(ready), ready_odd),
+        buffers + (array((query_rows, LANES)),) * 3,
+        (info,) + tuple(placed) + tuple(held[apart] for apart in soon),
+        [],
+        aliases={1: 0, 2: 1, 3: 2},
+    )
+    places = tuple(apart // 2 for apart in query_order)
     crossing, keys, values = call(
-        attend_last_kernel,
-        (
-            array((half, rows, LANES), jnp.bfloat16),
-            array((total, 2 * LANES), jnp.bfloat16),
-            array((total, LANES), jnp.bfloat16),
-        ),
-        (info,) + tuple(parts) + (held[chips - 1],),
+        functools.partial(attend_last_kernel, last, places),
+        (array((half, rows, LANES), jnp.bfloat16),) + buffers[:2],
+        (info, keys, values, early_queries) + tuple(parts) + (held[last],),
         [VMEM((2 * rows, 2 * LANES), jnp.bfloat16)],
+        aliases={1: 1, 2: 2},
     )
     crossed = across(crossing, 2, count)
     staying = call(

time: 59.6 us -> 60 us (level)
  waiting for transfers between devices: 14 us -> 12.7 us
  starting transfers between devices: 21.2 us -> 22.4 us
  Pallas kernels: 18.4 us -> 19 us
    ppermute x14, waiting for transfers between devices: 13.5 us -> 12.2 us  [across(): return lax.ppermute(value, 'seq', [(i, i ^ apart) for i in range(count)])]
    ppermute x14, starting transfers between devices: 18.3 us -> 19.4 us  [across(): return lax.ppermute(value, 'seq', [(i, i ^ apart) for i in range(count)])]
    pallas_call x10 -> x11, Pallas kernels: 18.4 us -> 19 us  [call(): pl.pallas_call(kernel, out_shape=out_shape, in_specs=[smem_spec()] + spec...]
  transfers between devices with their start and end apart: 15 -> 15, of which waited for: 7 -> 6; matrix products, arithmetic and copies ran while one was open for 2% -> 2% of each run, Pallas kernels for 14% -> 15%
where the time goes in v5:
time: 60 us; the launch traced here: 59.8 us
  starting transfers between devices  22.4 us (37%)
  Pallas kernels  19 us (32%)
  waiting for transfers between devices  12.7 us (21%)
  between operations  2.85 us (5%)
  local copies, waits for them, and re-layouts  1.86 us (3%)
  other arithmetic  1.01 us (2%)
    ppermute x14, starting transfers between devices, across(): return lax.ppermute(value, 'seq', [(i, i ^ apart) for i in range(count)])  19.4 us
    pallas_call x11, Pallas kernels, call(): pl.pallas_call(kernel, out_shape=out_shape, in_specs=[smem_spec()] + spec...  19 us
    ppermute x14, waiting for transfers between devices, across(): return lax.ppermute(value, 'seq', [(i, i ^ apart) for i in range(count)])  12.2 us
    ppermute x1, starting transfers between devices, per_device(): lax.ppermute(edges, ('clip', 'seq'), facing_pairs(lax.axis_size('clip'),...  2.97 us
  transfers between devices with their start and end apart: 15, of which 6 were waited for; matrix products, arithmetic and copies ran while one was open for 2% of the time, Pallas kernels for 15%

profile of v5, /device:TPU:0, one launch (start us, length us, event | category | flops | bytes accessed | tf_op | source)
XLA Modules:
  0.0 59.8 jit_solution(15053803520957406077)
XLA Ops:
  0.6 0.9 %constant_dynamic-slice_fusion = bf16[2,16,1536]{2,1,0:T(8,128)(2,1)S(1)} fusion(bf16[2,56,1536]{2,1,0:T(8,128)(2,1)} %hidden_hbm.1, s32[]{:T(128)S(6)} %select_n.45), kind=kLoop, calls=%fused_computation.15 | loop fusion | bytes 196612 | tf_op jit(solution)/shard_map/dynamic_slice | solution.py:589
  1.5 3.0 %collective-permute-start.1 = (bf16[2,16,1536]{2,1,0:T(8,128)(2,1)S(1)}, bf16[2,16,1536]{2,1,0:T(8,128)(2,1)S(1)}, u32[]{:S(2)}, u32[]{:S(2)}) collective-permute-start(bf16[2,16,1536]{2,1,0:T(8,128)(2,1)S(1)} %constant_dynamic-slice_fusion), channel_id=1, source_target_pairs={{1,2},{2,1},{3,4},{4,3},{5,6},{6,5},{7,8},{8,7},{9,10},{10,9},{11,... | collective-permute-start | bytes 294920 | tf_op jit(solution)/shard_map/ppermute | solution.py:591
  4.5 0.9 %dynamic-slice_bitcast_fusion = bf16[56,1536]{1,0:T(8,128)(2,1)S(1)} fusion(bf16[2,56,1536]{2,1,0:T(8,128)(2,1)} %hidden_hbm.1, s32[]{:T(128)S(6)} %select_n.44), kind=kLoop, calls=%fused_computation | loop fusion | bytes 344068 | tf_op jit(solution)/shard_map/squeeze | solution.py:590
  5.4 0.2 collective-permute-start
  5.7 0.3 fusion
  6.6 0.5 collective-permute-done.1.near_ref
  7.1 0.1 collective-permute-start.2
  7.2 0.1 pad_add_fusion.info_ref
  7.3 1.6 %shard_map.113 = (bf16[56,1536]{1,0:T(8,128)(2,1)S(1)}, f32[31,1536]{1,0:T(8,128)S(1)}, f32[5,1536]{1,0:T(8,128)S(1)}, f32[56,100]{1,0:T(8,128)S(1)}, f32[56,100]{1,0:T(8,128)S(1)}) custom-call(s32[3]{0:T(128)S(1)} %pad_add_fusion.info_ref, bf16[2,56,1536]{2,1,0:T(8,128)(2,1)} %hidden_hbm.1, f32[31,1536]{1,0:T(8,128)} %taps_hbm.1, f32[5,1536]{1,0:T(8,128)} %mod_hbm.1), custom_call_target="tpu_custom_call" | custom-call | tf_op jit(solution)/shard_map/pallas_call | solution.py:384
  8.9 0.0 collective-permute-done.partner_ref
  8.9 0.0 collective-permute-done.2.far_ref
  8.9 4.7 %shard_map.114 = (f32[112,1536]{1,0:T(8,128)S(1)}, bf16[112,1536]{1,0:T(8,128)(2,1)S(1)}, bf16[1536,3072]{1,0:T(8,128)(2,1)S(1)}, bf16[3,112,128]{2,1,0:T(8,128)(2,1)S(1)}, bf16[3,112,128]{2,1,0:T(8,128)(2,1)S(1)}) custom-call(s32[3]{0:T(128)S(1)} %pad_add_fusion.info_ref, bf16[56,1536]{1,0:T(8,128)(2,1)S(1)} %get-tuple-element.37.own_ref, ...), custom_call_target="tpu_custom_call" | custom-call | tf_op jit(solution)/shard_map/pallas_call | solution.py:384
  13.6 1.2 %shard_map.116 = (bf16[3,112,128]{2,1,0:T(8,128)(2,1)S(1)}, bf16[3,112,128]{2,1,0:T(8,128)(2,1)S(1)}) custom-call(s32[3]{0:T(128)S(1)} %pad_add_fusion.info_ref, bf16[112,1536]{1,0:T(8,128)(2,1)S(1)} %get-tuple-element.41.normed_ref, bf16[1536,3072]{1,0:T(8,128)(2,1)S(1)} %get-tuple-element.42.weight_ref, f32[112,128]{1,0:T(8,128)S(1)} %get-tuple-element.71.cos_ref, ...), custom_call_target="tpu_custom_call" | custom-call | tf_op jit(solution)/shard_map/pallas_call | solution.py:384
  14.8 2.5 %collective-permute-start.3 = (bf16[3,112,128]{2,1,0:T(8,128)(2,1)S(1)}, bf16[3,112,128]{2,1,0:T(8,128)(2,1)S(1)}, u32[]{:S(2)}, u32[]{:S(2)}) collective-permute-start(bf16[3,112,128]{2,1,0:T(8,128)(2,1)S(1)} %get-tuple-element.44), channel_id=1, source_target_pairs={{0,4},{1,5},{2,6},{3,7},{4,0},{5,1},{6,2},{7,3},{8,12},{9,13},{10,... | collective-permute-start | bytes 258056 | tf_op jit(solution)/shard_map/ppermute | solution.py:425
  17.3 1.4 %collective-permute-start.4 = (bf16[3,112,128]{2,1,0:T(8,128)(2,1)S(1)}, bf16[3,112,128]{2,1,0:T(8,128)(2,1)S(1)}, u32[]{:S(2)}, u32[]{:S(2)}) collective-permute-start(bf16[3,112,128]{2,1,0:T(8,128)(2,1)S(1)} %get-tuple-element.45), channel_id=1, source_target_pairs={{0,6},{1,7},{2,4},{3,5},{4,2},{5,3},{6,0},{7,1},{8,14},{9,15},{10,... | collective-permute-start | bytes 258056 | tf_op jit(solution)/shard_map/ppermute | solution.py:425
  18.7 1.2 %shard_map.118 = (bf16[3,112,128]{2,1,0:T(8,128)(2,1)S(1)}, bf16[3,112,128]{2,1,0:T(8,128)(2,1)S(1)}) custom-call(s32[3]{0:T(128)S(1)} %pad_add_fusion.info_ref, bf16[112,1536]{1,0:T(8,128)(2,1)S(1)} %get-tuple-element.41.normed_ref, bf16[1536,3072]{1,0:T(8,128)(2,1)S(1)} %get-tuple-element.42.weight_ref, f32[112,128]{1,0:T(8,128)S(1)} %get-tuple-element.71.cos_ref, ...), custom_call_target="tpu_custom_call" | custom-call | tf_op jit(solution)/shard_map/pallas_call | solution.py:384
  19.9 0.0 copy-start
  20.0 0.0 copy-start.1
  20.0 0.0 copy-start.2
  20.0 1.2 %shard_map.115 = (bf16[3,112,128]{2,1,0:T(8,128)(2,1)S(1)}, bf16[3,112,128]{2,1,0:T(8,128)(2,1)S(1)}) custom-call(s32[3]{0:T(128)S(1)} %pad_add_fusion.info_ref, bf16[112,1536]{1,0:T(8,128)(2,1)S(1)} %get-tuple-element.41.normed_ref, bf16[1536,3072]{1,0:T(8,128)(2,1)S(1)} %get-tuple-element.42.weight_ref, f32[112,128]{1,0:T(8,128)S(1)} %get-tuple-element.71.cos_ref, ...), custom_call_target="tpu_custom_call" | custom-call | tf_op jit(solution)/shard_map/pallas_call | solution.py:384
  21.2 2.7 %collective-permute-start.5 = (bf16[3,112,128]{2,1,0:T(8,128)(2,1)S(1)}, bf16[3,112,128]{2,1,0:T(8,128)(2,1)S(1)}, u32[]{:S(2)}, u32[]{:S(2)}) collective-permute-start(bf16[3,112,128]{2,1,0:T(8,128)(2,1)S(1)} %get-tuple-element.46), channel_id=1, source_target_pairs={{0,8},{1,9},{2,10},{3,11},{4,12},{5,13},{6,14},{7,15},{8,0},{9,1},... | collective-permute-start | bytes 258056 | tf_op jit(solution)/shard_map/ppermute | solution.py:425
  23.8 0.0 collective-permute-start.6
  23.9 3.8 %collective-permute-start.8 = (bf16[3,112,128]{2,1,0:T(8,128)(2,1)S(1)}, bf16[3,112,128]{2,1,0:T(8,128)(2,1)S(1)}, u32[]{:S(2)}, u32[]{:S(2)}) collective-permute-start(bf16[3,112,128]{2,1,0:T(8,128)(2,1)S(1)} %get-tuple-element.52), channel_id=1, source_target_pairs={{0,12},{1,13},{2,14},{3,15},{4,8},{5,9},{6,10},{7,11},{8,4},{9,5},... | collective-permute-start | bytes 258056 | tf_op jit(solution)/shard_map/ppermute | solution.py:425
  27.7 0.0 collective-permute-done.3.refs_1_
  27.7 0.5 collective-permute-start.7
  28.1 0.0 collective-permute-done.4.refs_2_
  28.1 1.0 %collective-permute-start.9 = (bf16[3,112,128]{2,1,0:T(8,128)(2,1)S(1)}, bf16[3,112,128]{2,1,0:T(8,128)(2,1)S(1)}, u32[]{:S(2)}, u32[]{:S(2)}) collective-permute-start(bf16[3,112,128]{2,1,0:T(8,128)(2,1)S(1)} %get-tuple-element.59), channel_id=1, source_target_pairs={{0,14},{1,15},{2,12},{3,13},{4,10},{5,11},{6,8},{7,9},{8,6},{9,7},... | collective-permute-start | bytes 258056 | tf_op jit(solution)/shard_map/ppermute | solution.py:425
  29.1 4.7 %collective-permute-done.5.refs_3_.refs_2_ = bf16[3,112,128]{2,1,0:T(8,128)(2,1)S(1)} collective-permute-done((bf16[3,112,128]{2,1,0:T(8,128)(2,1)S(1)}, bf16[3,112,128]{2,1,0:T(8,128)(2,1)S(1)}, u32[]{:S(2)}, u32[]{:S(2)}) %collective-permute-start.5) | collective-permute-done | bytes 86048 | tf_op jit(solution)/shard_map/ppermute | solution.py:425
  33.8 2.1 %collective-permute-done.6.refs_4_ = bf16[3,112,128]{2,1,0:T(8,128)(2,1)S(1)} collective-permute-done((bf16[3,112,128]{2,1,0:T(8,128)(2,1)S(1)}, bf16[3,112,128]{2,1,0:T(8,128)(2,1)S(1)}, u32[]{:S(2)}, u32[]{:S(2)}) %collective-permute-start.6) | collective-permute-done | bytes 86048 | tf_op jit(solution)/shard_map/ppermute | solution.py:425
  36.0 0.6 %shard_map.117 = (bf16[896,256]{1,0:T(8,128)(2,1)S(1)}, bf16[896,128]{1,0:T(8,128)(2,1)S(1)}, bf16[672,256]{1,0:T(8,128)(2,1)S(1)}) custom-call(s32[3]{0:T(128)S(1)} %pad_add_fusion.info_ref, bf16[3,112,128]{2,1,0:T(8,128)(2,1)S(1)} %get-tuple-element.43.refs_0_, bf16[3,112,128]{2,1,0:T(8,128)(2,1)S(1)} %collective-permute-done.3.refs_1_, ...), custom_call_target="tpu_custom_call" | custom-call | tf_op jit(solution)/shard_map/pallas_call | solution.py:384
  36.6 0.0 collective-permute-done.8.refs_1_.refs_3_
  36.6 0.0 collective-permute-done.7.refs_0_
  36.6 2.1 %shard_map.119 = (bf16[896,256]{1,0:T(8,128)(2,1)S(1)}, bf16[896,128]{1,0:T(8,128)(2,1)S(1)}, bf16[672,256]{1,0:T(8,128)(2,1)S(1)}, f32[672,128]{1,0:T(8,128)S(1...) custom-call(s32[3]{0:T(128)S(1)} %pad_add_fusion.info_ref, ...), custom_call_target="tpu_custom_call", output_to_operand_aliasing={{0}: (1, {}), {1}: (2, {}), {2}: (3, {})} | custom-call | tf_op jit(solution)/shard_map/pallas_call | solution.py:384
  38.7 0.0 collective-permute-done.9.last_ref
  38.8 1.5 %shard_map.120 = (bf16[4,112,128]{2,1,0:T(8,128)(2,1)S(1)}, bf16[896,256]{1,0:T(8,128)(2,1)S(1)}, bf16[896,128]{1,0:T(8,128)(2,1)S(1)}) custom-call(s32[3]{0:T(128)S(1)} %pad_add_fusion.info_ref, bf16[896,256]{1,0:T(8,128)(2,1)S(1)} %get-tuple-element.53.keys_in, ...), custom_call_target="tpu_custom_call", output_to_operand_aliasing={{1}: (1, {}), {2}: (2, {})} | custom-call | tf_op jit(solution)/shard_map/pallas_call | solution.py:384
  40.3 2.2 %collective-permute-start.10 = (bf16[4,112,128]{2,1,0:T(8,128)(2,1)S(1)}, bf16[4,112,128]{2,1,0:T(8,128)(2,1)S(1)}, u32[]{:S(2)}, u32[]{:S(2)}) collective-permute-start(bf16[4,112,128]{2,1,0:T(8,128)(2,1)S(1)} %get-tuple-element.62), channel_id=1, source_target_pairs={{0,2},{1,3},{2,0},{3,1},{4,6},{5,7},{6,4},{7,5},{8,10},{9,11},{10,... | collective-permute-start | bytes 344072 | tf_op jit(solution)/shard_map/ppermute | solution.py:425
  42.5 2.3 %shard_map.121.own_ref.refs_0_ = bf16[4,112,128]{2,1,0:T(8,128)(2,1)S(1)} custom-call(s32[3]{0:T(128)S(1)} %pad_add_fusion.info_ref, bf16[896,256]{1,0:T(8,128)(2,1)S(1)} %get-tuple-element.60.keys, bf16[896,128]{1,0:T(8,128)(2,1)S(1)} %get-tuple-element.61.values, bf16[3,112,128]{2,1,0:T(8,128)(2,1)S(1)} %get-tuple-element.43.refs_0_, ...), custom_call_target="tpu_custom_call" | custom-call | tf_op jit(solution)/shard_map/pallas_call | solution.py:384
  44.8 0.5 collective-permute-done.10.got_ref.refs_1_
  45.2 0.6 shard_map.122
  45.8 2.4 %collective-permute-start.11 = (bf16[2,112,128]{2,1,0:T(8,128)(2,1)S(1)}, bf16[2,112,128]{2,1,0:T(8,128)(2,1)S(1)}, u32[]{:S(2)}, u32[]{:S(2)}) collective-permute-start(bf16[2,112,128]{2,1,0:T(8,128)(2,1)S(1)} %get-tuple-element.63), channel_id=1, source_target_pairs={{0,4},{1,5},{2,6},{3,7},{4,0},{5,1},{6,2},{7,3},{8,12},{9,13},{10,... | collective-permute-start | bytes 172040 | tf_op jit(solution)/shard_map/ppermute | solution.py:425
  48.1 1.5 %collective-permute-start.12 = (bf16[2,112,128]{2,1,0:T(8,128)(2,1)S(1)}, bf16[2,112,128]{2,1,0:T(8,128)(2,1)S(1)}, u32[]{:S(2)}, u32[]{:S(2)}) collective-permute-start(bf16[2,112,128]{2,1,0:T(8,128)(2,1)S(1)} %get-tuple-element.64), channel_id=1, source_target_pairs={{0,8},{1,9},{2,10},{3,11},{4,12},{5,13},{6,14},{7,15},{8,0},{9,1},... | collective-permute-start | bytes 172040 | tf_op jit(solution)/shard_map/ppermute | solution.py:425
  49.7 1.1 %collective-permute-start.13 = (bf16[2,112,128]{2,1,0:T(8,128)(2,1)S(1)}, bf16[2,112,128]{2,1,0:T(8,128)(2,1)S(1)}, u32[]{:S(2)}, u32[]{:S(2)}) collective-permute-start(bf16[2,112,128]{2,1,0:T(8,128)(2,1)S(1)} %get-tuple-element.65), channel_id=1, source_target_pairs={{0,12},{1,13},{2,14},{3,15},{4,8},{5,9},{6,10},{7,11},{8,4},{9,5},... | collective-permute-start | bytes 172040 | tf_op jit(solution)/shard_map/ppermute | solution.py:425
  50.7 3.6 %collective-permute-done.12.refs_3_ = bf16[2,112,128]{2,1,0:T(8,128)(2,1)S(1)} collective-permute-done((bf16[2,112,128]{2,1,0:T(8,128)(2,1)S(1)}, bf16[2,112,128]{2,1,0:T(8,128)(2,1)S(1)}, u32[]{:S(2)}, u32[]{:S(2)}) %collective-permute-start.12) | collective-permute-done | bytes 57376 | tf_op jit(solution)/shard_map/ppermute | solution.py:425
  54.4 1.3 %collective-permute-done.13.refs_4_ = bf16[2,112,128]{2,1,0:T(8,128)(2,1)S(1)} collective-permute-done((bf16[2,112,128]{2,1,0:T(8,128)(2,1)S(1)}, bf16[2,112,128]{2,1,0:T(8,128)(2,1)S(1)}, u32[]{:S(2)}, u32[]{:S(2)}) %collective-permute-start.13) | collective-permute-done | bytes 57376 | tf_op jit(solution)/shard_map/ppermute | solution.py:425
  55.7 2.0 %shard_map.123 = (f32[56,100]{1,0:T(8,128)S(1)}, f32[56,100]{1,0:T(8,128)S(1)}) custom-call(s32[3]{0:T(128)S(1)} %pad_add_fusion.info_ref, f32[112,1536]{1,0:T(8,128)S(1)} %get-tuple-element.40.residual, bf16[100,1536]{1,0:T(8,128)(2,1)S(1)} %bitcast.8, f32[5,1536]{1,0:T(8,128)S(1)} %get-tuple-element.39.mod_ref, bf16[1024,1536]{1,0:T(8,128)(2,1)S(1)} %copy-done, ...), custom_call_target="tpu_custom_call" | custom-call | tf_op jit(solution)/shard_map/pallas_call | solution.py:384
  57.7 0.1 collective-permute-start.14
  59.2 0.0 collective-permute-done.14
  59.2 0.6 %multiply_add_fusion = (f32[56,100]{1,0:T(8,128)}, f32[56,100]{1,0:T(8,128)}) fusion(f32[56,100]{1,0:T(8,128)S(1)} %copy-done.2, f32[]{:T(128)} %bitcast.5, f32[56,100]{1,0:T(8,128)S(1)} %collective-permute-done.14, f32[56,100]{1,0:T(8,128)S(1)} %get-tuple-element.66, f32[]{:T(128)} %bitcast.7, f32[56,100]{1,0:T(8,128)S(1)} %get-tuple-element.36, ...), kind=kLoop, calls=%fused_computation.4 | loop fusion | flops 56000 | bytes 156808 | tf_op jit(solution)/shard_map/add | solution.py:648
  (6 shorter events, 0.0 us)
Async XLA Ops:
  1.5 5.6 %collective-permute-start.1 = (bf16[2,16,1536]{2,1,0:T(8,128)(2,1)S(1)}, bf16[2,16,1536]{2,1,0:T(8,128)(2,1)S(1)}, u32[]{:S(2)}, u32[]{:S(2)}) collective-permute-start(bf16[2,16,1536]{2,1,0:T(8,128)(2,1)S(1)} %constant_dynamic-slice_fusion), channel_id=1, source_target_pairs={{1,2},{2,1},{3,4},{4,3},{5,6},{6,5},{7,8},{8,7},{9,10},{10,9},{11,... | collective-permute-start | bytes 294920 | tf_op jit(solution)/shard_map/ppermute | solution.py:591
  5.4 3.4 %collective-permute-start = (bf16[56,1536]{1,0:T(8,128)(2,1)S(1)}, bf16[56,1536]{1,0:T(8,128)(2,1)S(1)}, u32[]{:S(2)}, u32[]{:S(2)}) collective-permute-start(bf16[56,1536]{1,0:T(8,128)(2,1)S(1)} %dynamic-slice_bitcast_fusion), channel_id=1, source_target_pairs={{0,1},{1,0},{2,3},{3,2},{4,5},{5,4},{6,7},{7,6},{8,9},{9,8},{10,11... | collective-permute-start | bytes 516104 | tf_op jit(solution)/shard_map/ppermute | solution.py:425
  7.1 1.8 %collective-permute-start.2 = (bf16[2,16,1536]{2,1,0:T(8,128)(2,1)S(1)}, bf16[2,16,1536]{2,1,0:T(8,128)(2,1)S(1)}, u32[]{:S(2)}, u32[]{:S(2)}) collective-permute-start(bf16[2,16,1536]{2,1,0:T(8,128)(2,1)S(1)} %collective-permute-done.1.near_ref), channel_id=1, source_target_pairs={{0,1},{1,0},{2,3},{3,2},{4,5},{5,4},{6,7},{7,6},{8,9},{9,8},{10,11... | collective-permute-start | bytes 294920 | tf_op jit(solution)/shard_map/ppermute | solution.py:425
  14.8 12.9 %collective-permute-start.3 = (bf16[3,112,128]{2,1,0:T(8,128)(2,1)S(1)}, bf16[3,112,128]{2,1,0:T(8,128)(2,1)S(1)}, u32[]{:S(2)}, u32[]{:S(2)}) collective-permute-start(bf16[3,112,128]{2,1,0:T(8,128)(2,1)S(1)} %get-tuple-element.44), channel_id=1, source_target_pairs={{0,4},{1,5},{2,6},{3,7},{4,0},{5,1},{6,2},{7,3},{8,12},{9,13},{10,... | collective-permute-start | bytes 258056 | tf_op jit(solution)/shard_map/ppermute | solution.py:425
  17.3 10.8 %collective-permute-start.4 = (bf16[3,112,128]{2,1,0:T(8,128)(2,1)S(1)}, bf16[3,112,128]{2,1,0:T(8,128)(2,1)S(1)}, u32[]{:S(2)}, u32[]{:S(2)}) collective-permute-start(bf16[3,112,128]{2,1,0:T(8,128)(2,1)S(1)} %get-tuple-element.45), channel_id=1, source_target_pairs={{0,6},{1,7},{2,4},{3,5},{4,2},{5,3},{6,0},{7,1},{8,14},{9,15},{10,... | collective-permute-start | bytes 258056 | tf_op jit(solution)/shard_map/ppermute | solution.py:425
  19.9 35.7 %copy-start = (bf16[1024,1536]{1,0:T(8,128)(2,1)S(1)}, bf16[1024,1536]{1,0:T(8,128)(2,1)}, u32[]{:S(2)}) copy-start(bf16[1024,1536]{1,0:T(8,128)(2,1)} %w_out_ref.1) | copy-start | bytes 9437188
  20.0 35.7 %copy-start.1 = (bf16[1536,100]{0,1:T(8,128)(2,1)S(1)}, bf16[1536,100]{0,1:T(8,128)(2,1)}, u32[]{:S(2)}) copy-start(bf16[1536,100]{0,1:T(8,128)(2,1)} %param.19) | copy-start | bytes 921604
  20.0 39.2 %copy-start.2 = (f32[56,100]{1,0:T(8,128)S(1)}, f32[56,100]{1,0:T(8,128)}, u32[]{:S(2)}) copy-start(f32[56,100]{1,0:T(8,128)} %param.11) | copy-start | bytes 67204
  21.2 12.7 %collective-permute-start.5 = (bf16[3,112,128]{2,1,0:T(8,128)(2,1)S(1)}, bf16[3,112,128]{2,1,0:T(8,128)(2,1)S(1)}, u32[]{:S(2)}, u32[]{:S(2)}) collective-permute-start(bf16[3,112,128]{2,1,0:T(8,128)(2,1)S(1)} %get-tuple-element.46), channel_id=1, source_target_pairs={{0,8},{1,9},{2,10},{3,11},{4,12},{5,13},{6,14},{7,15},{8,0},{9,1},... | collective-permute-start | bytes 258056 | tf_op jit(solution)/shard_map/ppermute | solution.py:425
  23.8 12.1 %collective-permute-start.6 = (bf16[3,112,128]{2,1,0:T(8,128)(2,1)S(1)}, bf16[3,112,128]{2,1,0:T(8,128)(2,1)S(1)}, u32[]{:S(2)}, u32[]{:S(2)}) collective-permute-start(bf16[3,112,128]{2,1,0:T(8,128)(2,1)S(1)} %get-tuple-element.47), channel_id=1, source_target_pairs={{0,10},{1,11},{2,8},{3,9},{4,14},{5,15},{6,12},{7,13},{8,2},{9,3},... | collective-permute-start | bytes 258056 | tf_op jit(solution)/shard_map/ppermute | solution.py:425
  23.9 12.8 %collective-permute-start.8 = (bf16[3,112,128]{2,1,0:T(8,128)(2,1)S(1)}, bf16[3,112,128]{2,1,0:T(8,128)(2,1)S(1)}, u32[]{:S(2)}, u32[]{:S(2)}) collective-permute-start(bf16[3,112,128]{2,1,0:T(8,128)(2,1)S(1)} %get-tuple-element.52), channel_id=1, source_target_pairs={{0,12},{1,13},{2,14},{3,15},{4,8},{5,9},{6,10},{7,11},{8,4},{9,5},... | collective-permute-start | bytes 258056 | tf_op jit(solution)/shard_map/ppermute | solution.py:425
  27.7 9.0 %collective-permute-start.7 = (bf16[3,112,128]{2,1,0:T(8,128)(2,1)S(1)}, bf16[3,112,128]{2,1,0:T(8,128)(2,1)S(1)}, u32[]{:S(2)}, u32[]{:S(2)}) collective-permute-start(bf16[3,112,128]{2,1,0:T(8,128)(2,1)S(1)} %get-tuple-element.51), channel_id=1, source_target_pairs={{0,2},{1,3},{2,0},{3,1},{4,6},{5,7},{6,4},{7,5},{8,10},{9,11},{10,... | collective-permute-start | bytes 258056 | tf_op jit(solution)/shard_map/ppermute | solution.py:425
  28.1 10.6 %collective-permute-start.9 = (bf16[3,112,128]{2,1,0:T(8,128)(2,1)S(1)}, bf16[3,112,128]{2,1,0:T(8,128)(2,1)S(1)}, u32[]{:S(2)}, u32[]{:S(2)}) collective-permute-start(bf16[3,112,128]{2,1,0:T(8,128)(2,1)S(1)} %get-tuple-element.59), channel_id=1, source_target_pairs={{0,14},{1,15},{2,12},{3,13},{4,10},{5,11},{6,8},{7,9},{8,6},{9,7},... | collective-permute-start | bytes 258056 | tf_op jit(solution)/shard_map/ppermute | solution.py:425
  40.3 5.0 %collective-permute-start.10 = (bf16[4,112,128]{2,1,0:T(8,128)(2,1)S(1)}, bf16[4,112,128]{2,1,0:T(8,128)(2,1)S(1)}, u32[]{:S(2)}, u32[]{:S(2)}) collective-permute-start(bf16[4,112,128]{2,1,0:T(8,128)(2,1)S(1)} %get-tuple-element.62), channel_id=1, source_target_pairs={{0,2},{1,3},{2,0},{3,1},{4,6},{5,7},{6,4},{7,5},{8,10},{9,11},{10,... | collective-permute-start | bytes 344072 | tf_op jit(solution)/shard_map/ppermute | solution.py:425
  45.8 5.0 %collective-permute-start.11 = (bf16[2,112,128]{2,1,0:T(8,128)(2,1)S(1)}, bf16[2,112,128]{2,1,0:T(8,128)(2,1)S(1)}, u32[]{:S(2)}, u32[]{:S(2)}) collective-permute-start(bf16[2,112,128]{2,1,0:T(8,128)(2,1)S(1)} %get-tuple-element.63), channel_id=1, source_target_pairs={{0,4},{1,5},{2,6},{3,7},{4,0},{5,1},{6,2},{7,3},{8,12},{9,13},{10,... | collective-permute-start | bytes 172040 | tf_op jit(solution)/shard_map/ppermute | solution.py:425
  48.1 6.2 %collective-permute-start.12 = (bf16[2,112,128]{2,1,0:T(8,128)(2,1)S(1)}, bf16[2,112,128]{2,1,0:T(8,128)(2,1)S(1)}, u32[]{:S(2)}, u32[]{:S(2)}) collective-permute-start(bf16[2,112,128]{2,1,0:T(8,128)(2,1)S(1)} %get-tuple-element.64), channel_id=1, source_target_pairs={{0,8},{1,9},{2,10},{3,11},{4,12},{5,13},{6,14},{7,15},{8,0},{9,1},... | collective-permute-start | bytes 172040 | tf_op jit(solution)/shard_map/ppermute | solution.py:425
  49.7 6.0 %collective-permute-start.13 = (bf16[2,112,128]{2,1,0:T(8,128)(2,1)S(1)}, bf16[2,112,128]{2,1,0:T(8,128)(2,1)S(1)}, u32[]{:S(2)}, u32[]{:S(2)}) collective-permute-start(bf16[2,112,128]{2,1,0:T(8,128)(2,1)S(1)} %get-tuple-element.65), channel_id=1, source_target_pairs={{0,12},{1,13},{2,14},{3,15},{4,8},{5,9},{6,10},{7,11},{8,4},{9,5},... | collective-permute-start | bytes 172040 | tf_op jit(solution)/shard_map/ppermute | solution.py:425
  57.7 1.5 %collective-permute-start.14 = (f32[56,100]{1,0:T(8,128)S(1)}, f32[56,100]{1,0:T(8,128)S(1)}, u32[]{:S(2)}, u32[]{:S(2)}) collective-permute-start(f32[56,100]{1,0:T(8,128)S(1)} %get-tuple-element.67), channel_id=1, source_target_pairs={{0,1},{1,0},{2,3},{3,2},{4,5},{5,4},{6,7},{7,6},{8,9},{9,8},{10,11... | collective-permute-start | bytes 67208 | tf_op jit(solution)/shard_map/ppermute | solution.py:425

commit v6 on v4

--- a/solution.py
+++ b/solution.py
@@ -278,33 +278,32 @@
         store_heads(mix(weights, values[...]) / weight_sum, out_ref, first + base // (2 * rows))
 
 
-def attend_early_kernel(info_ref, *refs):
+def attend_early_kernel(first, info_ref, *refs):
     chips = len(refs) - 6
     got_refs = refs[:chips]
     keys, values, queries, mixed_ref, peak_ref, sum_ref = refs[chips:]
     _, rows, _ = got_refs[0].shape
     for apart, got_ref in enumerate(got_refs):
         place_keys(info_ref, apart, got_ref, keys, values, apart * rows)
-    place_queries(got_refs[1::2], queries)
-    scores = score(queries[...], keys[...])
-    peak = jnp.max(scores, axis=1, keepdims=True)
-    weights = jnp.exp(scores - peak)
-    peak_ref[...] = jnp.broadcast_to(peak, peak_ref.shape)
-    sum_ref[...] = jnp.broadcast_to(jnp.sum(weights, axis=1, keepdims=True), sum_ref.shape)
-    mixed_ref[...] = mix(weights, values[...])
+    place_queries(got_refs[first : first + 2], queries)
+    half = queries.shape[0] // 2
+    for block in (slice(0, half), slice(half, 2 * half)):
+        scores = score(queries[block, :], keys[...])
+        peak = jnp.max(scores, axis=1, keepdims=True)
+        weights = jnp.exp(scores - peak)
+        peak_ref[block, :] = jnp.broadcast_to(peak, (half, LANES))
+        weight_sum = jnp.sum(weights, axis=1, keepdims=True)
+        sum_ref[block, :] = jnp.broadcast_to(weight_sum, (half, LANES))
+        mixed_ref[block, :] = mix(weights, values[...])
 
 
 def attend_last_kernel(
     info_ref, early_keys, early_values, early_queries, mixed_ref, peak_ref, sum_ref, last_ref,
-    out_ref, keys, values, queries,
+    out_ref, keys, values,
 ):
     held, _ = early_values.shape
     _, rows, _ = last_ref.shape
-    keys[:held, :] = early_keys[...]
-    values[:held, :] = early_values[...]
     place_keys(info_ref, held // rows, last_ref, keys, values, held)
-    place_queries([last_ref], queries)
-    attend_rows(keys, values, queries, out_ref, out_ref.shape[0] - 1)
     scores = score(early_queries[...], keys[held:, :])
     peak = peak_ref[...]
     joined = jnp.maximum(peak, jnp.max(scores, axis=1, keepdims=True))
@@ -313,6 +312,8 @@
     weight_sum = sum_ref[...] * scale + jnp.sum(weights, axis=1, keepdims=True)
     mixed = mixed_ref[...] * scale + mix(weights, values[held:, :])
     store_heads(mixed / weight_sum, out_ref, 0)
+    keys[:held, :] = early_keys[...]
+    values[:held, :] = early_values[...]
 
 
 def attend_second_kernel(info_ref, keys, values, *refs):
@@ -322,11 +323,10 @@
     attend_rows(keys, values, queries, out_ref, 0)
 
 
-def merge_kernel(info_ref, own_ref, got_ref, *out_refs):
+def merge_kernel(info_ref, *refs):
     del info_ref
-    for at, out_ref in enumerate(out_refs):
-        out_ref[0] = own_ref[at + 1]
-        out_ref[1] = got_ref[at + 1]
+    for at, got_ref in enumerate(refs[:-1]):
+        refs[-1][at] = got_ref[1]
 
 
 def back_kernel(blocks, info_ref, residual, w_mel, mod_ref, w_out_ref, *refs):
@@ -495,6 +495,10 @@
     return far[:1] + list(range(2, chips // 2, 2)) + far[1:] + [0]
 
 
+def return_order(chips):
+    return list(range(chips // 2, chips, 2)) + list(range(2, chips // 2, 2)) + [0]
+
+
 def attend_chips(made, normed, w_qkv, tables, info, count):
     rows = normed.shape[0]
     chips = count // 2
@@ -506,9 +510,10 @@
             apart = first + side
             held[apart] = across(made[side], 2 * apart, count) if apart else made[side]
     total, half = chips * rows, chips // 2
-    early, early_rows = total - rows, 2 * (half - 1) * rows
+    order = return_order(chips)
+    early, early_rows = total - rows, 4 * rows
     parts = call(
-        attend_early_kernel,
+        functools.partial(attend_early_kernel, order[0]),
         (
             array((early, 2 * LANES), jnp.bfloat16),
             array((early, LANES), jnp.bfloat16),
@@ -518,35 +523,33 @@
         (info,) + tuple(held[apart] for apart in range(chips - 1)),
         [],
     )
-    crossing, keys, values = call(
-        attend_last_kernel,
-        (
-            array((half, rows, LANES), jnp.bfloat16),
-            array((total, 2 * LANES), jnp.bfloat16),
-            array((total, LANES), jnp.bfloat16),
-        ),
-        (info,) + tuple(parts) + (held[chips - 1],),
-        [VMEM((2 * rows, 2 * LANES), jnp.bfloat16)],
-    )
-    crossed = across(crossing, 2, count)
-    staying = call(
-        attend_second_kernel,
-        array((half, rows, LANES), jnp.bfloat16),
-        (info, keys, values) + tuple(held[apart] for apart in range(0, chips, 2)),
-        [VMEM((total, 2 * LANES), jnp.bfloat16)],
-    )
-    joined = call(
-        merge_kernel,
-        (array((2, rows, LANES), jnp.bfloat16),) * (half - 1),
-        (info, staying, crossed),
-        [],
-    )
-    back, blocks = [staying, crossed], [(0, 0, 0), (1, 0, 1)]
-    apart_first = sorted(range(1, half), reverse=True)
-    got = {apart: across(joined[apart - 1], 4 * apart, count) for apart in apart_first}
-    for apart in range(1, half):
-        blocks += [(len(back), side, 2 * apart + side) for side in range(2)]
-        back.append(got[apart])
+    pair = array((2, rows, LANES), jnp.bfloat16)
+    got = {}
+    for first in order:
+        if first == order[0]:
+            attended, keys, values = call(
+                attend_last_kernel,
+                (
+                    pair,
+                    array((total, 2 * LANES), jnp.bfloat16),
+                    array((total, LANES), jnp.bfloat16),
+                ),
+                (info,) + tuple(parts) + (held[chips - 1],),
+                [],
+            )
+        else:
+            attended = call(
+                attend_second_kernel,
+                pair,
+                (info, keys, values, held[first], held[first + 1]),
+                [VMEM((4 * rows, 2 * LANES), jnp.bfloat16)],
+            )
+        got[first] = across(attended, 2 * first, count) if first else attended
+    back = [got[2 * at] for at in range(half)]
+    blocks = [(at, 0, 2 * at) for at in range(half)]
+    merged = call(merge_kernel, array((half, rows, LANES), jnp.bfloat16), [info] + back, [])
+    blocks += [(half, at, 2 * at + 1) for at in range(half)]
+    back.append(across(merged, 2, count))
     return back, blocks
 
 

time: 59.6 us -> 60.5 us (1.015)
  Pallas kernels: 18.4 us -> 20 us
    pallas_call x10 -> x12, Pallas kernels: 18.4 us -> 20 us  [call(): pl.pallas_call(kernel, out_shape=out_shape, in_specs=[smem_spec()] + spec...]
  transfers between devices with their start and end apart: 15 -> 15, of which waited for: 7 -> 7; matrix products, arithmetic and copies ran while one was open for 2% -> 2% of each run, Pallas kernels for 14% -> 15%
where the time goes in v6:
time: 60.5 us; the launch traced here: 60.3 us
  starting transfers between devices  20.7 us (34%)
  Pallas kernels  20 us (33%)
  waiting for transfers between devices  13.8 us (23%)
  between operations  2.86 us (5%)
  local copies, waits for them, and re-layouts  1.86 us (3%)
  other arithmetic  1.01 us (2%)
    pallas_call x12, Pallas kernels, call(): pl.pallas_call(kernel, out_shape=out_shape, in_specs=[smem_spec()] + spec...  20 us
    ppermute x14, starting transfers between devices, across(): return lax.ppermute(value, 'seq', [(i, i ^ apart) for i in range(count)])  17.8 us
    ppermute x14, waiting for transfers between devices, across(): return lax.ppermute(value, 'seq', [(i, i ^ apart) for i in range(count)])  13.3 us
    ppermute x1, starting transfers between devices, per_device(): lax.ppermute(edges, ('clip', 'seq'), facing_pairs(lax.axis_size('clip'),...  2.97 us
  transfers between devices with their start and end apart: 15, of which 7 were waited for; matrix products, arithmetic and copies ran while one was open for 2% of the time, Pallas kernels for 15%

profile of v6, /device:TPU:0, one launch (start us, length us, event | category | flops | bytes accessed | tf_op | source)
XLA Modules:
  0.0 60.3 jit_solution(2202580110903561185)
XLA Ops:
  0.6 0.9 %constant_dynamic-slice_fusion = bf16[2,16,1536]{2,1,0:T(8,128)(2,1)S(1)} fusion(bf16[2,56,1536]{2,1,0:T(8,128)(2,1)} %hidden_hbm.1, s32[]{:T(128)S(6)} %select_n.45), kind=kLoop, calls=%fused_computation.15 | loop fusion | bytes 196612 | tf_op jit(solution)/shard_map/dynamic_slice | solution.py:567
  1.5 3.0 %collective-permute-start.1 = (bf16[2,16,1536]{2,1,0:T(8,128)(2,1)S(1)}, bf16[2,16,1536]{2,1,0:T(8,128)(2,1)S(1)}, u32[]{:S(2)}, u32[]{:S(2)}) collective-permute-start(bf16[2,16,1536]{2,1,0:T(8,128)(2,1)S(1)} %constant_dynamic-slice_fusion), channel_id=1, source_target_pairs={{1,2},{2,1},{3,4},{4,3},{5,6},{6,5},{7,8},{8,7},{9,10},{10,9},{11,... | collective-permute-start | bytes 294920 | tf_op jit(solution)/shard_map/ppermute | solution.py:569
  4.5 0.9 %dynamic-slice_bitcast_fusion = bf16[56,1536]{1,0:T(8,128)(2,1)S(1)} fusion(bf16[2,56,1536]{2,1,0:T(8,128)(2,1)} %hidden_hbm.1, s32[]{:T(128)S(6)} %select_n.44), kind=kLoop, calls=%fused_computation | loop fusion | bytes 344068 | tf_op jit(solution)/shard_map/squeeze | solution.py:568
  5.4 0.2 collective-permute-start
  5.7 0.3 fusion
  6.6 0.5 collective-permute-done.1.near_ref
  7.1 0.1 collective-permute-start.2
  7.2 0.1 pad_add_fusion.info_ref
  7.3 1.6 %shard_map.113 = (bf16[56,1536]{1,0:T(8,128)(2,1)S(1)}, f32[31,1536]{1,0:T(8,128)S(1)}, f32[5,1536]{1,0:T(8,128)S(1)}, f32[56,100]{1,0:T(8,128)S(1)}, f32[56,100]{1,0:T(8,128)S(1)}) custom-call(s32[3]{0:T(128)S(1)} %pad_add_fusion.info_ref, bf16[2,56,1536]{2,1,0:T(8,128)(2,1)} %hidden_hbm.1, f32[31,1536]{1,0:T(8,128)} %taps_hbm.1, f32[5,1536]{1,0:T(8,128)} %mod_hbm.1), custom_call_target="tpu_custom_call" | custom-call | tf_op jit(solution)/shard_map/pallas_call | solution.py:370
  8.9 0.0 collective-permute-done.partner_ref
  8.9 0.0 collective-permute-done.2.far_ref
  8.9 4.7 %shard_map.114 = (f32[112,1536]{1,0:T(8,128)S(1)}, bf16[112,1536]{1,0:T(8,128)(2,1)S(1)}, bf16[1536,3072]{1,0:T(8,128)(2,1)S(1)}, bf16[3,112,128]{2,1,0:T(8,128)(2,1)S(1)}, bf16[3,112,128]{2,1,0:T(8,128)(2,1)S(1)}) custom-call(s32[3]{0:T(128)S(1)} %pad_add_fusion.info_ref, bf16[56,1536]{1,0:T(8,128)(2,1)S(1)} %get-tuple-element.31.own_ref, ...), custom_call_target="tpu_custom_call" | custom-call | tf_op jit(solution)/shard_map/pallas_call | solution.py:370
  13.6 1.2 %shard_map.117 = (bf16[3,112,128]{2,1,0:T(8,128)(2,1)S(1)}, bf16[3,112,128]{2,1,0:T(8,128)(2,1)S(1)}) custom-call(s32[3]{0:T(128)S(1)} %pad_add_fusion.info_ref, bf16[112,1536]{1,0:T(8,128)(2,1)S(1)} %get-tuple-element.35.normed_ref, bf16[1536,3072]{1,0:T(8,128)(2,1)S(1)} %get-tuple-element.36.weight_ref, f32[112,128]{1,0:T(8,128)S(1)} %get-tuple-element.59.cos_ref, ...), custom_call_target="tpu_custom_call" | custom-call | tf_op jit(solution)/shard_map/pallas_call | solution.py:370
  14.8 4.5 %collective-permute-start.8 = (bf16[3,112,128]{2,1,0:T(8,128)(2,1)S(1)}, bf16[3,112,128]{2,1,0:T(8,128)(2,1)S(1)}, u32[]{:S(2)}, u32[]{:S(2)}) collective-permute-start(bf16[3,112,128]{2,1,0:T(8,128)(2,1)S(1)} %get-tuple-element.43), channel_id=1, source_target_pairs={{0,12},{1,13},{2,14},{3,15},{4,8},{5,9},{6,10},{7,11},{8,4},{9,5},... | collective-permute-start | bytes 258056 | tf_op jit(solution)/shard_map/ppermute | solution.py:410
  19.3 1.2 %shard_map.116 = (bf16[3,112,128]{2,1,0:T(8,128)(2,1)S(1)}, bf16[3,112,128]{2,1,0:T(8,128)(2,1)S(1)}) custom-call(s32[3]{0:T(128)S(1)} %pad_add_fusion.info_ref, bf16[112,1536]{1,0:T(8,128)(2,1)S(1)} %get-tuple-element.35.normed_ref, bf16[1536,3072]{1,0:T(8,128)(2,1)S(1)} %get-tuple-element.36.weight_ref, f32[112,128]{1,0:T(8,128)S(1)} %get-tuple-element.59.cos_ref, ...), custom_call_target="tpu_custom_call" | custom-call | tf_op jit(solution)/shard_map/pallas_call | solution.py:370
  20.5 0.0 copy-start
  20.6 0.0 copy-start.1
  20.6 0.0 copy-start.2
  20.6 0.1 collective-permute-start.4
  20.7 1.2 %shard_map.115 = (bf16[3,112,128]{2,1,0:T(8,128)(2,1)S(1)}, bf16[3,112,128]{2,1,0:T(8,128)(2,1)S(1)}) custom-call(s32[3]{0:T(128)S(1)} %pad_add_fusion.info_ref, bf16[112,1536]{1,0:T(8,128)(2,1)S(1)} %get-tuple-element.35.normed_ref, bf16[1536,3072]{1,0:T(8,128)(2,1)S(1)} %get-tuple-element.36.weight_ref, f32[112,128]{1,0:T(8,128)S(1)} %get-tuple-element.59.cos_ref, ...), custom_call_target="tpu_custom_call" | custom-call | tf_op jit(solution)/shard_map/pallas_call | solution.py:370
  21.8 2.0 %collective-permute-start.5 = (bf16[3,112,128]{2,1,0:T(8,128)(2,1)S(1)}, bf16[3,112,128]{2,1,0:T(8,128)(2,1)S(1)}, u32[]{:S(2)}, u32[]{:S(2)}) collective-permute-start(bf16[3,112,128]{2,1,0:T(8,128)(2,1)S(1)} %get-tuple-element.40), channel_id=1, source_target_pairs={{0,6},{1,7},{2,4},{3,5},{4,2},{5,3},{6,0},{7,1},{8,14},{9,15},{10,... | collective-permute-start | bytes 258056 | tf_op jit(solution)/shard_map/ppermute | solution.py:410
  23.8 1.6 %collective-permute-start.3 = (bf16[3,112,128]{2,1,0:T(8,128)(2,1)S(1)}, bf16[3,112,128]{2,1,0:T(8,128)(2,1)S(1)}, u32[]{:S(2)}, u32[]{:S(2)}) collective-permute-start(bf16[3,112,128]{2,1,0:T(8,128)(2,1)S(1)} %get-tuple-element.38), channel_id=1, source_target_pairs={{0,2},{1,3},{2,0},{3,1},{4,6},{5,7},{6,4},{7,5},{8,10},{9,11},{10,... | collective-permute-start | bytes 258056 | tf_op jit(solution)/shard_map/ppermute | solution.py:410
  25.4 0.0 collective-permute-start.6
  25.4 0.0 collective-permute-done.8.refs_6_.refs_0_
  25.4 2.8 %collective-permute-start.7 = (bf16[3,112,128]{2,1,0:T(8,128)(2,1)S(1)}, bf16[3,112,128]{2,1,0:T(8,128)(2,1)S(1)}, u32[]{:S(2)}, u32[]{:S(2)}) collective-permute-start(bf16[3,112,128]{2,1,0:T(8,128)(2,1)S(1)} %get-tuple-element.42), channel_id=1, source_target_pairs={{0,10},{1,11},{2,8},{3,9},{4,14},{5,15},{6,12},{7,13},{8,2},{9,3},... | collective-permute-start | bytes 258056 | tf_op jit(solution)/shard_map/ppermute | solution.py:410
  28.2 0.0 collective-permute-done.4.refs_2_.refs_0_
  28.2 1.0 %collective-permute-start.9 = (bf16[3,112,128]{2,1,0:T(8,128)(2,1)S(1)}, bf16[3,112,128]{2,1,0:T(8,128)(2,1)S(1)}, u32[]{:S(2)}, u32[]{:S(2)}) collective-permute-start(bf16[3,112,128]{2,1,0:T(8,128)(2,1)S(1)} %get-tuple-element.50), channel_id=1, source_target_pairs={{0,14},{1,15},{2,12},{3,13},{4,10},{5,11},{6,8},{7,9},{8,6},{9,7},... | collective-permute-start | bytes 258056 | tf_op jit(solution)/shard_map/ppermute | solution.py:410
  29.2 0.1 collective-permute-done.3.refs_1_
  29.2 5.4 %collective-permute-done.6.refs_4_ = bf16[3,112,128]{2,1,0:T(8,128)(2,1)S(1)} collective-permute-done((bf16[3,112,128]{2,1,0:T(8,128)(2,1)S(1)}, bf16[3,112,128]{2,1,0:T(8,128)(2,1)S(1)}, u32[]{:S(2)}, u32[]{:S(2)}) %collective-permute-start.6) | collective-permute-done | bytes 86048 | tf_op jit(solution)/shard_map/ppermute | solution.py:410
  34.7 2.8 %collective-permute-done.7.refs_5_ = bf16[3,112,128]{2,1,0:T(8,128)(2,1)S(1)} collective-permute-done((bf16[3,112,128]{2,1,0:T(8,128)(2,1)S(1)}, bf16[3,112,128]{2,1,0:T(8,128)(2,1)S(1)}, u32[]{:S(2)}, u32[]{:S(2)}) %collective-permute-start.7) | collective-permute-done | bytes 86048 | tf_op jit(solution)/shard_map/ppermute | solution.py:410
  37.5 1.7 %shard_map.118 = (bf16[784,256]{1,0:T(8,128)(2,1)S(1)}, bf16[784,128]{1,0:T(8,128)(2,1)S(1)}, bf16[448,256]{1,0:T(8,128)(2,1)S(1)}, f32[448,128]{1,0:T(8,128)S(1...) custom-call(s32[3]{0:T(128)S(1)} %pad_add_fusion.info_ref, bf16[3,112,128]{2,1,0:T(8,128)(2,1)S(1)} %get-tuple-element.37.refs_0_, ...), custom_call_target="tpu_custom_call" | custom-call | tf_op jit(solution)/shard_map/pallas_call | solution.py:370
  39.2 1.1 %shard_map.119 = (bf16[2,112,128]{2,1,0:T(8,128)(2,1)S(1)}, bf16[896,256]{1,0:T(8,128)(2,1)S(1)}, bf16[896,128]{1,0:T(8,128)(2,1)S(1)}) custom-call(s32[3]{0:T(128)S(1)} %pad_add_fusion.info_ref, bf16[784,256]{1,0:T(8,128)(2,1)S(1)} %get-tuple-element.44.early_keys, bf16[784,128]{1,0:T(8,128)(2,1)S(1)} %get-tuple-element.45.early_values, ...), custom_call_target="tpu_custom_call" | custom-call | tf_op jit(solution)/shard_map/pallas_call | solution.py:370
  40.3 1.6 %shard_map.122 = bf16[2,112,128]{2,1,0:T(8,128)(2,1)S(1)} custom-call(s32[3]{0:T(128)S(1)} %pad_add_fusion.info_ref, bf16[896,256]{1,0:T(8,128)(2,1)S(1)} %get-tuple-element.51.keys, bf16[896,128]{1,0:T(8,128)(2,1)S(1)} %get-tuple-element.52.values, bf16[3,112,128]{2,1,0:T(8,128)(2,1)S(1)} %collective-permute-done.8.refs_6_.refs_0_, ...), custom_call_target="tpu_custom_call" | custom-call | tf_op jit(solution)/shard_map/pallas_call | solution.py:370
  41.9 2.0 %collective-permute-start.12 = (bf16[2,112,128]{2,1,0:T(8,128)(2,1)S(1)}, bf16[2,112,128]{2,1,0:T(8,128)(2,1)S(1)}, u32[]{:S(2)}, u32[]{:S(2)}) collective-permute-start(bf16[2,112,128]{2,1,0:T(8,128)(2,1)S(1)} %shard_map.122), channel_id=1, source_target_pairs={{0,12},{1,13},{2,14},{3,15},{4,8},{5,9},{6,10},{7,11},{8,4},{9,5},... | collective-permute-start | bytes 172040 | tf_op jit(solution)/shard_map/ppermute | solution.py:410
  43.9 1.6 %shard_map.121 = bf16[2,112,128]{2,1,0:T(8,128)(2,1)S(1)} custom-call(s32[3]{0:T(128)S(1)} %pad_add_fusion.info_ref, bf16[896,256]{1,0:T(8,128)(2,1)S(1)} %get-tuple-element.51.keys, bf16[896,128]{1,0:T(8,128)(2,1)S(1)} %get-tuple-element.52.values, bf16[3,112,128]{2,1,0:T(8,128)(2,1)S(1)} %collective-permute-done.4.refs_2_.refs_0_, ...), custom_call_target="tpu_custom_call" | custom-call | tf_op jit(solution)/shard_map/pallas_call | solution.py:370
  45.5 0.1 collective-permute-start.10
  45.6 2.4 %collective-permute-start.11 = (bf16[2,112,128]{2,1,0:T(8,128)(2,1)S(1)}, bf16[2,112,128]{2,1,0:T(8,128)(2,1)S(1)}, u32[]{:S(2)}, u32[]{:S(2)}) collective-permute-start(bf16[2,112,128]{2,1,0:T(8,128)(2,1)S(1)} %get-tuple-element.53), channel_id=1, source_target_pairs={{0,8},{1,9},{2,10},{3,11},{4,12},{5,13},{6,14},{7,15},{8,0},{9,1},... | collective-permute-start | bytes 172040 | tf_op jit(solution)/shard_map/ppermute | solution.py:410
  48.0 1.6 %shard_map.120.refs_0_ = bf16[2,112,128]{2,1,0:T(8,128)(2,1)S(1)} custom-call(s32[3]{0:T(128)S(1)} %pad_add_fusion.info_ref, bf16[896,256]{1,0:T(8,128)(2,1)S(1)} %get-tuple-element.51.keys, bf16[896,128]{1,0:T(8,128)(2,1)S(1)} %get-tuple-element.52.values, bf16[3,112,128]{2,1,0:T(8,128)(2,1)S(1)} %get-tuple-element.37.refs_0_, ...), custom_call_target="tpu_custom_call" | custom-call | tf_op jit(solution)/shard_map/pallas_call | solution.py:370
  49.6 0.0 collective-permute-done.12.refs_3_
  49.7 0.1 collective-permute-done.10.refs_1_
  49.8 1.0 %collective-permute-done.11.refs_2_ = bf16[2,112,128]{2,1,0:T(8,128)(2,1)S(1)} collective-permute-done((bf16[2,112,128]{2,1,0:T(8,128)(2,1)S(1)}, bf16[2,112,128]{2,1,0:T(8,128)(2,1)S(1)}, u32[]{:S(2)}, u32[]{:S(2)}) %collective-permute-start.11) | collective-permute-done | bytes 57376 | tf_op jit(solution)/shard_map/ppermute | solution.py:410
  50.7 0.5 shard_map.123
  51.3 0.9 %collective-permute-start.13 = (bf16[4,112,128]{2,1,0:T(8,128)(2,1)S(1)}, bf16[4,112,128]{2,1,0:T(8,128)(2,1)S(1)}, u32[]{:S(2)}, u32[]{:S(2)}) collective-permute-start(bf16[4,112,128]{2,1,0:T(8,128)(2,1)S(1)} %shard_map.123), channel_id=1, source_target_pairs={{0,2},{1,3},{2,0},{3,1},{4,6},{5,7},{6,4},{7,5},{8,10},{9,11},{10,... | collective-permute-start | bytes 344072 | tf_op jit(solution)/shard_map/ppermute | solution.py:410
  52.2 3.9 %collective-permute-done.13.refs_4_ = bf16[4,112,128]{2,1,0:T(8,128)(2,1)S(1)} collective-permute-done((bf16[4,112,128]{2,1,0:T(8,128)(2,1)S(1)}, bf16[4,112,128]{2,1,0:T(8,128)(2,1)S(1)}, u32[]{:S(2)}, u32[]{:S(2)}) %collective-permute-start.13) | collective-permute-done | bytes 114720 | tf_op jit(solution)/shard_map/ppermute | solution.py:410
  56.1 2.0 %shard_map.124 = (f32[56,100]{1,0:T(8,128)S(1)}, f32[56,100]{1,0:T(8,128)S(1)}) custom-call(s32[3]{0:T(128)S(1)} %pad_add_fusion.info_ref, f32[112,1536]{1,0:T(8,128)S(1)} %get-tuple-element.34.residual, bf16[100,1536]{1,0:T(8,128)(2,1)S(1)} %bitcast.8, f32[5,1536]{1,0:T(8,128)S(1)} %get-tuple-element.33.mod_ref, bf16[1024,1536]{1,0:T(8,128)(2,1)S(1)} %copy-done, ...), custom_call_target="tpu_custom_call" | custom-call | tf_op jit(solution)/shard_map/pallas_call | solution.py:370
  58.2 0.1 collective-permute-start.14
  59.6 0.0 collective-permute-done.14
  59.7 0.6 %multiply_add_fusion = (f32[56,100]{1,0:T(8,128)}, f32[56,100]{1,0:T(8,128)}) fusion(f32[56,100]{1,0:T(8,128)S(1)} %copy-done.2, f32[]{:T(128)} %bitcast.5, f32[56,100]{1,0:T(8,128)S(1)} %collective-permute-done.14, f32[56,100]{1,0:T(8,128)S(1)} %get-tuple-element.54, f32[]{:T(128)} %bitcast.7, f32[56,100]{1,0:T(8,128)S(1)} %get-tuple-element.30, ...), kind=kLoop, calls=%fused_computation.4 | loop fusion | flops 56000 | bytes 156808 | tf_op jit(solution)/shard_map/add | solution.py:626
  (7 shorter events, 0.0 us)
Async XLA Ops:
  1.5 5.6 %collective-permute-start.1 = (bf16[2,16,1536]{2,1,0:T(8,128)(2,1)S(1)}, bf16[2,16,1536]{2,1,0:T(8,128)(2,1)S(1)}, u32[]{:S(2)}, u32[]{:S(2)}) collective-permute-start(bf16[2,16,1536]{2,1,0:T(8,128)(2,1)S(1)} %constant_dynamic-slice_fusion), channel_id=1, source_target_pairs={{1,2},{2,1},{3,4},{4,3},{5,6},{6,5},{7,8},{8,7},{9,10},{10,9},{11,... | collective-permute-start | bytes 294920 | tf_op jit(solution)/shard_map/ppermute | solution.py:569
  5.4 3.4 %collective-permute-start = (bf16[56,1536]{1,0:T(8,128)(2,1)S(1)}, bf16[56,1536]{1,0:T(8,128)(2,1)S(1)}, u32[]{:S(2)}, u32[]{:S(2)}) collective-permute-start(bf16[56,1536]{1,0:T(8,128)(2,1)S(1)} %dynamic-slice_bitcast_fusion), channel_id=1, source_target_pairs={{0,1},{1,0},{2,3},{3,2},{4,5},{5,4},{6,7},{7,6},{8,9},{9,8},{10,11... | collective-permute-start | bytes 516104 | tf_op jit(solution)/shard_map/ppermute | solution.py:410
  7.1 1.8 %collective-permute-start.2 = (bf16[2,16,1536]{2,1,0:T(8,128)(2,1)S(1)}, bf16[2,16,1536]{2,1,0:T(8,128)(2,1)S(1)}, u32[]{:S(2)}, u32[]{:S(2)}) collective-permute-start(bf16[2,16,1536]{2,1,0:T(8,128)(2,1)S(1)} %collective-permute-done.1.near_ref), channel_id=1, source_target_pairs={{0,1},{1,0},{2,3},{3,2},{4,5},{5,4},{6,7},{7,6},{8,9},{9,8},{10,11... | collective-permute-start | bytes 294920 | tf_op jit(solution)/shard_map/ppermute | solution.py:410
  14.8 10.6 %collective-permute-start.8 = (bf16[3,112,128]{2,1,0:T(8,128)(2,1)S(1)}, bf16[3,112,128]{2,1,0:T(8,128)(2,1)S(1)}, u32[]{:S(2)}, u32[]{:S(2)}) collective-permute-start(bf16[3,112,128]{2,1,0:T(8,128)(2,1)S(1)} %get-tuple-element.43), channel_id=1, source_target_pairs={{0,12},{1,13},{2,14},{3,15},{4,8},{5,9},{6,10},{7,11},{8,4},{9,5},... | collective-permute-start | bytes 258056 | tf_op jit(solution)/shard_map/ppermute | solution.py:410
  20.5 35.6 %copy-start = (bf16[1024,1536]{1,0:T(8,128)(2,1)S(1)}, bf16[1024,1536]{1,0:T(8,128)(2,1)}, u32[]{:S(2)}) copy-start(bf16[1024,1536]{1,0:T(8,128)(2,1)} %w_out_ref.1) | copy-start | bytes 9437188
  20.6 35.6 %copy-start.1 = (bf16[1536,100]{0,1:T(8,128)(2,1)S(1)}, bf16[1536,100]{0,1:T(8,128)(2,1)}, u32[]{:S(2)}) copy-start(bf16[1536,100]{0,1:T(8,128)(2,1)} %param.19) | copy-start | bytes 921604
  20.6 39.1 %copy-start.2 = (f32[56,100]{1,0:T(8,128)S(1)}, f32[56,100]{1,0:T(8,128)}, u32[]{:S(2)}) copy-start(f32[56,100]{1,0:T(8,128)} %param.11) | copy-start | bytes 67204
  20.6 7.7 %collective-permute-start.4 = (bf16[3,112,128]{2,1,0:T(8,128)(2,1)S(1)}, bf16[3,112,128]{2,1,0:T(8,128)(2,1)S(1)}, u32[]{:S(2)}, u32[]{:S(2)}) collective-permute-start(bf16[3,112,128]{2,1,0:T(8,128)(2,1)S(1)} %get-tuple-element.39), channel_id=1, source_target_pairs={{0,4},{1,5},{2,6},{3,7},{4,0},{5,1},{6,2},{7,3},{8,12},{9,13},{10,... | collective-permute-start | bytes 258056 | tf_op jit(solution)/shard_map/ppermute | solution.py:410
  21.8 7.4 %collective-permute-start.5 = (bf16[3,112,128]{2,1,0:T(8,128)(2,1)S(1)}, bf16[3,112,128]{2,1,0:T(8,128)(2,1)S(1)}, u32[]{:S(2)}, u32[]{:S(2)}) collective-permute-start(bf16[3,112,128]{2,1,0:T(8,128)(2,1)S(1)} %get-tuple-element.40), channel_id=1, source_target_pairs={{0,6},{1,7},{2,4},{3,5},{4,2},{5,3},{6,0},{7,1},{8,14},{9,15},{10,... | collective-permute-start | bytes 258056 | tf_op jit(solution)/shard_map/ppermute | solution.py:410
  23.8 5.4 %collective-permute-start.3 = (bf16[3,112,128]{2,1,0:T(8,128)(2,1)S(1)}, bf16[3,112,128]{2,1,0:T(8,128)(2,1)S(1)}, u32[]{:S(2)}, u32[]{:S(2)}) collective-permute-start(bf16[3,112,128]{2,1,0:T(8,128)(2,1)S(1)} %get-tuple-element.38), channel_id=1, source_target_pairs={{0,2},{1,3},{2,0},{3,1},{4,6},{5,7},{6,4},{7,5},{8,10},{9,11},{10,... | collective-permute-start | bytes 258056 | tf_op jit(solution)/shard_map/ppermute | solution.py:410
  25.4 9.3 %collective-permute-start.6 = (bf16[3,112,128]{2,1,0:T(8,128)(2,1)S(1)}, bf16[3,112,128]{2,1,0:T(8,128)(2,1)S(1)}, u32[]{:S(2)}, u32[]{:S(2)}) collective-permute-start(bf16[3,112,128]{2,1,0:T(8,128)(2,1)S(1)} %get-tuple-element.41), channel_id=1, source_target_pairs={{0,8},{1,9},{2,10},{3,11},{4,12},{5,13},{6,14},{7,15},{8,0},{9,1},... | collective-permute-start | bytes 258056 | tf_op jit(solution)/shard_map/ppermute | solution.py:410
  25.4 12.1 %collective-permute-start.7 = (bf16[3,112,128]{2,1,0:T(8,128)(2,1)S(1)}, bf16[3,112,128]{2,1,0:T(8,128)(2,1)S(1)}, u32[]{:S(2)}, u32[]{:S(2)}) collective-permute-start(bf16[3,112,128]{2,1,0:T(8,128)(2,1)S(1)} %get-tuple-element.42), channel_id=1, source_target_pairs={{0,10},{1,11},{2,8},{3,9},{4,14},{5,15},{6,12},{7,13},{8,2},{9,3},... | collective-permute-start | bytes 258056 | tf_op jit(solution)/shard_map/ppermute | solution.py:410
  28.2 11.0 %collective-permute-start.9 = (bf16[3,112,128]{2,1,0:T(8,128)(2,1)S(1)}, bf16[3,112,128]{2,1,0:T(8,128)(2,1)S(1)}, u32[]{:S(2)}, u32[]{:S(2)}) collective-permute-start(bf16[3,112,128]{2,1,0:T(8,128)(2,1)S(1)} %get-tuple-element.50), channel_id=1, source_target_pairs={{0,14},{1,15},{2,12},{3,13},{4,10},{5,11},{6,8},{7,9},{8,6},{9,7},... | collective-permute-start | bytes 258056 | tf_op jit(solution)/shard_map/ppermute | solution.py:410
  41.9 7.7 %collective-permute-start.12 = (bf16[2,112,128]{2,1,0:T(8,128)(2,1)S(1)}, bf16[2,112,128]{2,1,0:T(8,128)(2,1)S(1)}, u32[]{:S(2)}, u32[]{:S(2)}) collective-permute-start(bf16[2,112,128]{2,1,0:T(8,128)(2,1)S(1)} %shard_map.122), channel_id=1, source_target_pairs={{0,12},{1,13},{2,14},{3,15},{4,8},{5,9},{6,10},{7,11},{8,4},{9,5},... | collective-permute-start | bytes 172040 | tf_op jit(solution)/shard_map/ppermute | solution.py:410
  45.5 4.3 %collective-permute-start.10 = (bf16[2,112,128]{2,1,0:T(8,128)(2,1)S(1)}, bf16[2,112,128]{2,1,0:T(8,128)(2,1)S(1)}, u32[]{:S(2)}, u32[]{:S(2)}) collective-permute-start(bf16[2,112,128]{2,1,0:T(8,128)(2,1)S(1)} %shard_map.121), channel_id=1, source_target_pairs={{0,4},{1,5},{2,6},{3,7},{4,0},{5,1},{6,2},{7,3},{8,12},{9,13},{10,... | collective-permute-start | bytes 172040 | tf_op jit(solution)/shard_map/ppermute | solution.py:410
  45.6 5.1 %collective-permute-start.11 = (bf16[2,112,128]{2,1,0:T(8,128)(2,1)S(1)}, bf16[2,112,128]{2,1,0:T(8,128)(2,1)S(1)}, u32[]{:S(2)}, u32[]{:S(2)}) collective-permute-start(bf16[2,112,128]{2,1,0:T(8,128)(2,1)S(1)} %get-tuple-element.53), channel_id=1, source_target_pairs={{0,8},{1,9},{2,10},{3,11},{4,12},{5,13},{6,14},{7,15},{8,0},{9,1},... | collective-permute-start | bytes 172040 | tf_op jit(solution)/shard_map/ppermute | solution.py:410
  51.3 4.9 %collective-permute-start.13 = (bf16[4,112,128]{2,1,0:T(8,128)(2,1)S(1)}, bf16[4,112,128]{2,1,0:T(8,128)(2,1)S(1)}, u32[]{:S(2)}, u32[]{:S(2)}) collective-permute-start(bf16[4,112,128]{2,1,0:T(8,128)(2,1)S(1)} %shard_map.123), channel_id=1, source_target_pairs={{0,2},{1,3},{2,0},{3,1},{4,6},{5,7},{6,4},{7,5},{8,10},{9,11},{10,... | collective-permute-start | bytes 344072 | tf_op jit(solution)/shard_map/ppermute | solution.py:410
  58.2 1.5 %collective-permute-start.14 = (f32[56,100]{1,0:T(8,128)S(1)}, f32[56,100]{1,0:T(8,128)S(1)}, u32[]{:S(2)}, u32[]{:S(2)}) collective-permute-start(f32[56,100]{1,0:T(8,128)S(1)} %get-tuple-element.55), channel_id=1, source_target_pairs={{0,1},{1,0},{2,3},{3,2},{4,5},{5,4},{6,7},{7,6},{8,9},{9,8},{10,11... | collective-permute-start | bytes 67208 | tf_op jit(solution)/shard_map/ppermute | solution.py:410

commit v7 on v4

--- a/solution.py
+++ b/solution.py
@@ -286,12 +286,15 @@
     for apart, got_ref in enumerate(got_refs):
         place_keys(info_ref, apart, got_ref, keys, values, apart * rows)
     place_queries(got_refs[1::2], queries)
-    scores = score(queries[...], keys[...])
-    peak = jnp.max(scores, axis=1, keepdims=True)
-    weights = jnp.exp(scores - peak)
-    peak_ref[...] = jnp.broadcast_to(peak, peak_ref.shape)
-    sum_ref[...] = jnp.broadcast_to(jnp.sum(weights, axis=1, keepdims=True), sum_ref.shape)
-    mixed_ref[...] = mix(weights, values[...])
+    half = queries.shape[0] // 2
+    for block in (slice(0, half), slice(half, 2 * half)):
+        scores = score(queries[block, :], keys[...])
+        peak = jnp.max(scores, axis=1, keepdims=True)
+        weights = jnp.exp(scores - peak)
+        peak_ref[block, :] = jnp.broadcast_to(peak, (half, LANES))
+        weight_sum = jnp.sum(weights, axis=1, keepdims=True)
+        sum_ref[block, :] = jnp.broadcast_to(weight_sum, (half, LANES))
+        mixed_ref[block, :] = mix(weights, values[...])
 
 
 def attend_last_kernel(
@@ -542,7 +545,7 @@
         [],
     )
     back, blocks = [staying, crossed], [(0, 0, 0), (1, 0, 1)]
-    apart_first = sorted(range(1, half), reverse=True)
+    apart_first = list(range(half // 2, half)) + list(range(1, half // 2))
     got = {apart: across(joined[apart - 1], 4 * apart, count) for apart in apart_first}
     for apart in range(1, half):
         blocks += [(len(back), side, 2 * apart + side) for side in range(2)]

time: 59.6 us -> 59.5 us (level)
  no operation moved by 1% of the time
where the time goes in v7:
time: 59.5 us; the launch traced here: 59.3 us
  starting transfers between devices  21.2 us (36%)
  Pallas kernels  18.4 us (31%)
  waiting for transfers between devices  14 us (24%)
  between operations  2.84 us (5%)
  local copies, waits for them, and re-layouts  1.86 us (3%)
  other arithmetic  1.01 us (2%)
    pallas_call x10, Pallas kernels, call(): pl.pallas_call(kernel, out_shape=out_shape, in_specs=[smem_spec()] + spec...  18.4 us
    ppermute x14, starting transfers between devices, across(): return lax.ppermute(value, 'seq', [(i, i ^ apart) for i in range(count)])  18.3 us
    ppermute x14, waiting for transfers between devices, across(): return lax.ppermute(value, 'seq', [(i, i ^ apart) for i in range(count)])  13.5 us
    ppermute x1, starting transfers between devices, per_device(): lax.ppermute(edges, ('clip', 'seq'), facing_pairs(lax.axis_size('clip'),...  2.97 us
  transfers between devices with their start and end apart: 15, of which 7 were waited for; matrix products, arithmetic and copies ran while one was open for 2% of the time, Pallas kernels for 14%

profile of v7, /device:TPU:0, one launch (start us, length us, event | category | flops | bytes accessed | tf_op | source)
XLA Modules:
  0.0 59.3 jit_solution(12493823659224916099)
XLA Ops:
  0.6 0.9 %constant_dynamic-slice_fusion = bf16[2,16,1536]{2,1,0:T(8,128)(2,1)S(1)} fusion(bf16[2,56,1536]{2,1,0:T(8,128)(2,1)} %hidden_hbm.1, s32[]{:T(128)S(6)} %select_n.45), kind=kLoop, calls=%fused_computation.15 | loop fusion | bytes 196612 | tf_op jit(solution)/shard_map/dynamic_slice | solution.py:567
  1.5 3.0 %collective-permute-start.1 = (bf16[2,16,1536]{2,1,0:T(8,128)(2,1)S(1)}, bf16[2,16,1536]{2,1,0:T(8,128)(2,1)S(1)}, u32[]{:S(2)}, u32[]{:S(2)}) collective-permute-start(bf16[2,16,1536]{2,1,0:T(8,128)(2,1)S(1)} %constant_dynamic-slice_fusion), channel_id=1, source_target_pairs={{1,2},{2,1},{3,4},{4,3},{5,6},{6,5},{7,8},{8,7},{9,10},{10,9},{11,... | collective-permute-start | bytes 294920 | tf_op jit(solution)/shard_map/ppermute | solution.py:569
  4.5 0.9 %dynamic-slice_bitcast_fusion = bf16[56,1536]{1,0:T(8,128)(2,1)S(1)} fusion(bf16[2,56,1536]{2,1,0:T(8,128)(2,1)} %hidden_hbm.1, s32[]{:T(128)S(6)} %select_n.44), kind=kLoop, calls=%fused_computation | loop fusion | bytes 344068 | tf_op jit(solution)/shard_map/squeeze | solution.py:568
  5.4 0.2 collective-permute-start
  5.7 0.3 fusion
  6.6 0.5 collective-permute-done.1.near_ref
  7.1 0.1 collective-permute-start.2
  7.2 0.1 pad_add_fusion.info_ref
  7.3 1.6 %shard_map.113 = (bf16[56,1536]{1,0:T(8,128)(2,1)S(1)}, f32[31,1536]{1,0:T(8,128)S(1)}, f32[5,1536]{1,0:T(8,128)S(1)}, f32[56,100]{1,0:T(8,128)S(1)}, f32[56,100]{1,0:T(8,128)S(1)}) custom-call(s32[3]{0:T(128)S(1)} %pad_add_fusion.info_ref, bf16[2,56,1536]{2,1,0:T(8,128)(2,1)} %hidden_hbm.1, f32[31,1536]{1,0:T(8,128)} %taps_hbm.1, f32[5,1536]{1,0:T(8,128)} %mod_hbm.1), custom_call_target="tpu_custom_call" | custom-call | tf_op jit(solution)/shard_map/pallas_call | solution.py:373
  8.9 0.0 collective-permute-done.partner_ref
  8.9 0.0 collective-permute-done.2.far_ref
  8.9 4.7 %shard_map.114 = (f32[112,1536]{1,0:T(8,128)S(1)}, bf16[112,1536]{1,0:T(8,128)(2,1)S(1)}, bf16[1536,3072]{1,0:T(8,128)(2,1)S(1)}, bf16[3,112,128]{2,1,0:T(8,128)(2,1)S(1)}, bf16[3,112,128]{2,1,0:T(8,128)(2,1)S(1)}) custom-call(s32[3]{0:T(128)S(1)} %pad_add_fusion.info_ref, bf16[56,1536]{1,0:T(8,128)(2,1)S(1)} %get-tuple-element.34.own_ref, ...), custom_call_target="tpu_custom_call" | custom-call | tf_op jit(solution)/shard_map/pallas_call | solution.py:373
  13.6 1.2 %shard_map.117 = (bf16[3,112,128]{2,1,0:T(8,128)(2,1)S(1)}, bf16[3,112,128]{2,1,0:T(8,128)(2,1)S(1)}) custom-call(s32[3]{0:T(128)S(1)} %pad_add_fusion.info_ref, bf16[112,1536]{1,0:T(8,128)(2,1)S(1)} %get-tuple-element.38.normed_ref, bf16[1536,3072]{1,0:T(8,128)(2,1)S(1)} %get-tuple-element.39.weight_ref, f32[112,128]{1,0:T(8,128)S(1)} %get-tuple-element.65.cos_ref, ...), custom_call_target="tpu_custom_call" | custom-call | tf_op jit(solution)/shard_map/pallas_call | solution.py:373
  14.8 4.5 %collective-permute-start.8 = (bf16[3,112,128]{2,1,0:T(8,128)(2,1)S(1)}, bf16[3,112,128]{2,1,0:T(8,128)(2,1)S(1)}, u32[]{:S(2)}, u32[]{:S(2)}) collective-permute-start(bf16[3,112,128]{2,1,0:T(8,128)(2,1)S(1)} %get-tuple-element.46), channel_id=1, source_target_pairs={{0,12},{1,13},{2,14},{3,15},{4,8},{5,9},{6,10},{7,11},{8,4},{9,5},... | collective-permute-start | bytes 258056 | tf_op jit(solution)/shard_map/ppermute | solution.py:413
  19.3 1.2 %shard_map.116 = (bf16[3,112,128]{2,1,0:T(8,128)(2,1)S(1)}, bf16[3,112,128]{2,1,0:T(8,128)(2,1)S(1)}) custom-call(s32[3]{0:T(128)S(1)} %pad_add_fusion.info_ref, bf16[112,1536]{1,0:T(8,128)(2,1)S(1)} %get-tuple-element.38.normed_ref, bf16[1536,3072]{1,0:T(8,128)(2,1)S(1)} %get-tuple-element.39.weight_ref, f32[112,128]{1,0:T(8,128)S(1)} %get-tuple-element.65.cos_ref, ...), custom_call_target="tpu_custom_call" | custom-call | tf_op jit(solution)/shard_map/pallas_call | solution.py:373
  20.5 0.0 copy-start
  20.6 0.0 copy-start.1
  20.6 0.0 copy-start.2
  20.6 0.1 collective-permute-start.4
  20.7 1.2 %shard_map.115 = (bf16[3,112,128]{2,1,0:T(8,128)(2,1)S(1)}, bf16[3,112,128]{2,1,0:T(8,128)(2,1)S(1)}) custom-call(s32[3]{0:T(128)S(1)} %pad_add_fusion.info_ref, bf16[112,1536]{1,0:T(8,128)(2,1)S(1)} %get-tuple-element.38.normed_ref, bf16[1536,3072]{1,0:T(8,128)(2,1)S(1)} %get-tuple-element.39.weight_ref, f32[112,128]{1,0:T(8,128)S(1)} %get-tuple-element.65.cos_ref, ...), custom_call_target="tpu_custom_call" | custom-call | tf_op jit(solution)/shard_map/pallas_call | solution.py:373
  21.8 2.0 %collective-permute-start.5 = (bf16[3,112,128]{2,1,0:T(8,128)(2,1)S(1)}, bf16[3,112,128]{2,1,0:T(8,128)(2,1)S(1)}, u32[]{:S(2)}, u32[]{:S(2)}) collective-permute-start(bf16[3,112,128]{2,1,0:T(8,128)(2,1)S(1)} %get-tuple-element.43), channel_id=1, source_target_pairs={{0,6},{1,7},{2,4},{3,5},{4,2},{5,3},{6,0},{7,1},{8,14},{9,15},{10,... | collective-permute-start | bytes 258056 | tf_op jit(solution)/shard_map/ppermute | solution.py:413
  23.8 1.6 %collective-permute-start.3 = (bf16[3,112,128]{2,1,0:T(8,128)(2,1)S(1)}, bf16[3,112,128]{2,1,0:T(8,128)(2,1)S(1)}, u32[]{:S(2)}, u32[]{:S(2)}) collective-permute-start(bf16[3,112,128]{2,1,0:T(8,128)(2,1)S(1)} %get-tuple-element.41), channel_id=1, source_target_pairs={{0,2},{1,3},{2,0},{3,1},{4,6},{5,7},{6,4},{7,5},{8,10},{9,11},{10,... | collective-permute-start | bytes 258056 | tf_op jit(solution)/shard_map/ppermute | solution.py:413
  25.4 0.0 collective-permute-start.6
  25.4 0.0 collective-permute-done.8.refs_6_.refs_3_
  25.4 2.8 %collective-permute-start.7 = (bf16[3,112,128]{2,1,0:T(8,128)(2,1)S(1)}, bf16[3,112,128]{2,1,0:T(8,128)(2,1)S(1)}, u32[]{:S(2)}, u32[]{:S(2)}) collective-permute-start(bf16[3,112,128]{2,1,0:T(8,128)(2,1)S(1)} %get-tuple-element.45), channel_id=1, source_target_pairs={{0,10},{1,11},{2,8},{3,9},{4,14},{5,15},{6,12},{7,13},{8,2},{9,3},... | collective-permute-start | bytes 258056 | tf_op jit(solution)/shard_map/ppermute | solution.py:413
  28.2 0.0 collective-permute-done.4.refs_2_.refs_1_
  28.2 1.0 %collective-permute-start.9 = (bf16[3,112,128]{2,1,0:T(8,128)(2,1)S(1)}, bf16[3,112,128]{2,1,0:T(8,128)(2,1)S(1)}, u32[]{:S(2)}, u32[]{:S(2)}) collective-permute-start(bf16[3,112,128]{2,1,0:T(8,128)(2,1)S(1)} %get-tuple-element.53), channel_id=1, source_target_pairs={{0,14},{1,15},{2,12},{3,13},{4,10},{5,11},{6,8},{7,9},{8,6},{9,7},... | collective-permute-start | bytes 258056 | tf_op jit(solution)/shard_map/ppermute | solution.py:413
  29.2 0.0 collective-permute-done.5.refs_3_
  29.2 0.1 collective-permute-done.3.refs_1_
  29.2 5.4 %collective-permute-done.6.refs_4_.refs_2_ = bf16[3,112,128]{2,1,0:T(8,128)(2,1)S(1)} collective-permute-done((bf16[3,112,128]{2,1,0:T(8,128)(2,1)S(1)}, bf16[3,112,128]{2,1,0:T(8,128)(2,1)S(1)}, u32[]{:S(2)}, u32[]{:S(2)}) %collective-permute-start.6) | collective-permute-done | bytes 86048 | tf_op jit(solution)/shard_map/ppermute | solution.py:413
  34.7 2.8 %collective-permute-done.7.refs_5_ = bf16[3,112,128]{2,1,0:T(8,128)(2,1)S(1)} collective-permute-done((bf16[3,112,128]{2,1,0:T(8,128)(2,1)S(1)}, bf16[3,112,128]{2,1,0:T(8,128)(2,1)S(1)}, u32[]{:S(2)}, u32[]{:S(2)}) %collective-permute-start.7) | collective-permute-done | bytes 86048 | tf_op jit(solution)/shard_map/ppermute | solution.py:413
  37.5 2.1 %shard_map.118 = (bf16[784,256]{1,0:T(8,128)(2,1)S(1)}, bf16[784,128]{1,0:T(8,128)(2,1)S(1)}, bf16[672,256]{1,0:T(8,128)(2,1)S(1)}, f32[672,128]{1,0:T(8,128)S(1...) custom-call(s32[3]{0:T(128)S(1)} %pad_add_fusion.info_ref, bf16[3,112,128]{2,1,0:T(8,128)(2,1)S(1)} %get-tuple-element.40.refs_0_, ...), custom_call_target="tpu_custom_call" | custom-call | tf_op jit(solution)/shard_map/pallas_call | solution.py:373
  39.6 0.0 collective-permute-done.9.last_ref
  39.6 1.5 %shard_map.119 = (bf16[4,112,128]{2,1,0:T(8,128)(2,1)S(1)}, bf16[896,256]{1,0:T(8,128)(2,1)S(1)}, bf16[896,128]{1,0:T(8,128)(2,1)S(1)}) custom-call(s32[3]{0:T(128)S(1)} %pad_add_fusion.info_ref, bf16[784,256]{1,0:T(8,128)(2,1)S(1)} %get-tuple-element.47.early_keys, bf16[784,128]{1,0:T(8,128)(2,1)S(1)} %get-tuple-element.48.early_values, ...), custom_call_target="tpu_custom_call" | custom-call | tf_op jit(solution)/shard_map/pallas_call | solution.py:373
  41.2 1.5 %collective-permute-start.10 = (bf16[4,112,128]{2,1,0:T(8,128)(2,1)S(1)}, bf16[4,112,128]{2,1,0:T(8,128)(2,1)S(1)}, u32[]{:S(2)}, u32[]{:S(2)}) collective-permute-start(bf16[4,112,128]{2,1,0:T(8,128)(2,1)S(1)} %get-tuple-element.56), channel_id=1, source_target_pairs={{0,2},{1,3},{2,0},{3,1},{4,6},{5,7},{6,4},{7,5},{8,10},{9,11},{10,... | collective-permute-start | bytes 344072 | tf_op jit(solution)/shard_map/ppermute | solution.py:413
  42.6 2.3 %shard_map.120.own_ref.refs_0_ = bf16[4,112,128]{2,1,0:T(8,128)(2,1)S(1)} custom-call(s32[3]{0:T(128)S(1)} %pad_add_fusion.info_ref, bf16[896,256]{1,0:T(8,128)(2,1)S(1)} %get-tuple-element.54.keys, bf16[896,128]{1,0:T(8,128)(2,1)S(1)} %get-tuple-element.55.values, bf16[3,112,128]{2,1,0:T(8,128)(2,1)S(1)} %get-tuple-element.40.refs_0_, ...), custom_call_target="tpu_custom_call" | custom-call | tf_op jit(solution)/shard_map/pallas_call | solution.py:373
  44.9 1.2 %collective-permute-done.10.got_ref.refs_1_ = bf16[4,112,128]{2,1,0:T(8,128)(2,1)S(1)} collective-permute-done((bf16[4,112,128]{2,1,0:T(8,128)(2,1)S(1)}, bf16[4,112,128]{2,1,0:T(8,128)(2,1)S(1)}, u32[]{:S(2)}, u32[]{:S(2)}) %collective-permute-start.10) | collective-permute-done | bytes 114720 | tf_op jit(solution)/shard_map/ppermute | solution.py:413
  46.2 0.6 shard_map.121
  46.7 0.4 collective-permute-start.11
  47.1 2.0 %collective-permute-start.12 = (bf16[2,112,128]{2,1,0:T(8,128)(2,1)S(1)}, bf16[2,112,128]{2,1,0:T(8,128)(2,1)S(1)}, u32[]{:S(2)}, u32[]{:S(2)}) collective-permute-start(bf16[2,112,128]{2,1,0:T(8,128)(2,1)S(1)} %get-tuple-element.58), channel_id=1, source_target_pairs={{0,8},{1,9},{2,10},{3,11},{4,12},{5,13},{6,14},{7,15},{8,0},{9,1},... | collective-permute-start | bytes 172040 | tf_op jit(solution)/shard_map/ppermute | solution.py:413
  49.1 2.1 %collective-permute-start.13 = (bf16[2,112,128]{2,1,0:T(8,128)(2,1)S(1)}, bf16[2,112,128]{2,1,0:T(8,128)(2,1)S(1)}, u32[]{:S(2)}, u32[]{:S(2)}) collective-permute-start(bf16[2,112,128]{2,1,0:T(8,128)(2,1)S(1)} %get-tuple-element.59), channel_id=1, source_target_pairs={{0,12},{1,13},{2,14},{3,15},{4,8},{5,9},{6,10},{7,11},{8,4},{9,5},... | collective-permute-start | bytes 172040 | tf_op jit(solution)/shard_map/ppermute | solution.py:413
  51.2 0.0 collective-permute-done.11.refs_2_
  51.2 1.4 %collective-permute-done.12.refs_3_ = bf16[2,112,128]{2,1,0:T(8,128)(2,1)S(1)} collective-permute-done((bf16[2,112,128]{2,1,0:T(8,128)(2,1)S(1)}, bf16[2,112,128]{2,1,0:T(8,128)(2,1)S(1)}, u32[]{:S(2)}, u32[]{:S(2)}) %collective-permute-start.12) | collective-permute-done | bytes 57376 | tf_op jit(solution)/shard_map/ppermute | solution.py:413
  52.6 2.5 %collective-permute-done.13.refs_4_ = bf16[2,112,128]{2,1,0:T(8,128)(2,1)S(1)} collective-permute-done((bf16[2,112,128]{2,1,0:T(8,128)(2,1)S(1)}, bf16[2,112,128]{2,1,0:T(8,128)(2,1)S(1)}, u32[]{:S(2)}, u32[]{:S(2)}) %collective-permute-start.13) | collective-permute-done | bytes 57376 | tf_op jit(solution)/shard_map/ppermute | solution.py:413
  55.1 2.0 %shard_map.122 = (f32[56,100]{1,0:T(8,128)S(1)}, f32[56,100]{1,0:T(8,128)S(1)}) custom-call(s32[3]{0:T(128)S(1)} %pad_add_fusion.info_ref, f32[112,1536]{1,0:T(8,128)S(1)} %get-tuple-element.37.residual, bf16[100,1536]{1,0:T(8,128)(2,1)S(1)} %bitcast.8, f32[5,1536]{1,0:T(8,128)S(1)} %get-tuple-element.36.mod_ref, bf16[1024,1536]{1,0:T(8,128)(2,1)S(1)} %copy-done, ...), custom_call_target="tpu_custom_call" | custom-call | tf_op jit(solution)/shard_map/pallas_call | solution.py:373
  57.2 0.1 collective-permute-start.14
  58.6 0.0 collective-permute-done.14
  58.6 0.6 %multiply_add_fusion = (f32[56,100]{1,0:T(8,128)}, f32[56,100]{1,0:T(8,128)}) fusion(f32[56,100]{1,0:T(8,128)S(1)} %copy-done.2, f32[]{:T(128)} %bitcast.5, f32[56,100]{1,0:T(8,128)S(1)} %collective-permute-done.14, f32[56,100]{1,0:T(8,128)S(1)} %get-tuple-element.60, f32[]{:T(128)} %bitcast.7, f32[56,100]{1,0:T(8,128)S(1)} %get-tuple-element.33, ...), kind=kLoop, calls=%fused_computation.4 | loop fusion | flops 56000 | bytes 156808 | tf_op jit(solution)/shard_map/add | solution.py:626
  (5 shorter events, 0.0 us)
Async XLA Ops:
  1.5 5.6 %collective-permute-start.1 = (bf16[2,16,1536]{2,1,0:T(8,128)(2,1)S(1)}, bf16[2,16,1536]{2,1,0:T(8,128)(2,1)S(1)}, u32[]{:S(2)}, u32[]{:S(2)}) collective-permute-start(bf16[2,16,1536]{2,1,0:T(8,128)(2,1)S(1)} %constant_dynamic-slice_fusion), channel_id=1, source_target_pairs={{1,2},{2,1},{3,4},{4,3},{5,6},{6,5},{7,8},{8,7},{9,10},{10,9},{11,... | collective-permute-start | bytes 294920 | tf_op jit(solution)/shard_map/ppermute | solution.py:569
  5.4 3.4 %collective-permute-start = (bf16[56,1536]{1,0:T(8,128)(2,1)S(1)}, bf16[56,1536]{1,0:T(8,128)(2,1)S(1)}, u32[]{:S(2)}, u32[]{:S(2)}) collective-permute-start(bf16[56,1536]{1,0:T(8,128)(2,1)S(1)} %dynamic-slice_bitcast_fusion), channel_id=1, source_target_pairs={{0,1},{1,0},{2,3},{3,2},{4,5},{5,4},{6,7},{7,6},{8,9},{9,8},{10,11... | collective-permute-start | bytes 516104 | tf_op jit(solution)/shard_map/ppermute | solution.py:413
  7.1 1.8 %collective-permute-start.2 = (bf16[2,16,1536]{2,1,0:T(8,128)(2,1)S(1)}, bf16[2,16,1536]{2,1,0:T(8,128)(2,1)S(1)}, u32[]{:S(2)}, u32[]{:S(2)}) collective-permute-start(bf16[2,16,1536]{2,1,0:T(8,128)(2,1)S(1)} %collective-permute-done.1.near_ref), channel_id=1, source_target_pairs={{0,1},{1,0},{2,3},{3,2},{4,5},{5,4},{6,7},{7,6},{8,9},{9,8},{10,11... | collective-permute-start | bytes 294920 | tf_op jit(solution)/shard_map/ppermute | solution.py:413
  14.8 10.6 %collective-permute-start.8 = (bf16[3,112,128]{2,1,0:T(8,128)(2,1)S(1)}, bf16[3,112,128]{2,1,0:T(8,128)(2,1)S(1)}, u32[]{:S(2)}, u32[]{:S(2)}) collective-permute-start(bf16[3,112,128]{2,1,0:T(8,128)(2,1)S(1)} %get-tuple-element.46), channel_id=1, source_target_pairs={{0,12},{1,13},{2,14},{3,15},{4,8},{5,9},{6,10},{7,11},{8,4},{9,5},... | collective-permute-start | bytes 258056 | tf_op jit(solution)/shard_map/ppermute | solution.py:413
  20.5 34.6 %copy-start = (bf16[1024,1536]{1,0:T(8,128)(2,1)S(1)}, bf16[1024,1536]{1,0:T(8,128)(2,1)}, u32[]{:S(2)}) copy-start(bf16[1024,1536]{1,0:T(8,128)(2,1)} %w_out_ref.1) | copy-start | bytes 9437188
  20.6 34.6 %copy-start.1 = (bf16[1536,100]{0,1:T(8,128)(2,1)S(1)}, bf16[1536,100]{0,1:T(8,128)(2,1)}, u32[]{:S(2)}) copy-start(bf16[1536,100]{0,1:T(8,128)(2,1)} %param.19) | copy-start | bytes 921604
  20.6 38.1 %copy-start.2 = (f32[56,100]{1,0:T(8,128)S(1)}, f32[56,100]{1,0:T(8,128)}, u32[]{:S(2)}) copy-start(f32[56,100]{1,0:T(8,128)} %param.11) | copy-start | bytes 67204
  20.6 7.7 %collective-permute-start.4 = (bf16[3,112,128]{2,1,0:T(8,128)(2,1)S(1)}, bf16[3,112,128]{2,1,0:T(8,128)(2,1)S(1)}, u32[]{:S(2)}, u32[]{:S(2)}) collective-permute-start(bf16[3,112,128]{2,1,0:T(8,128)(2,1)S(1)} %get-tuple-element.42), channel_id=1, source_target_pairs={{0,4},{1,5},{2,6},{3,7},{4,0},{5,1},{6,2},{7,3},{8,12},{9,13},{10,... | collective-permute-start | bytes 258056 | tf_op jit(solution)/shard_map/ppermute | solution.py:413
  21.8 7.4 %collective-permute-start.5 = (bf16[3,112,128]{2,1,0:T(8,128)(2,1)S(1)}, bf16[3,112,128]{2,1,0:T(8,128)(2,1)S(1)}, u32[]{:S(2)}, u32[]{:S(2)}) collective-permute-start(bf16[3,112,128]{2,1,0:T(8,128)(2,1)S(1)} %get-tuple-element.43), channel_id=1, source_target_pairs={{0,6},{1,7},{2,4},{3,5},{4,2},{5,3},{6,0},{7,1},{8,14},{9,15},{10,... | collective-permute-start | bytes 258056 | tf_op jit(solution)/shard_map/ppermute | solution.py:413
  23.8 5.4 %collective-permute-start.3 = (bf16[3,112,128]{2,1,0:T(8,128)(2,1)S(1)}, bf16[3,112,128]{2,1,0:T(8,128)(2,1)S(1)}, u32[]{:S(2)}, u32[]{:S(2)}) collective-permute-start(bf16[3,112,128]{2,1,0:T(8,128)(2,1)S(1)} %get-tuple-element.41), channel_id=1, source_target_pairs={{0,2},{1,3},{2,0},{3,1},{4,6},{5,7},{6,4},{7,5},{8,10},{9,11},{10,... | collective-permute-start | bytes 258056 | tf_op jit(solution)/shard_map/ppermute | solution.py:413
  25.4 9.3 %collective-permute-start.6 = (bf16[3,112,128]{2,1,0:T(8,128)(2,1)S(1)}, bf16[3,112,128]{2,1,0:T(8,128)(2,1)S(1)}, u32[]{:S(2)}, u32[]{:S(2)}) collective-permute-start(bf16[3,112,128]{2,1,0:T(8,128)(2,1)S(1)} %get-tuple-element.44), channel_id=1, source_target_pairs={{0,8},{1,9},{2,10},{3,11},{4,12},{5,13},{6,14},{7,15},{8,0},{9,1},... | collective-permute-start | bytes 258056 | tf_op jit(solution)/shard_map/ppermute | solution.py:413
  25.4 12.1 %collective-permute-start.7 = (bf16[3,112,128]{2,1,0:T(8,128)(2,1)S(1)}, bf16[3,112,128]{2,1,0:T(8,128)(2,1)S(1)}, u32[]{:S(2)}, u32[]{:S(2)}) collective-permute-start(bf16[3,112,128]{2,1,0:T(8,128)(2,1)S(1)} %get-tuple-element.45), channel_id=1, source_target_pairs={{0,10},{1,11},{2,8},{3,9},{4,14},{5,15},{6,12},{7,13},{8,2},{9,3},... | collective-permute-start | bytes 258056 | tf_op jit(solution)/shard_map/ppermute | solution.py:413
  28.2 11.4 %collective-permute-start.9 = (bf16[3,112,128]{2,1,0:T(8,128)(2,1)S(1)}, bf16[3,112,128]{2,1,0:T(8,128)(2,1)S(1)}, u32[]{:S(2)}, u32[]{:S(2)}) collective-permute-start(bf16[3,112,128]{2,1,0:T(8,128)(2,1)S(1)} %get-tuple-element.53), channel_id=1, source_target_pairs={{0,14},{1,15},{2,12},{3,13},{4,10},{5,11},{6,8},{7,9},{8,6},{9,7},... | collective-permute-start | bytes 258056 | tf_op jit(solution)/shard_map/ppermute | solution.py:413
  41.2 5.0 %collective-permute-start.10 = (bf16[4,112,128]{2,1,0:T(8,128)(2,1)S(1)}, bf16[4,112,128]{2,1,0:T(8,128)(2,1)S(1)}, u32[]{:S(2)}, u32[]{:S(2)}) collective-permute-start(bf16[4,112,128]{2,1,0:T(8,128)(2,1)S(1)} %get-tuple-element.56), channel_id=1, source_target_pairs={{0,2},{1,3},{2,0},{3,1},{4,6},{5,7},{6,4},{7,5},{8,10},{9,11},{10,... | collective-permute-start | bytes 344072 | tf_op jit(solution)/shard_map/ppermute | solution.py:413
  46.7 4.5 %collective-permute-start.11 = (bf16[2,112,128]{2,1,0:T(8,128)(2,1)S(1)}, bf16[2,112,128]{2,1,0:T(8,128)(2,1)S(1)}, u32[]{:S(2)}, u32[]{:S(2)}) collective-permute-start(bf16[2,112,128]{2,1,0:T(8,128)(2,1)S(1)} %get-tuple-element.57), channel_id=1, source_target_pairs={{0,4},{1,5},{2,6},{3,7},{4,0},{5,1},{6,2},{7,3},{8,12},{9,13},{10,... | collective-permute-start | bytes 172040 | tf_op jit(solution)/shard_map/ppermute | solution.py:413
  47.1 5.5 %collective-permute-start.12 = (bf16[2,112,128]{2,1,0:T(8,128)(2,1)S(1)}, bf16[2,112,128]{2,1,0:T(8,128)(2,1)S(1)}, u32[]{:S(2)}, u32[]{:S(2)}) collective-permute-start(bf16[2,112,128]{2,1,0:T(8,128)(2,1)S(1)} %get-tuple-element.58), channel_id=1, source_target_pairs={{0,8},{1,9},{2,10},{3,11},{4,12},{5,13},{6,14},{7,15},{8,0},{9,1},... | collective-permute-start | bytes 172040 | tf_op jit(solution)/shard_map/ppermute | solution.py:413
  49.1 6.0 %collective-permute-start.13 = (bf16[2,112,128]{2,1,0:T(8,128)(2,1)S(1)}, bf16[2,112,128]{2,1,0:T(8,128)(2,1)S(1)}, u32[]{:S(2)}, u32[]{:S(2)}) collective-permute-start(bf16[2,112,128]{2,1,0:T(8,128)(2,1)S(1)} %get-tuple-element.59), channel_id=1, source_target_pairs={{0,12},{1,13},{2,14},{3,15},{4,8},{5,9},{6,10},{7,11},{8,4},{9,5},... | collective-permute-start | bytes 172040 | tf_op jit(solution)/shard_map/ppermute | solution.py:413
  57.2 1.5 %collective-permute-start.14 = (f32[56,100]{1,0:T(8,128)S(1)}, f32[56,100]{1,0:T(8,128)S(1)}, u32[]{:S(2)}, u32[]{:S(2)}) collective-permute-start(f32[56,100]{1,0:T(8,128)S(1)} %get-tuple-element.61), channel_id=1, source_target_pairs={{0,1},{1,0},{2,3},{3,2},{4,5},{5,4},{6,7},{7,6},{8,9},{9,8},{10,11... | collective-permute-start | bytes 67208 | tf_op jit(solution)/shard_map/ppermute | solution.py:413

commit v8 on v7

--- a/solution.py
+++ b/solution.py
@@ -545,8 +545,9 @@
         [],
     )
     back, blocks = [staying, crossed], [(0, 0, 0), (1, 0, 1)]
-    apart_first = list(range(half // 2, half)) + list(range(1, half // 2))
-    got = {apart: across(joined[apart - 1], 4 * apart, count) for apart in apart_first}
+    got = {}
+    for apart in range(1, half):
+        got[apart] = across(joined[apart - 1], 4 * apart, count)
     for apart in range(1, half):
         blocks += [(len(back), side, 2 * apart + side) for side in range(2)]
         back.append(got[apart])

time: 59.5 us -> 59.5 us (level)
  no operation moved by 1% of the time
where the time goes in v8:
time: 59.5 us; the launch traced here: 59.3 us
  starting transfers between devices  21.2 us (36%)
  Pallas kernels  18.4 us (31%)
  waiting for transfers between devices  14 us (24%)
  between operations  2.84 us (5%)
  local copies, waits for them, and re-layouts  1.86 us (3%)
  other arithmetic  1.01 us (2%)
    pallas_call x10, Pallas kernels, call(): pl.pallas_call(kernel, out_shape=out_shape, in_specs=[smem_spec()] + spec...  18.4 us
    ppermute x14, starting transfers between devices, across(): return lax.ppermute(value, 'seq', [(i, i ^ apart) for i in range(count)])  18.3 us
    ppermute x14, waiting for transfers between devices, across(): return lax.ppermute(value, 'seq', [(i, i ^ apart) for i in range(count)])  13.5 us
    ppermute x1, starting transfers between devices, per_device(): lax.ppermute(edges, ('clip', 'seq'), facing_pairs(lax.axis_size('clip'),...  2.97 us
  transfers between devices with their start and end apart: 15, of which 7 were waited for; matrix products, arithmetic and copies ran while one was open for 2% of the time, Pallas kernels for 14%

profile of v8, /device:TPU:0, one launch (start us, length us, event | category | flops | bytes accessed | tf_op | source)
XLA Modules:
  0.0 59.3 jit_solution(12493823659224916099)
XLA Ops:
  0.6 0.9 %constant_dynamic-slice_fusion = bf16[2,16,1536]{2,1,0:T(8,128)(2,1)S(1)} fusion(bf16[2,56,1536]{2,1,0:T(8,128)(2,1)} %hidden_hbm.1, s32[]{:T(128)S(6)} %select_n.45), kind=kLoop, calls=%fused_computation.15 | loop fusion | bytes 196612 | tf_op jit(solution)/shard_map/dynamic_slice | solution.py:568
  1.5 3.0 %collective-permute-start.1 = (bf16[2,16,1536]{2,1,0:T(8,128)(2,1)S(1)}, bf16[2,16,1536]{2,1,0:T(8,128)(2,1)S(1)}, u32[]{:S(2)}, u32[]{:S(2)}) collective-permute-start(bf16[2,16,1536]{2,1,0:T(8,128)(2,1)S(1)} %constant_dynamic-slice_fusion), channel_id=1, source_target_pairs={{1,2},{2,1},{3,4},{4,3},{5,6},{6,5},{7,8},{8,7},{9,10},{10,9},{11,... | collective-permute-start | bytes 294920 | tf_op jit(solution)/shard_map/ppermute | solution.py:570
  4.5 0.9 %dynamic-slice_bitcast_fusion = bf16[56,1536]{1,0:T(8,128)(2,1)S(1)} fusion(bf16[2,56,1536]{2,1,0:T(8,128)(2,1)} %hidden_hbm.1, s32[]{:T(128)S(6)} %select_n.44), kind=kLoop, calls=%fused_computation | loop fusion | bytes 344068 | tf_op jit(solution)/shard_map/squeeze | solution.py:569
  5.4 0.2 collective-permute-start
  5.7 0.3 fusion
  6.6 0.5 collective-permute-done.1.near_ref
  7.1 0.1 collective-permute-start.2
  7.2 0.1 pad_add_fusion.info_ref
  7.3 1.6 %shard_map.113 = (bf16[56,1536]{1,0:T(8,128)(2,1)S(1)}, f32[31,1536]{1,0:T(8,128)S(1)}, f32[5,1536]{1,0:T(8,128)S(1)}, f32[56,100]{1,0:T(8,128)S(1)}, f32[56,100]{1,0:T(8,128)S(1)}) custom-call(s32[3]{0:T(128)S(1)} %pad_add_fusion.info_ref, bf16[2,56,1536]{2,1,0:T(8,128)(2,1)} %hidden_hbm.1, f32[31,1536]{1,0:T(8,128)} %taps_hbm.1, f32[5,1536]{1,0:T(8,128)} %mod_hbm.1), custom_call_target="tpu_custom_call" | custom-call | tf_op jit(solution)/shard_map/pallas_call | solution.py:373
  8.9 0.0 collective-permute-done.partner_ref
  8.9 0.0 collective-permute-done.2.far_ref
  8.9 4.7 %shard_map.114 = (f32[112,1536]{1,0:T(8,128)S(1)}, bf16[112,1536]{1,0:T(8,128)(2,1)S(1)}, bf16[1536,3072]{1,0:T(8,128)(2,1)S(1)}, bf16[3,112,128]{2,1,0:T(8,128)(2,1)S(1)}, bf16[3,112,128]{2,1,0:T(8,128)(2,1)S(1)}) custom-call(s32[3]{0:T(128)S(1)} %pad_add_fusion.info_ref, bf16[56,1536]{1,0:T(8,128)(2,1)S(1)} %get-tuple-element.34.own_ref, ...), custom_call_target="tpu_custom_call" | custom-call | tf_op jit(solution)/shard_map/pallas_call | solution.py:373
  13.6 1.2 %shard_map.117 = (bf16[3,112,128]{2,1,0:T(8,128)(2,1)S(1)}, bf16[3,112,128]{2,1,0:T(8,128)(2,1)S(1)}) custom-call(s32[3]{0:T(128)S(1)} %pad_add_fusion.info_ref, bf16[112,1536]{1,0:T(8,128)(2,1)S(1)} %get-tuple-element.38.normed_ref, bf16[1536,3072]{1,0:T(8,128)(2,1)S(1)} %get-tuple-element.39.weight_ref, f32[112,128]{1,0:T(8,128)S(1)} %get-tuple-element.65.cos_ref, ...), custom_call_target="tpu_custom_call" | custom-call | tf_op jit(solution)/shard_map/pallas_call | solution.py:373
  14.8 4.5 %collective-permute-start.8 = (bf16[3,112,128]{2,1,0:T(8,128)(2,1)S(1)}, bf16[3,112,128]{2,1,0:T(8,128)(2,1)S(1)}, u32[]{:S(2)}, u32[]{:S(2)}) collective-permute-start(bf16[3,112,128]{2,1,0:T(8,128)(2,1)S(1)} %get-tuple-element.46), channel_id=1, source_target_pairs={{0,12},{1,13},{2,14},{3,15},{4,8},{5,9},{6,10},{7,11},{8,4},{9,5},... | collective-permute-start | bytes 258056 | tf_op jit(solution)/shard_map/ppermute | solution.py:413
  19.3 1.2 %shard_map.116 = (bf16[3,112,128]{2,1,0:T(8,128)(2,1)S(1)}, bf16[3,112,128]{2,1,0:T(8,128)(2,1)S(1)}) custom-call(s32[3]{0:T(128)S(1)} %pad_add_fusion.info_ref, bf16[112,1536]{1,0:T(8,128)(2,1)S(1)} %get-tuple-element.38.normed_ref, bf16[1536,3072]{1,0:T(8,128)(2,1)S(1)} %get-tuple-element.39.weight_ref, f32[112,128]{1,0:T(8,128)S(1)} %get-tuple-element.65.cos_ref, ...), custom_call_target="tpu_custom_call" | custom-call | tf_op jit(solution)/shard_map/pallas_call | solution.py:373
  20.5 0.0 copy-start
  20.6 0.0 copy-start.1
  20.6 0.0 copy-start.2
  20.6 0.1 collective-permute-start.4
  20.7 1.2 %shard_map.115 = (bf16[3,112,128]{2,1,0:T(8,128)(2,1)S(1)}, bf16[3,112,128]{2,1,0:T(8,128)(2,1)S(1)}) custom-call(s32[3]{0:T(128)S(1)} %pad_add_fusion.info_ref, bf16[112,1536]{1,0:T(8,128)(2,1)S(1)} %get-tuple-element.38.normed_ref, bf16[1536,3072]{1,0:T(8,128)(2,1)S(1)} %get-tuple-element.39.weight_ref, f32[112,128]{1,0:T(8,128)S(1)} %get-tuple-element.65.cos_ref, ...), custom_call_target="tpu_custom_call" | custom-call | tf_op jit(solution)/shard_map/pallas_call | solution.py:373
  21.8 2.0 %collective-permute-start.5 = (bf16[3,112,128]{2,1,0:T(8,128)(2,1)S(1)}, bf16[3,112,128]{2,1,0:T(8,128)(2,1)S(1)}, u32[]{:S(2)}, u32[]{:S(2)}) collective-permute-start(bf16[3,112,128]{2,1,0:T(8,128)(2,1)S(1)} %get-tuple-element.43), channel_id=1, source_target_pairs={{0,6},{1,7},{2,4},{3,5},{4,2},{5,3},{6,0},{7,1},{8,14},{9,15},{10,... | collective-permute-start | bytes 258056 | tf_op jit(solution)/shard_map/ppermute | solution.py:413
  23.8 1.6 %collective-permute-start.3 = (bf16[3,112,128]{2,1,0:T(8,128)(2,1)S(1)}, bf16[3,112,128]{2,1,0:T(8,128)(2,1)S(1)}, u32[]{:S(2)}, u32[]{:S(2)}) collective-permute-start(bf16[3,112,128]{2,1,0:T(8,128)(2,1)S(1)} %get-tuple-element.41), channel_id=1, source_target_pairs={{0,2},{1,3},{2,0},{3,1},{4,6},{5,7},{6,4},{7,5},{8,10},{9,11},{10,... | collective-permute-start | bytes 258056 | tf_op jit(solution)/shard_map/ppermute | solution.py:413
  25.4 0.0 collective-permute-start.6
  25.4 0.0 collective-permute-done.8.refs_6_.refs_3_
  25.4 2.8 %collective-permute-start.7 = (bf16[3,112,128]{2,1,0:T(8,128)(2,1)S(1)}, bf16[3,112,128]{2,1,0:T(8,128)(2,1)S(1)}, u32[]{:S(2)}, u32[]{:S(2)}) collective-permute-start(bf16[3,112,128]{2,1,0:T(8,128)(2,1)S(1)} %get-tuple-element.45), channel_id=1, source_target_pairs={{0,10},{1,11},{2,8},{3,9},{4,14},{5,15},{6,12},{7,13},{8,2},{9,3},... | collective-permute-start | bytes 258056 | tf_op jit(solution)/shard_map/ppermute | solution.py:413
  28.2 0.0 collective-permute-done.4.refs_2_.refs_1_
  28.2 1.0 %collective-permute-start.9 = (bf16[3,112,128]{2,1,0:T(8,128)(2,1)S(1)}, bf16[3,112,128]{2,1,0:T(8,128)(2,1)S(1)}, u32[]{:S(2)}, u32[]{:S(2)}) collective-permute-start(bf16[3,112,128]{2,1,0:T(8,128)(2,1)S(1)} %get-tuple-element.53), channel_id=1, source_target_pairs={{0,14},{1,15},{2,12},{3,13},{4,10},{5,11},{6,8},{7,9},{8,6},{9,7},... | collective-permute-start | bytes 258056 | tf_op jit(solution)/shard_map/ppermute | solution.py:413
  29.2 0.0 collective-permute-done.5.refs_3_
  29.2 0.1 collective-permute-done.3.refs_1_
  29.2 5.4 %collective-permute-done.6.refs_4_.refs_2_ = bf16[3,112,128]{2,1,0:T(8,128)(2,1)S(1)} collective-permute-done((bf16[3,112,128]{2,1,0:T(8,128)(2,1)S(1)}, bf16[3,112,128]{2,1,0:T(8,128)(2,1)S(1)}, u32[]{:S(2)}, u32[]{:S(2)}) %collective-permute-start.6) | collective-permute-done | bytes 86048 | tf_op jit(solution)/shard_map/ppermute | solution.py:413
  34.7 2.8 %collective-permute-done.7.refs_5_ = bf16[3,112,128]{2,1,0:T(8,128)(2,1)S(1)} collective-permute-done((bf16[3,112,128]{2,1,0:T(8,128)(2,1)S(1)}, bf16[3,112,128]{2,1,0:T(8,128)(2,1)S(1)}, u32[]{:S(2)}, u32[]{:S(2)}) %collective-permute-start.7) | collective-permute-done | bytes 86048 | tf_op jit(solution)/shard_map/ppermute | solution.py:413
  37.5 2.1 %shard_map.118 = (bf16[784,256]{1,0:T(8,128)(2,1)S(1)}, bf16[784,128]{1,0:T(8,128)(2,1)S(1)}, bf16[672,256]{1,0:T(8,128)(2,1)S(1)}, f32[672,128]{1,0:T(8,128)S(1...) custom-call(s32[3]{0:T(128)S(1)} %pad_add_fusion.info_ref, bf16[3,112,128]{2,1,0:T(8,128)(2,1)S(1)} %get-tuple-element.40.refs_0_, ...), custom_call_target="tpu_custom_call" | custom-call | tf_op jit(solution)/shard_map/pallas_call | solution.py:373
  39.6 0.0 collective-permute-done.9.last_ref
  39.6 1.5 %shard_map.119 = (bf16[4,112,128]{2,1,0:T(8,128)(2,1)S(1)}, bf16[896,256]{1,0:T(8,128)(2,1)S(1)}, bf16[896,128]{1,0:T(8,128)(2,1)S(1)}) custom-call(s32[3]{0:T(128)S(1)} %pad_add_fusion.info_ref, bf16[784,256]{1,0:T(8,128)(2,1)S(1)} %get-tuple-element.47.early_keys, bf16[784,128]{1,0:T(8,128)(2,1)S(1)} %get-tuple-element.48.early_values, ...), custom_call_target="tpu_custom_call" | custom-call | tf_op jit(solution)/shard_map/pallas_call | solution.py:373
  41.2 1.5 %collective-permute-start.10 = (bf16[4,112,128]{2,1,0:T(8,128)(2,1)S(1)}, bf16[4,112,128]{2,1,0:T(8,128)(2,1)S(1)}, u32[]{:S(2)}, u32[]{:S(2)}) collective-permute-start(bf16[4,112,128]{2,1,0:T(8,128)(2,1)S(1)} %get-tuple-element.56), channel_id=1, source_target_pairs={{0,2},{1,3},{2,0},{3,1},{4,6},{5,7},{6,4},{7,5},{8,10},{9,11},{10,... | collective-permute-start | bytes 344072 | tf_op jit(solution)/shard_map/ppermute | solution.py:413
  42.6 2.3 %shard_map.120.own_ref.refs_0_ = bf16[4,112,128]{2,1,0:T(8,128)(2,1)S(1)} custom-call(s32[3]{0:T(128)S(1)} %pad_add_fusion.info_ref, bf16[896,256]{1,0:T(8,128)(2,1)S(1)} %get-tuple-element.54.keys, bf16[896,128]{1,0:T(8,128)(2,1)S(1)} %get-tuple-element.55.values, bf16[3,112,128]{2,1,0:T(8,128)(2,1)S(1)} %get-tuple-element.40.refs_0_, ...), custom_call_target="tpu_custom_call" | custom-call | tf_op jit(solution)/shard_map/pallas_call | solution.py:373
  44.9 1.2 %collective-permute-done.10.got_ref.refs_1_ = bf16[4,112,128]{2,1,0:T(8,128)(2,1)S(1)} collective-permute-done((bf16[4,112,128]{2,1,0:T(8,128)(2,1)S(1)}, bf16[4,112,128]{2,1,0:T(8,128)(2,1)S(1)}, u32[]{:S(2)}, u32[]{:S(2)}) %collective-permute-start.10) | collective-permute-done | bytes 114720 | tf_op jit(solution)/shard_map/ppermute | solution.py:413
  46.2 0.6 shard_map.121
  46.7 0.4 collective-permute-start.11
  47.1 2.0 %collective-permute-start.12 = (bf16[2,112,128]{2,1,0:T(8,128)(2,1)S(1)}, bf16[2,112,128]{2,1,0:T(8,128)(2,1)S(1)}, u32[]{:S(2)}, u32[]{:S(2)}) collective-permute-start(bf16[2,112,128]{2,1,0:T(8,128)(2,1)S(1)} %get-tuple-element.58), channel_id=1, source_target_pairs={{0,8},{1,9},{2,10},{3,11},{4,12},{5,13},{6,14},{7,15},{8,0},{9,1},... | collective-permute-start | bytes 172040 | tf_op jit(solution)/shard_map/ppermute | solution.py:413
  49.1 2.1 %collective-permute-start.13 = (bf16[2,112,128]{2,1,0:T(8,128)(2,1)S(1)}, bf16[2,112,128]{2,1,0:T(8,128)(2,1)S(1)}, u32[]{:S(2)}, u32[]{:S(2)}) collective-permute-start(bf16[2,112,128]{2,1,0:T(8,128)(2,1)S(1)} %get-tuple-element.59), channel_id=1, source_target_pairs={{0,12},{1,13},{2,14},{3,15},{4,8},{5,9},{6,10},{7,11},{8,4},{9,5},... | collective-permute-start | bytes 172040 | tf_op jit(solution)/shard_map/ppermute | solution.py:413
  51.2 0.0 collective-permute-done.11.refs_2_
  51.2 1.4 %collective-permute-done.12.refs_3_ = bf16[2,112,128]{2,1,0:T(8,128)(2,1)S(1)} collective-permute-done((bf16[2,112,128]{2,1,0:T(8,128)(2,1)S(1)}, bf16[2,112,128]{2,1,0:T(8,128)(2,1)S(1)}, u32[]{:S(2)}, u32[]{:S(2)}) %collective-permute-start.12) | collective-permute-done | bytes 57376 | tf_op jit(solution)/shard_map/ppermute | solution.py:413
  52.6 2.5 %collective-permute-done.13.refs_4_ = bf16[2,112,128]{2,1,0:T(8,128)(2,1)S(1)} collective-permute-done((bf16[2,112,128]{2,1,0:T(8,128)(2,1)S(1)}, bf16[2,112,128]{2,1,0:T(8,128)(2,1)S(1)}, u32[]{:S(2)}, u32[]{:S(2)}) %collective-permute-start.13) | collective-permute-done | bytes 57376 | tf_op jit(solution)/shard_map/ppermute | solution.py:413
  55.1 2.0 %shard_map.122 = (f32[56,100]{1,0:T(8,128)S(1)}, f32[56,100]{1,0:T(8,128)S(1)}) custom-call(s32[3]{0:T(128)S(1)} %pad_add_fusion.info_ref, f32[112,1536]{1,0:T(8,128)S(1)} %get-tuple-element.37.residual, bf16[100,1536]{1,0:T(8,128)(2,1)S(1)} %bitcast.8, f32[5,1536]{1,0:T(8,128)S(1)} %get-tuple-element.36.mod_ref, bf16[1024,1536]{1,0:T(8,128)(2,1)S(1)} %copy-done, ...), custom_call_target="tpu_custom_call" | custom-call | tf_op jit(solution)/shard_map/pallas_call | solution.py:373
  57.2 0.1 collective-permute-start.14
  58.6 0.0 collective-permute-done.14
  58.6 0.6 %multiply_add_fusion = (f32[56,100]{1,0:T(8,128)}, f32[56,100]{1,0:T(8,128)}) fusion(f32[56,100]{1,0:T(8,128)S(1)} %copy-done.2, f32[]{:T(128)} %bitcast.5, f32[56,100]{1,0:T(8,128)S(1)} %collective-permute-done.14, f32[56,100]{1,0:T(8,128)S(1)} %get-tuple-element.60, f32[]{:T(128)} %bitcast.7, f32[56,100]{1,0:T(8,128)S(1)} %get-tuple-element.33, ...), kind=kLoop, calls=%fused_computation.4 | loop fusion | flops 56000 | bytes 156808 | tf_op jit(solution)/shard_map/add | solution.py:627
  (5 shorter events, 0.0 us)
Async XLA Ops:
  1.5 5.6 %collective-permute-start.1 = (bf16[2,16,1536]{2,1,0:T(8,128)(2,1)S(1)}, bf16[2,16,1536]{2,1,0:T(8,128)(2,1)S(1)}, u32[]{:S(2)}, u32[]{:S(2)}) collective-permute-start(bf16[2,16,1536]{2,1,0:T(8,128)(2,1)S(1)} %constant_dynamic-slice_fusion), channel_id=1, source_target_pairs={{1,2},{2,1},{3,4},{4,3},{5,6},{6,5},{7,8},{8,7},{9,10},{10,9},{11,... | collective-permute-start | bytes 294920 | tf_op jit(solution)/shard_map/ppermute | solution.py:570
  5.4 3.4 %collective-permute-start = (bf16[56,1536]{1,0:T(8,128)(2,1)S(1)}, bf16[56,1536]{1,0:T(8,128)(2,1)S(1)}, u32[]{:S(2)}, u32[]{:S(2)}) collective-permute-start(bf16[56,1536]{1,0:T(8,128)(2,1)S(1)} %dynamic-slice_bitcast_fusion), channel_id=1, source_target_pairs={{0,1},{1,0},{2,3},{3,2},{4,5},{5,4},{6,7},{7,6},{8,9},{9,8},{10,11... | collective-permute-start | bytes 516104 | tf_op jit(solution)/shard_map/ppermute | solution.py:413
  7.1 1.8 %collective-permute-start.2 = (bf16[2,16,1536]{2,1,0:T(8,128)(2,1)S(1)}, bf16[2,16,1536]{2,1,0:T(8,128)(2,1)S(1)}, u32[]{:S(2)}, u32[]{:S(2)}) collective-permute-start(bf16[2,16,1536]{2,1,0:T(8,128)(2,1)S(1)} %collective-permute-done.1.near_ref), channel_id=1, source_target_pairs={{0,1},{1,0},{2,3},{3,2},{4,5},{5,4},{6,7},{7,6},{8,9},{9,8},{10,11... | collective-permute-start | bytes 294920 | tf_op jit(solution)/shard_map/ppermute | solution.py:413
  14.8 10.6 %collective-permute-start.8 = (bf16[3,112,128]{2,1,0:T(8,128)(2,1)S(1)}, bf16[3,112,128]{2,1,0:T(8,128)(2,1)S(1)}, u32[]{:S(2)}, u32[]{:S(2)}) collective-permute-start(bf16[3,112,128]{2,1,0:T(8,128)(2,1)S(1)} %get-tuple-element.46), channel_id=1, source_target_pairs={{0,12},{1,13},{2,14},{3,15},{4,8},{5,9},{6,10},{7,11},{8,4},{9,5},... | collective-permute-start | bytes 258056 | tf_op jit(solution)/shard_map/ppermute | solution.py:413
  20.5 34.6 %copy-start = (bf16[1024,1536]{1,0:T(8,128)(2,1)S(1)}, bf16[1024,1536]{1,0:T(8,128)(2,1)}, u32[]{:S(2)}) copy-start(bf16[1024,1536]{1,0:T(8,128)(2,1)} %w_out_ref.1) | copy-start | bytes 9437188
  20.6 34.6 %copy-start.1 = (bf16[1536,100]{0,1:T(8,128)(2,1)S(1)}, bf16[1536,100]{0,1:T(8,128)(2,1)}, u32[]{:S(2)}) copy-start(bf16[1536,100]{0,1:T(8,128)(2,1)} %param.19) | copy-start | bytes 921604
  20.6 38.1 %copy-start.2 = (f32[56,100]{1,0:T(8,128)S(1)}, f32[56,100]{1,0:T(8,128)}, u32[]{:S(2)}) copy-start(f32[56,100]{1,0:T(8,128)} %param.11) | copy-start | bytes 67204
  20.6 7.7 %collective-permute-start.4 = (bf16[3,112,128]{2,1,0:T(8,128)(2,1)S(1)}, bf16[3,112,128]{2,1,0:T(8,128)(2,1)S(1)}, u32[]{:S(2)}, u32[]{:S(2)}) collective-permute-start(bf16[3,112,128]{2,1,0:T(8,128)(2,1)S(1)} %get-tuple-element.42), channel_id=1, source_target_pairs={{0,4},{1,5},{2,6},{3,7},{4,0},{5,1},{6,2},{7,3},{8,12},{9,13},{10,... | collective-permute-start | bytes 258056 | tf_op jit(solution)/shard_map/ppermute | solution.py:413
  21.8 7.4 %collective-permute-start.5 = (bf16[3,112,128]{2,1,0:T(8,128)(2,1)S(1)}, bf16[3,112,128]{2,1,0:T(8,128)(2,1)S(1)}, u32[]{:S(2)}, u32[]{:S(2)}) collective-permute-start(bf16[3,112,128]{2,1,0:T(8,128)(2,1)S(1)} %get-tuple-element.43), channel_id=1, source_target_pairs={{0,6},{1,7},{2,4},{3,5},{4,2},{5,3},{6,0},{7,1},{8,14},{9,15},{10,... | collective-permute-start | bytes 258056 | tf_op jit(solution)/shard_map/ppermute | solution.py:413
  23.8 5.4 %collective-permute-start.3 = (bf16[3,112,128]{2,1,0:T(8,128)(2,1)S(1)}, bf16[3,112,128]{2,1,0:T(8,128)(2,1)S(1)}, u32[]{:S(2)}, u32[]{:S(2)}) collective-permute-start(bf16[3,112,128]{2,1,0:T(8,128)(2,1)S(1)} %get-tuple-element.41), channel_id=1, source_target_pairs={{0,2},{1,3},{2,0},{3,1},{4,6},{5,7},{6,4},{7,5},{8,10},{9,11},{10,... | collective-permute-start | bytes 258056 | tf_op jit(solution)/shard_map/ppermute | solution.py:413
  25.4 9.3 %collective-permute-start.6 = (bf16[3,112,128]{2,1,0:T(8,128)(2,1)S(1)}, bf16[3,112,128]{2,1,0:T(8,128)(2,1)S(1)}, u32[]{:S(2)}, u32[]{:S(2)}) collective-permute-start(bf16[3,112,128]{2,1,0:T(8,128)(2,1)S(1)} %get-tuple-element.44), channel_id=1, source_target_pairs={{0,8},{1,9},{2,10},{3,11},{4,12},{5,13},{6,14},{7,15},{8,0},{9,1},... | collective-permute-start | bytes 258056 | tf_op jit(solution)/shard_map/ppermute | solution.py:413
  25.4 12.1 %collective-permute-start.7 = (bf16[3,112,128]{2,1,0:T(8,128)(2,1)S(1)}, bf16[3,112,128]{2,1,0:T(8,128)(2,1)S(1)}, u32[]{:S(2)}, u32[]{:S(2)}) collective-permute-start(bf16[3,112,128]{2,1,0:T(8,128)(2,1)S(1)} %get-tuple-element.45), channel_id=1, source_target_pairs={{0,10},{1,11},{2,8},{3,9},{4,14},{5,15},{6,12},{7,13},{8,2},{9,3},... | collective-permute-start | bytes 258056 | tf_op jit(solution)/shard_map/ppermute | solution.py:413
  28.2 11.4 %collective-permute-start.9 = (bf16[3,112,128]{2,1,0:T(8,128)(2,1)S(1)}, bf16[3,112,128]{2,1,0:T(8,128)(2,1)S(1)}, u32[]{:S(2)}, u32[]{:S(2)}) collective-permute-start(bf16[3,112,128]{2,1,0:T(8,128)(2,1)S(1)} %get-tuple-element.53), channel_id=1, source_target_pairs={{0,14},{1,15},{2,12},{3,13},{4,10},{5,11},{6,8},{7,9},{8,6},{9,7},... | collective-permute-start | bytes 258056 | tf_op jit(solution)/shard_map/ppermute | solution.py:413
  41.2 5.0 %collective-permute-start.10 = (bf16[4,112,128]{2,1,0:T(8,128)(2,1)S(1)}, bf16[4,112,128]{2,1,0:T(8,128)(2,1)S(1)}, u32[]{:S(2)}, u32[]{:S(2)}) collective-permute-start(bf16[4,112,128]{2,1,0:T(8,128)(2,1)S(1)} %get-tuple-element.56), channel_id=1, source_target_pairs={{0,2},{1,3},{2,0},{3,1},{4,6},{5,7},{6,4},{7,5},{8,10},{9,11},{10,... | collective-permute-start | bytes 344072 | tf_op jit(solution)/shard_map/ppermute | solution.py:413
  46.7 4.5 %collective-permute-start.11 = (bf16[2,112,128]{2,1,0:T(8,128)(2,1)S(1)}, bf16[2,112,128]{2,1,0:T(8,128)(2,1)S(1)}, u32[]{:S(2)}, u32[]{:S(2)}) collective-permute-start(bf16[2,112,128]{2,1,0:T(8,128)(2,1)S(1)} %get-tuple-element.57), channel_id=1, source_target_pairs={{0,4},{1,5},{2,6},{3,7},{4,0},{5,1},{6,2},{7,3},{8,12},{9,13},{10,... | collective-permute-start | bytes 172040 | tf_op jit(solution)/shard_map/ppermute | solution.py:413
  47.1 5.5 %collective-permute-start.12 = (bf16[2,112,128]{2,1,0:T(8,128)(2,1)S(1)}, bf16[2,112,128]{2,1,0:T(8,128)(2,1)S(1)}, u32[]{:S(2)}, u32[]{:S(2)}) collective-permute-start(bf16[2,112,128]{2,1,0:T(8,128)(2,1)S(1)} %get-tuple-element.58), channel_id=1, source_target_pairs={{0,8},{1,9},{2,10},{3,11},{4,12},{5,13},{6,14},{7,15},{8,0},{9,1},... | collective-permute-start | bytes 172040 | tf_op jit(solution)/shard_map/ppermute | solution.py:413
  49.1 6.0 %collective-permute-start.13 = (bf16[2,112,128]{2,1,0:T(8,128)(2,1)S(1)}, bf16[2,112,128]{2,1,0:T(8,128)(2,1)S(1)}, u32[]{:S(2)}, u32[]{:S(2)}) collective-permute-start(bf16[2,112,128]{2,1,0:T(8,128)(2,1)S(1)} %get-tuple-element.59), channel_id=1, source_target_pairs={{0,12},{1,13},{2,14},{3,15},{4,8},{5,9},{6,10},{7,11},{8,4},{9,5},... | collective-permute-start | bytes 172040 | tf_op jit(solution)/shard_map/ppermute | solution.py:413
  57.2 1.5 %collective-permute-start.14 = (f32[56,100]{1,0:T(8,128)S(1)}, f32[56,100]{1,0:T(8,128)S(1)}, u32[]{:S(2)}, u32[]{:S(2)}) collective-permute-start(f32[56,100]{1,0:T(8,128)S(1)} %get-tuple-element.61), channel_id=1, source_target_pairs={{0,1},{1,0},{2,3},{3,2},{4,5},{5,4},{6,7},{7,6},{8,9},{9,8},{10,11... | collective-permute-start | bytes 67208 | tf_op jit(solution)/shard_map/ppermute | solution.py:413

commit v9 on v8

--- a/solution.py
+++ b/solution.py
@@ -257,17 +257,17 @@
     return jnp.dot(weights.astype(jnp.bfloat16), values, preferred_element_type=jnp.float32)
 
 
-def store_heads(mixed, out_ref, first):
+def store_heads(mixed, out_ref, places):
     _, rows, _ = out_ref.shape
     low = lax.broadcasted_iota(jnp.int32, (rows, LANES), 1) < HEAD_DIM
     for at in range(mixed.shape[0] // (2 * rows)):
         base = 2 * at * rows
-        out_ref[first + at] = jnp.where(
+        out_ref[places[at]] = jnp.where(
             low, mixed[base : base + rows], mixed[base + rows : base + 2 * rows]
         ).astype(jnp.bfloat16)
 
 
-def attend_rows(keys, values, queries, out_ref, first):
+def attend_rows(keys, values, queries, out_ref, places):
     _, rows, _ = out_ref.shape
     total = queries.shape[0]
     for base in range(0, total, 4 * rows):
@@ -275,17 +275,18 @@
         scores = score(queries[block, :], keys[...])
         weights = jnp.exp(scores - jnp.max(scores, axis=1, keepdims=True))
         weight_sum = jnp.sum(weights, axis=1, keepdims=True)
-        store_heads(mix(weights, values[...]) / weight_sum, out_ref, first + base // (2 * rows))
-
-
-def attend_early_kernel(info_ref, *refs):
+        mixed = mix(weights, values[...]) / weight_sum
+        store_heads(mixed, out_ref, places[base // (2 * rows) :])
+
+
+def attend_early_kernel(aparts, info_ref, *refs):
     chips = len(refs) - 6
     got_refs = refs[:chips]
     keys, values, queries, mixed_ref, peak_ref, sum_ref = refs[chips:]
     _, rows, _ = got_refs[0].shape
-    for apart, got_ref in enumerate(got_refs):
-        place_keys(info_ref, apart, got_ref, keys, values, apart * rows)
-    place_queries(got_refs[1::2], queries)
+    for at, got_ref in enumerate(got_refs):
+        place_keys(info_ref, aparts[at], got_ref, keys, values, at * rows)
+    place_queries([ref for apart, ref in zip(aparts, got_refs) if apart % 2], queries)
     half = queries.shape[0] // 2
     for block in (slice(0, half), slice(half, 2 * half)):
         scores = score(queries[block, :], keys[...])
@@ -298,16 +299,15 @@
 
 
 def attend_last_kernel(
-    info_ref, early_keys, early_values, early_queries, mixed_ref, peak_ref, sum_ref, last_ref,
+    late, places, info_ref, early_keys, early_values, early_queries, mixed_ref, peak_ref, sum_ref, last_ref,
     out_ref, keys, values, queries,
 ):
     held, _ = early_values.shape
-    _, rows, _ = last_ref.shape
     keys[:held, :] = early_keys[...]
     values[:held, :] = early_values[...]
-    place_keys(info_ref, held // rows, last_ref, keys, values, held)
+    place_keys(info_ref, late, last_ref, keys, values, held)
     place_queries([last_ref], queries)
-    attend_rows(keys, values, queries, out_ref, out_ref.shape[0] - 1)
+    attend_rows(keys, values, queries, out_ref, (late // 2,))
     scores = score(early_queries[...], keys[held:, :])
     peak = peak_ref[...]
     joined = jnp.maximum(peak, jnp.max(scores, axis=1, keepdims=True))
@@ -315,14 +315,14 @@
     weights = jnp.exp(scores - joined[:, : scores.shape[1]])
     weight_sum = sum_ref[...] * scale + jnp.sum(weights, axis=1, keepdims=True)
     mixed = mixed_ref[...] * scale + mix(weights, values[held:, :])
-    store_heads(mixed / weight_sum, out_ref, 0)
+    store_heads(mixed / weight_sum, out_ref, places)
 
 
 def attend_second_kernel(info_ref, keys, values, *refs):
     del info_ref
     out_ref, queries = refs[-2:]
     place_queries(refs[:-2], queries)
-    attend_rows(keys, values, queries, out_ref, 0)
+    attend_rows(keys, values, queries, out_ref, tuple(range(out_ref.shape[0])))
 
 
 def merge_kernel(info_ref, own_ref, got_ref, *out_refs):
@@ -494,8 +494,12 @@
 
 
 def send_order(chips):
-    far = list(range(chips // 2, chips, 2))
+    far = list(range(chips // 2, chips, 2))[::-1]
     return far[:1] + list(range(2, chips // 2, 2)) + far[1:] + [0]
+
+
+def late_send(chips):
+    return chips // 2 + 1
 
 
 def attend_chips(made, normed, w_qkv, tables, info, count):
@@ -509,26 +513,29 @@
             apart = first + side
             held[apart] = across(made[side], 2 * apart, count) if apart else made[side]
     total, half = chips * rows, chips // 2
+    late = late_send(chips)
+    soon = tuple(apart for apart in range(chips) if apart != late)
+    places = tuple(apart // 2 for apart in soon if apart % 2)
     early, early_rows = total - rows, 2 * (half - 1) * rows
     parts = call(
-        attend_early_kernel,
+        functools.partial(attend_early_kernel, soon),
         (
             array((early, 2 * LANES), jnp.bfloat16),
             array((early, LANES), jnp.bfloat16),
             array((early_rows, 2 * LANES), jnp.bfloat16),
         )
         + (array((early_rows, LANES)),) * 3,
-        (info,) + tuple(held[apart] for apart in range(chips - 1)),
+        (info,) + tuple(held[apart] for apart in soon),
         [],
     )
     crossing, keys, values = call(
-        attend_last_kernel,
+        functools.partial(attend_last_kernel, late, places),
         (
             array((half, rows, LANES), jnp.bfloat16),
             array((total, 2 * LANES), jnp.bfloat16),
             array((total, LANES), jnp.bfloat16),
         ),
-        (info,) + tuple(parts) + (held[chips - 1],),
+        (info,) + tuple(parts) + (held[late],),
         [VMEM((2 * rows, 2 * LANES), jnp.bfloat16)],
     )
     crossed = across(crossing, 2, count)

time: 59.5 us -> 58.2 us (0.978)
  waiting for transfers between devices: 14 us -> 12.7 us
    ppermute x14, waiting for transfers between devices: 13.5 us -> 12.2 us  [across(): return lax.ppermute(value, 'seq', [(i, i ^ apart) for i in range(count)])]
  transfers between devices with their start and end apart: 15 -> 15, of which waited for: 7 -> 8; matrix products, arithmetic and copies ran while one was open for 2% -> 2% of each run, Pallas kernels for 14% -> 14%
where the time goes in v9:
time: 58.2 us; the launch traced here: 58 us
  starting transfers between devices  21.3 us (37%)
  Pallas kernels  18.3 us (31%)
  waiting for transfers between devices  12.7 us (22%)
  between operations  2.82 us (5%)
  local copies, waits for them, and re-layouts  1.86 us (3%)
  other arithmetic  1.01 us (2%)
    ppermute x14, starting transfers between devices, across(): return lax.ppermute(value, 'seq', [(i, i ^ apart) for i in range(count)])  18.4 us
    pallas_call x10, Pallas kernels, call(): pl.pallas_call(kernel, out_shape=out_shape, in_specs=[smem_spec()] + spec...  18.3 us
    ppermute x14, waiting for transfers between devices, across(): return lax.ppermute(value, 'seq', [(i, i ^ apart) for i in range(count)])  12.2 us
    ppermute x1, starting transfers between devices, per_device(): lax.ppermute(edges, ('clip', 'seq'), facing_pairs(lax.axis_size('clip'),...  2.97 us
  transfers between devices with their start and end apart: 15, of which 8 were waited for; matrix products, arithmetic and copies ran while one was open for 2% of the time, Pallas kernels for 14%

profile of v9, /device:TPU:0, one launch (start us, length us, event | category | flops | bytes accessed | tf_op | source)
XLA Modules:
  0.0 58.0 jit_solution(2862515049432263401)
XLA Ops:
  0.6 0.9 %constant_dynamic-slice_fusion = bf16[2,16,1536]{2,1,0:T(8,128)(2,1)S(1)} fusion(bf16[2,56,1536]{2,1,0:T(8,128)(2,1)} %hidden_hbm.1, s32[]{:T(128)S(6)} %select_n.45), kind=kLoop, calls=%fused_computation.15 | loop fusion | bytes 196612 | tf_op jit(solution)/shard_map/dynamic_slice | solution.py:575
  1.5 3.0 %collective-permute-start.1 = (bf16[2,16,1536]{2,1,0:T(8,128)(2,1)S(1)}, bf16[2,16,1536]{2,1,0:T(8,128)(2,1)S(1)}, u32[]{:S(2)}, u32[]{:S(2)}) collective-permute-start(bf16[2,16,1536]{2,1,0:T(8,128)(2,1)S(1)} %constant_dynamic-slice_fusion), channel_id=1, source_target_pairs={{1,2},{2,1},{3,4},{4,3},{5,6},{6,5},{7,8},{8,7},{9,10},{10,9},{11,... | collective-permute-start | bytes 294920 | tf_op jit(solution)/shard_map/ppermute | solution.py:577
  4.5 0.9 %dynamic-slice_bitcast_fusion = bf16[56,1536]{1,0:T(8,128)(2,1)S(1)} fusion(bf16[2,56,1536]{2,1,0:T(8,128)(2,1)} %hidden_hbm.1, s32[]{:T(128)S(6)} %select_n.44), kind=kLoop, calls=%fused_computation | loop fusion | bytes 344068 | tf_op jit(solution)/shard_map/squeeze | solution.py:576
  5.4 0.2 collective-permute-start
  5.7 0.3 fusion
  6.6 0.5 collective-permute-done.1.near_ref
  7.1 0.1 collective-permute-start.2
  7.2 0.1 pad_add_fusion.info_ref
  7.3 1.6 %shard_map.113 = (bf16[56,1536]{1,0:T(8,128)(2,1)S(1)}, f32[31,1536]{1,0:T(8,128)S(1)}, f32[5,1536]{1,0:T(8,128)S(1)}, f32[56,100]{1,0:T(8,128)S(1)}, f32[56,100]{1,0:T(8,128)S(1)}) custom-call(s32[3]{0:T(128)S(1)} %pad_add_fusion.info_ref, bf16[2,56,1536]{2,1,0:T(8,128)(2,1)} %hidden_hbm.1, f32[31,1536]{1,0:T(8,128)} %taps_hbm.1, f32[5,1536]{1,0:T(8,128)} %mod_hbm.1), custom_call_target="tpu_custom_call" | custom-call | tf_op jit(solution)/shard_map/pallas_call | solution.py:373
  8.9 0.0 collective-permute-done.partner_ref
  8.9 0.0 collective-permute-done.2.far_ref
  8.9 4.7 %shard_map.114 = (f32[112,1536]{1,0:T(8,128)S(1)}, bf16[112,1536]{1,0:T(8,128)(2,1)S(1)}, bf16[1536,3072]{1,0:T(8,128)(2,1)S(1)}, bf16[3,112,128]{2,1,0:T(8,128)(2,1)S(1)}, bf16[3,112,128]{2,1,0:T(8,128)(2,1)S(1)}) custom-call(s32[3]{0:T(128)S(1)} %pad_add_fusion.info_ref, bf16[56,1536]{1,0:T(8,128)(2,1)S(1)} %get-tuple-element.34.own_ref, ...), custom_call_target="tpu_custom_call" | custom-call | tf_op jit(solution)/shard_map/pallas_call | solution.py:373
  13.6 1.2 %shard_map.117 = (bf16[3,112,128]{2,1,0:T(8,128)(2,1)S(1)}, bf16[3,112,128]{2,1,0:T(8,128)(2,1)S(1)}) custom-call(s32[3]{0:T(128)S(1)} %pad_add_fusion.info_ref, bf16[112,1536]{1,0:T(8,128)(2,1)S(1)} %get-tuple-element.38.normed_ref, bf16[1536,3072]{1,0:T(8,128)(2,1)S(1)} %get-tuple-element.39.weight_ref, f32[112,128]{1,0:T(8,128)S(1)} %get-tuple-element.65.cos_ref, ...), custom_call_target="tpu_custom_call" | custom-call | tf_op jit(solution)/shard_map/pallas_call | solution.py:373
  14.8 3.6 %collective-permute-start.6 = (bf16[3,112,128]{2,1,0:T(8,128)(2,1)S(1)}, bf16[3,112,128]{2,1,0:T(8,128)(2,1)S(1)}, u32[]{:S(2)}, u32[]{:S(2)}) collective-permute-start(bf16[3,112,128]{2,1,0:T(8,128)(2,1)S(1)} %get-tuple-element.44), channel_id=1, source_target_pairs={{0,8},{1,9},{2,10},{3,11},{4,12},{5,13},{6,14},{7,15},{8,0},{9,1},... | collective-permute-start | bytes 258056 | tf_op jit(solution)/shard_map/ppermute | solution.py:413
  18.3 1.2 %shard_map.116 = (bf16[3,112,128]{2,1,0:T(8,128)(2,1)S(1)}, bf16[3,112,128]{2,1,0:T(8,128)(2,1)S(1)}) custom-call(s32[3]{0:T(128)S(1)} %pad_add_fusion.info_ref, bf16[112,1536]{1,0:T(8,128)(2,1)S(1)} %get-tuple-element.38.normed_ref, bf16[1536,3072]{1,0:T(8,128)(2,1)S(1)} %get-tuple-element.39.weight_ref, f32[112,128]{1,0:T(8,128)S(1)} %get-tuple-element.65.cos_ref, ...), custom_call_target="tpu_custom_call" | custom-call | tf_op jit(solution)/shard_map/pallas_call | solution.py:373
  19.5 0.0 copy-start
  19.5 0.0 copy-start.1
  19.6 0.0 copy-start.2
  19.6 1.6 %collective-permute-start.4 = (bf16[3,112,128]{2,1,0:T(8,128)(2,1)S(1)}, bf16[3,112,128]{2,1,0:T(8,128)(2,1)S(1)}, u32[]{:S(2)}, u32[]{:S(2)}) collective-permute-start(bf16[3,112,128]{2,1,0:T(8,128)(2,1)S(1)} %get-tuple-element.42), channel_id=1, source_target_pairs={{0,4},{1,5},{2,6},{3,7},{4,0},{5,1},{6,2},{7,3},{8,12},{9,13},{10,... | collective-permute-start | bytes 258056 | tf_op jit(solution)/shard_map/ppermute | solution.py:413
  21.2 1.2 %shard_map.115 = (bf16[3,112,128]{2,1,0:T(8,128)(2,1)S(1)}, bf16[3,112,128]{2,1,0:T(8,128)(2,1)S(1)}) custom-call(s32[3]{0:T(128)S(1)} %pad_add_fusion.info_ref, bf16[112,1536]{1,0:T(8,128)(2,1)S(1)} %get-tuple-element.38.normed_ref, bf16[1536,3072]{1,0:T(8,128)(2,1)S(1)} %get-tuple-element.39.weight_ref, f32[112,128]{1,0:T(8,128)S(1)} %get-tuple-element.65.cos_ref, ...), custom_call_target="tpu_custom_call" | custom-call | tf_op jit(solution)/shard_map/pallas_call | solution.py:373
  22.4 1.5 %collective-permute-start.5 = (bf16[3,112,128]{2,1,0:T(8,128)(2,1)S(1)}, bf16[3,112,128]{2,1,0:T(8,128)(2,1)S(1)}, u32[]{:S(2)}, u32[]{:S(2)}) collective-permute-start(bf16[3,112,128]{2,1,0:T(8,128)(2,1)S(1)} %get-tuple-element.43), channel_id=1, source_target_pairs={{0,6},{1,7},{2,4},{3,5},{4,2},{5,3},{6,0},{7,1},{8,14},{9,15},{10,... | collective-permute-start | bytes 258056 | tf_op jit(solution)/shard_map/ppermute | solution.py:413
  23.9 0.5 collective-permute-start.3
  24.4 1.3 %collective-permute-start.7 = (bf16[3,112,128]{2,1,0:T(8,128)(2,1)S(1)}, bf16[3,112,128]{2,1,0:T(8,128)(2,1)S(1)}, u32[]{:S(2)}, u32[]{:S(2)}) collective-permute-start(bf16[3,112,128]{2,1,0:T(8,128)(2,1)S(1)} %get-tuple-element.45), channel_id=1, source_target_pairs={{0,12},{1,13},{2,14},{3,15},{4,8},{5,9},{6,10},{7,11},{8,4},{9,5},... | collective-permute-start | bytes 258056 | tf_op jit(solution)/shard_map/ppermute | solution.py:413
  25.7 0.0 collective-permute-done.6.refs_4_.refs_2_
  25.7 3.4 %collective-permute-start.8 = (bf16[3,112,128]{2,1,0:T(8,128)(2,1)S(1)}, bf16[3,112,128]{2,1,0:T(8,128)(2,1)S(1)}, u32[]{:S(2)}, u32[]{:S(2)}) collective-permute-start(bf16[3,112,128]{2,1,0:T(8,128)(2,1)S(1)} %get-tuple-element.46), channel_id=1, source_target_pairs={{0,14},{1,15},{2,12},{3,13},{4,10},{5,11},{6,8},{7,9},{8,6},{9,7},... | collective-permute-start | bytes 258056 | tf_op jit(solution)/shard_map/ppermute | solution.py:413
  29.2 0.0 collective-permute-done.4.refs_2_.refs_1_
  29.2 0.0 collective-permute-start.9
  29.2 0.0 collective-permute-done.5.refs_3_
  29.2 0.4 collective-permute-done.3.refs_1_
  29.6 1.7 %collective-permute-done.7.refs_5_.refs_3_ = bf16[3,112,128]{2,1,0:T(8,128)(2,1)S(1)} collective-permute-done((bf16[3,112,128]{2,1,0:T(8,128)(2,1)S(1)}, bf16[3,112,128]{2,1,0:T(8,128)(2,1)S(1)}, u32[]{:S(2)}, u32[]{:S(2)}) %collective-permute-start.7) | collective-permute-done | bytes 86048 | tf_op jit(solution)/shard_map/ppermute | solution.py:413
  31.3 2.6 %collective-permute-done.8.refs_6_ = bf16[3,112,128]{2,1,0:T(8,128)(2,1)S(1)} collective-permute-done((bf16[3,112,128]{2,1,0:T(8,128)(2,1)S(1)}, bf16[3,112,128]{2,1,0:T(8,128)(2,1)S(1)}, u32[]{:S(2)}, u32[]{:S(2)}) %collective-permute-start.8) | collective-permute-done | bytes 86048 | tf_op jit(solution)/shard_map/ppermute | solution.py:413
  33.8 2.1 %shard_map.118 = (bf16[784,256]{1,0:T(8,128)(2,1)S(1)}, bf16[784,128]{1,0:T(8,128)(2,1)S(1)}, bf16[672,256]{1,0:T(8,128)(2,1)S(1)}, f32[672,128]{1,0:T(8,128)S(1...) custom-call(s32[3]{0:T(128)S(1)} %pad_add_fusion.info_ref, bf16[3,112,128]{2,1,0:T(8,128)(2,1)S(1)} %get-tuple-element.40.refs_0_, ...), custom_call_target="tpu_custom_call" | custom-call | tf_op jit(solution)/shard_map/pallas_call | solution.py:373
  35.9 2.4 %collective-permute-done.9.last_ref = bf16[3,112,128]{2,1,0:T(8,128)(2,1)S(1)} collective-permute-done((bf16[3,112,128]{2,1,0:T(8,128)(2,1)S(1)}, bf16[3,112,128]{2,1,0:T(8,128)(2,1)S(1)}, u32[]{:S(2)}, u32[]{:S(2)}) %collective-permute-start.9) | collective-permute-done | bytes 86048 | tf_op jit(solution)/shard_map/ppermute | solution.py:413
  38.3 1.5 %shard_map.119 = (bf16[4,112,128]{2,1,0:T(8,128)(2,1)S(1)}, bf16[896,256]{1,0:T(8,128)(2,1)S(1)}, bf16[896,128]{1,0:T(8,128)(2,1)S(1)}) custom-call(s32[3]{0:T(128)S(1)} %pad_add_fusion.info_ref, bf16[784,256]{1,0:T(8,128)(2,1)S(1)} %get-tuple-element.47.early_keys, bf16[784,128]{1,0:T(8,128)(2,1)S(1)} %get-tuple-element.48.early_values, ...), custom_call_target="tpu_custom_call" | custom-call | tf_op jit(solution)/shard_map/pallas_call | solution.py:373
  39.9 1.5 %collective-permute-start.10 = (bf16[4,112,128]{2,1,0:T(8,128)(2,1)S(1)}, bf16[4,112,128]{2,1,0:T(8,128)(2,1)S(1)}, u32[]{:S(2)}, u32[]{:S(2)}) collective-permute-start(bf16[4,112,128]{2,1,0:T(8,128)(2,1)S(1)} %get-tuple-element.56), channel_id=1, source_target_pairs={{0,2},{1,3},{2,0},{3,1},{4,6},{5,7},{6,4},{7,5},{8,10},{9,11},{10,... | collective-permute-start | bytes 344072 | tf_op jit(solution)/shard_map/ppermute | solution.py:413
  41.4 2.3 %shard_map.120.own_ref.refs_0_ = bf16[4,112,128]{2,1,0:T(8,128)(2,1)S(1)} custom-call(s32[3]{0:T(128)S(1)} %pad_add_fusion.info_ref, bf16[896,256]{1,0:T(8,128)(2,1)S(1)} %get-tuple-element.54.keys, bf16[896,128]{1,0:T(8,128)(2,1)S(1)} %get-tuple-element.55.values, bf16[3,112,128]{2,1,0:T(8,128)(2,1)S(1)} %get-tuple-element.40.refs_0_, ...), custom_call_target="tpu_custom_call" | custom-call | tf_op jit(solution)/shard_map/pallas_call | solution.py:373
  43.7 1.0 %collective-permute-done.10.got_ref.refs_1_ = bf16[4,112,128]{2,1,0:T(8,128)(2,1)S(1)} collective-permute-done((bf16[4,112,128]{2,1,0:T(8,128)(2,1)S(1)}, bf16[4,112,128]{2,1,0:T(8,128)(2,1)S(1)}, u32[]{:S(2)}, u32[]{:S(2)}) %collective-permute-start.10) | collective-permute-done | bytes 114720 | tf_op jit(solution)/shard_map/ppermute | solution.py:413
  44.7 0.6 shard_map.121
  45.3 1.8 %collective-permute-start.11 = (bf16[2,112,128]{2,1,0:T(8,128)(2,1)S(1)}, bf16[2,112,128]{2,1,0:T(8,128)(2,1)S(1)}, u32[]{:S(2)}, u32[]{:S(2)}) collective-permute-start(bf16[2,112,128]{2,1,0:T(8,128)(2,1)S(1)} %get-tuple-element.57), channel_id=1, source_target_pairs={{0,4},{1,5},{2,6},{3,7},{4,0},{5,1},{6,2},{7,3},{8,12},{9,13},{10,... | collective-permute-start | bytes 172040 | tf_op jit(solution)/shard_map/ppermute | solution.py:413
  47.1 0.7 %collective-permute-start.12 = (bf16[2,112,128]{2,1,0:T(8,128)(2,1)S(1)}, bf16[2,112,128]{2,1,0:T(8,128)(2,1)S(1)}, u32[]{:S(2)}, u32[]{:S(2)}) collective-permute-start(bf16[2,112,128]{2,1,0:T(8,128)(2,1)S(1)} %get-tuple-element.58), channel_id=1, source_target_pairs={{0,8},{1,9},{2,10},{3,11},{4,12},{5,13},{6,14},{7,15},{8,0},{9,1},... | collective-permute-start | bytes 172040 | tf_op jit(solution)/shard_map/ppermute | solution.py:413
  47.9 1.9 %collective-permute-start.13 = (bf16[2,112,128]{2,1,0:T(8,128)(2,1)S(1)}, bf16[2,112,128]{2,1,0:T(8,128)(2,1)S(1)}, u32[]{:S(2)}, u32[]{:S(2)}) collective-permute-start(bf16[2,112,128]{2,1,0:T(8,128)(2,1)S(1)} %get-tuple-element.59), channel_id=1, source_target_pairs={{0,12},{1,13},{2,14},{3,15},{4,8},{5,9},{6,10},{7,11},{8,4},{9,5},... | collective-permute-start | bytes 172040 | tf_op jit(solution)/shard_map/ppermute | solution.py:413
  49.8 0.0 collective-permute-done.11.refs_2_
  49.8 2.8 %collective-permute-done.12.refs_3_ = bf16[2,112,128]{2,1,0:T(8,128)(2,1)S(1)} collective-permute-done((bf16[2,112,128]{2,1,0:T(8,128)(2,1)S(1)}, bf16[2,112,128]{2,1,0:T(8,128)(2,1)S(1)}, u32[]{:S(2)}, u32[]{:S(2)}) %collective-permute-start.12) | collective-permute-done | bytes 57376 | tf_op jit(solution)/shard_map/ppermute | solution.py:413
  52.6 1.2 %collective-permute-done.13.refs_4_ = bf16[2,112,128]{2,1,0:T(8,128)(2,1)S(1)} collective-permute-done((bf16[2,112,128]{2,1,0:T(8,128)(2,1)S(1)}, bf16[2,112,128]{2,1,0:T(8,128)(2,1)S(1)}, u32[]{:S(2)}, u32[]{:S(2)}) %collective-permute-start.13) | collective-permute-done | bytes 57376 | tf_op jit(solution)/shard_map/ppermute | solution.py:413
  53.8 2.0 %shard_map.122 = (f32[56,100]{1,0:T(8,128)S(1)}, f32[56,100]{1,0:T(8,128)S(1)}) custom-call(s32[3]{0:T(128)S(1)} %pad_add_fusion.info_ref, f32[112,1536]{1,0:T(8,128)S(1)} %get-tuple-element.37.residual, bf16[100,1536]{1,0:T(8,128)(2,1)S(1)} %bitcast.8, f32[5,1536]{1,0:T(8,128)S(1)} %get-tuple-element.36.mod_ref, bf16[1024,1536]{1,0:T(8,128)(2,1)S(1)} %copy-done, ...), custom_call_target="tpu_custom_call" | custom-call | tf_op jit(solution)/shard_map/pallas_call | solution.py:373
  55.9 0.1 collective-permute-start.14
  57.3 0.0 collective-permute-done.14
  57.4 0.6 %multiply_add_fusion = (f32[56,100]{1,0:T(8,128)}, f32[56,100]{1,0:T(8,128)}) fusion(f32[56,100]{1,0:T(8,128)S(1)} %copy-done.2, f32[]{:T(128)} %bitcast.5, f32[56,100]{1,0:T(8,128)S(1)} %collective-permute-done.14, f32[56,100]{1,0:T(8,128)S(1)} %get-tuple-element.60, f32[]{:T(128)} %bitcast.7, f32[56,100]{1,0:T(8,128)S(1)} %get-tuple-element.33, ...), kind=kLoop, calls=%fused_computation.4 | loop fusion | flops 56000 | bytes 156808 | tf_op jit(solution)/shard_map/add | solution.py:634
  (5 shorter events, 0.0 us)
Async XLA Ops:
  1.5 5.6 %collective-permute-start.1 = (bf16[2,16,1536]{2,1,0:T(8,128)(2,1)S(1)}, bf16[2,16,1536]{2,1,0:T(8,128)(2,1)S(1)}, u32[]{:S(2)}, u32[]{:S(2)}) collective-permute-start(bf16[2,16,1536]{2,1,0:T(8,128)(2,1)S(1)} %constant_dynamic-slice_fusion), channel_id=1, source_target_pairs={{1,2},{2,1},{3,4},{4,3},{5,6},{6,5},{7,8},{8,7},{9,10},{10,9},{11,... | collective-permute-start | bytes 294920 | tf_op jit(solution)/shard_map/ppermute | solution.py:577
  5.4 3.4 %collective-permute-start = (bf16[56,1536]{1,0:T(8,128)(2,1)S(1)}, bf16[56,1536]{1,0:T(8,128)(2,1)S(1)}, u32[]{:S(2)}, u32[]{:S(2)}) collective-permute-start(bf16[56,1536]{1,0:T(8,128)(2,1)S(1)} %dynamic-slice_bitcast_fusion), channel_id=1, source_target_pairs={{0,1},{1,0},{2,3},{3,2},{4,5},{5,4},{6,7},{7,6},{8,9},{9,8},{10,11... | collective-permute-start | bytes 516104 | tf_op jit(solution)/shard_map/ppermute | solution.py:413
  7.1 1.8 %collective-permute-start.2 = (bf16[2,16,1536]{2,1,0:T(8,128)(2,1)S(1)}, bf16[2,16,1536]{2,1,0:T(8,128)(2,1)S(1)}, u32[]{:S(2)}, u32[]{:S(2)}) collective-permute-start(bf16[2,16,1536]{2,1,0:T(8,128)(2,1)S(1)} %collective-permute-done.1.near_ref), channel_id=1, source_target_pairs={{0,1},{1,0},{2,3},{3,2},{4,5},{5,4},{6,7},{7,6},{8,9},{9,8},{10,11... | collective-permute-start | bytes 294920 | tf_op jit(solution)/shard_map/ppermute | solution.py:413
  14.8 10.9 %collective-permute-start.6 = (bf16[3,112,128]{2,1,0:T(8,128)(2,1)S(1)}, bf16[3,112,128]{2,1,0:T(8,128)(2,1)S(1)}, u32[]{:S(2)}, u32[]{:S(2)}) collective-permute-start(bf16[3,112,128]{2,1,0:T(8,128)(2,1)S(1)} %get-tuple-element.44), channel_id=1, source_target_pairs={{0,8},{1,9},{2,10},{3,11},{4,12},{5,13},{6,14},{7,15},{8,0},{9,1},... | collective-permute-start | bytes 258056 | tf_op jit(solution)/shard_map/ppermute | solution.py:413
  19.5 34.3 %copy-start = (bf16[1024,1536]{1,0:T(8,128)(2,1)S(1)}, bf16[1024,1536]{1,0:T(8,128)(2,1)}, u32[]{:S(2)}) copy-start(bf16[1024,1536]{1,0:T(8,128)(2,1)} %w_out_ref.1) | copy-start | bytes 9437188
  19.5 34.3 %copy-start.1 = (bf16[1536,100]{0,1:T(8,128)(2,1)S(1)}, bf16[1536,100]{0,1:T(8,128)(2,1)}, u32[]{:S(2)}) copy-start(bf16[1536,100]{0,1:T(8,128)(2,1)} %param.19) | copy-start | bytes 921604
  19.6 37.8 %copy-start.2 = (f32[56,100]{1,0:T(8,128)S(1)}, f32[56,100]{1,0:T(8,128)}, u32[]{:S(2)}) copy-start(f32[56,100]{1,0:T(8,128)} %param.11) | copy-start | bytes 67204
  19.6 9.6 %collective-permute-start.4 = (bf16[3,112,128]{2,1,0:T(8,128)(2,1)S(1)}, bf16[3,112,128]{2,1,0:T(8,128)(2,1)S(1)}, u32[]{:S(2)}, u32[]{:S(2)}) collective-permute-start(bf16[3,112,128]{2,1,0:T(8,128)(2,1)S(1)} %get-tuple-element.42), channel_id=1, source_target_pairs={{0,4},{1,5},{2,6},{3,7},{4,0},{5,1},{6,2},{7,3},{8,12},{9,13},{10,... | collective-permute-start | bytes 258056 | tf_op jit(solution)/shard_map/ppermute | solution.py:413
  22.4 6.8 %collective-permute-start.5 = (bf16[3,112,128]{2,1,0:T(8,128)(2,1)S(1)}, bf16[3,112,128]{2,1,0:T(8,128)(2,1)S(1)}, u32[]{:S(2)}, u32[]{:S(2)}) collective-permute-start(bf16[3,112,128]{2,1,0:T(8,128)(2,1)S(1)} %get-tuple-element.43), channel_id=1, source_target_pairs={{0,6},{1,7},{2,4},{3,5},{4,2},{5,3},{6,0},{7,1},{8,14},{9,15},{10,... | collective-permute-start | bytes 258056 | tf_op jit(solution)/shard_map/ppermute | solution.py:413
  23.9 5.7 %collective-permute-start.3 = (bf16[3,112,128]{2,1,0:T(8,128)(2,1)S(1)}, bf16[3,112,128]{2,1,0:T(8,128)(2,1)S(1)}, u32[]{:S(2)}, u32[]{:S(2)}) collective-permute-start(bf16[3,112,128]{2,1,0:T(8,128)(2,1)S(1)} %get-tuple-element.41), channel_id=1, source_target_pairs={{0,2},{1,3},{2,0},{3,1},{4,6},{5,7},{6,4},{7,5},{8,10},{9,11},{10,... | collective-permute-start | bytes 258056 | tf_op jit(solution)/shard_map/ppermute | solution.py:413
  24.4 6.9 %collective-permute-start.7 = (bf16[3,112,128]{2,1,0:T(8,128)(2,1)S(1)}, bf16[3,112,128]{2,1,0:T(8,128)(2,1)S(1)}, u32[]{:S(2)}, u32[]{:S(2)}) collective-permute-start(bf16[3,112,128]{2,1,0:T(8,128)(2,1)S(1)} %get-tuple-element.45), channel_id=1, source_target_pairs={{0,12},{1,13},{2,14},{3,15},{4,8},{5,9},{6,10},{7,11},{8,4},{9,5},... | collective-permute-start | bytes 258056 | tf_op jit(solution)/shard_map/ppermute | solution.py:413
  25.7 8.1 %collective-permute-start.8 = (bf16[3,112,128]{2,1,0:T(8,128)(2,1)S(1)}, bf16[3,112,128]{2,1,0:T(8,128)(2,1)S(1)}, u32[]{:S(2)}, u32[]{:S(2)}) collective-permute-start(bf16[3,112,128]{2,1,0:T(8,128)(2,1)S(1)} %get-tuple-element.46), channel_id=1, source_target_pairs={{0,14},{1,15},{2,12},{3,13},{4,10},{5,11},{6,8},{7,9},{8,6},{9,7},... | collective-permute-start | bytes 258056 | tf_op jit(solution)/shard_map/ppermute | solution.py:413
  29.2 9.2 %collective-permute-start.9 = (bf16[3,112,128]{2,1,0:T(8,128)(2,1)S(1)}, bf16[3,112,128]{2,1,0:T(8,128)(2,1)S(1)}, u32[]{:S(2)}, u32[]{:S(2)}) collective-permute-start(bf16[3,112,128]{2,1,0:T(8,128)(2,1)S(1)} %get-tuple-element.53), channel_id=1, source_target_pairs={{0,10},{1,11},{2,8},{3,9},{4,14},{5,15},{6,12},{7,13},{8,2},{9,3},... | collective-permute-start | bytes 258056 | tf_op jit(solution)/shard_map/ppermute | solution.py:413
  39.9 4.9 %collective-permute-start.10 = (bf16[4,112,128]{2,1,0:T(8,128)(2,1)S(1)}, bf16[4,112,128]{2,1,0:T(8,128)(2,1)S(1)}, u32[]{:S(2)}, u32[]{:S(2)}) collective-permute-start(bf16[4,112,128]{2,1,0:T(8,128)(2,1)S(1)} %get-tuple-element.56), channel_id=1, source_target_pairs={{0,2},{1,3},{2,0},{3,1},{4,6},{5,7},{6,4},{7,5},{8,10},{9,11},{10,... | collective-permute-start | bytes 344072 | tf_op jit(solution)/shard_map/ppermute | solution.py:413
  45.3 4.5 %collective-permute-start.11 = (bf16[2,112,128]{2,1,0:T(8,128)(2,1)S(1)}, bf16[2,112,128]{2,1,0:T(8,128)(2,1)S(1)}, u32[]{:S(2)}, u32[]{:S(2)}) collective-permute-start(bf16[2,112,128]{2,1,0:T(8,128)(2,1)S(1)} %get-tuple-element.57), channel_id=1, source_target_pairs={{0,4},{1,5},{2,6},{3,7},{4,0},{5,1},{6,2},{7,3},{8,12},{9,13},{10,... | collective-permute-start | bytes 172040 | tf_op jit(solution)/shard_map/ppermute | solution.py:413
  47.1 5.5 %collective-permute-start.12 = (bf16[2,112,128]{2,1,0:T(8,128)(2,1)S(1)}, bf16[2,112,128]{2,1,0:T(8,128)(2,1)S(1)}, u32[]{:S(2)}, u32[]{:S(2)}) collective-permute-start(bf16[2,112,128]{2,1,0:T(8,128)(2,1)S(1)} %get-tuple-element.58), channel_id=1, source_target_pairs={{0,8},{1,9},{2,10},{3,11},{4,12},{5,13},{6,14},{7,15},{8,0},{9,1},... | collective-permute-start | bytes 172040 | tf_op jit(solution)/shard_map/ppermute | solution.py:413
  47.9 6.0 %collective-permute-start.13 = (bf16[2,112,128]{2,1,0:T(8,128)(2,1)S(1)}, bf16[2,112,128]{2,1,0:T(8,128)(2,1)S(1)}, u32[]{:S(2)}, u32[]{:S(2)}) collective-permute-start(bf16[2,112,128]{2,1,0:T(8,128)(2,1)S(1)} %get-tuple-element.59), channel_id=1, source_target_pairs={{0,12},{1,13},{2,14},{3,15},{4,8},{5,9},{6,10},{7,11},{8,4},{9,5},... | collective-permute-start | bytes 172040 | tf_op jit(solution)/shard_map/ppermute | solution.py:413
  55.9 1.5 %collective-permute-start.14 = (f32[56,100]{1,0:T(8,128)S(1)}, f32[56,100]{1,0:T(8,128)S(1)}, u32[]{:S(2)}, u32[]{:S(2)}) collective-permute-start(f32[56,100]{1,0:T(8,128)S(1)} %get-tuple-element.61), channel_id=1, source_target_pairs={{0,1},{1,0},{2,3},{3,2},{4,5},{5,4},{6,7},{7,6},{8,9},{9,8},{10,11... | collective-permute-start | bytes 67208 | tf_op jit(solution)/shard_map/ppermute | solution.py:413
